TPU v7x, 32 devices: a whole 2x2x4 slice. The times are simulated.
32 devices in a mesh: context: 8 (over z, x), tensor: 4 (over y, core).
Axes of the slice: x: 2, y: 2, z: 4, core: 2. Of those that a mesh axis runs over, the one named last changes fastest.
Arguments:
- residual_in: float32 [1024, 2048], P(('context', 'tensor')), may hold values from -6 to 6
- grad_output: float32 [1024, 2048], P(('context', 'tensor')), may hold values from -6 to 6
- block_order: int32 [16], replicated, may hold values from 0 to 15, as said below
- w_query: bfloat16 [2, 2048, 2048], P(None, 'context', 'tensor'), may hold values from -0.125 to 0.125
- key_weight: bfloat16 [2, 2048, 1024], P(None, 'context', 'tensor'), may hold values from -0.125 to 0.125
- value_weight: bfloat16 [2, 2048, 1024], P(None, 'context', 'tensor'), may hold values from -0.125 to 0.125
- w_out: bfloat16 [2, 2048, 2048], P(None, 'tensor', 'context'), may hold values from -1.5 to 1.5
- w_gate: bfloat16 [2, 2048, 6144], P(None, 'context', 'tensor'), may hold values from -0.125 to 0.125
- w_up: bfloat16 [2, 2048, 6144], P(None, 'context', 'tensor'), may hold values from -0.125 to 0.125
- w_down: bfloat16 [2, 6144, 2048], P(None, 'tensor', 'context'), may hold values from -0.078125 to 0.078125
- attn_gain: bfloat16 [2, 2048], P(None, 'context'), may hold values from 0.5 to 1.5
- mlp_gain: bfloat16 [2, 2048], P(None, 'context'), may hold values from 0.5 to 1.5
- query_gain: float32 [2, 128], replicated, may hold values from 0.5 to 1.5
- key_gain: float32 [2, 128], replicated, may hold values from 0.5 to 1.5
Outputs:
- final_out: float32 [1024, 2048], P(('context', 'tensor'))
- grad_input: float32 [1024, 2048], P(('context', 'tensor'))
- d_query: float32 [2, 2048, 2048], P(None, 'context', 'tensor')
- d_key: float32 [2, 2048, 1024], P(None, 'context', 'tensor')
- d_value: float32 [2, 2048, 1024], P(None, 'context', 'tensor')
- d_out: float32 [2, 2048, 2048], P(None, 'tensor', 'context')
- d_gate: float32 [2, 2048, 6144], P(None, 'context', 'tensor')
- d_up: float32 [2, 2048, 6144], P(None, 'context', 'tensor')
- d_down: float32 [2, 6144, 2048], P(None, 'tensor', 'context')
- d_attn_gain: float32 [2, 2048], P(None, 'context')
- d_mlp_gain: float32 [2, 2048], P(None, 'context')
- d_query_gain: float32 [2, 128], replicated
- d_key_gain: float32 [2, 128], replicated
Inputs may be any that keep to these rules, and one draw needn't show every extreme that they name: `block_order`: a permutation of 0 to 15 in which the entries 2 i and 2 i + 1 always sum to 15.
All inputs are finite; a program needn't handle non-finite values.
Results may differ from a plain program's by a relative error of at most 0.033.
Values may be sent and summed in bfloat16 or wider, within the bound.
No kernel may reach another device: no remote copies, remote signals or barrier semaphores. Data moves between devices by JAX's collectives and lax.ppermute only.
A program may use at most 256 MiB of HBM per device.

v0:
```python
import functools

import jax
import jax.numpy as jnp
from jax import lax
from jax.experimental import pallas as pl
from jax.experimental.pallas import tpu as pltpu
from jax.sharding import PartitionSpec as P

EPSILON = 1e-06
THETA = 1000000.0
AXES = ("context", "tensor")
BF = jnp.bfloat16
F32 = jnp.float32


def mm(a, b):
    return jnp.dot(a, b, preferred_element_type=F32)


def mm_tn(a, b):
    return lax.dot_general(a, b, (((0,), (0,)), ((), ())), preferred_element_type=F32)


def mm_nt(a, b):
    return lax.dot_general(a, b, (((1,), (1,)), ((), ())), preferred_element_type=F32)


def rms_scale(row_data, gain_row):
    mean_square = jnp.mean(row_data * row_data, axis=-1, keepdims=True)
    return row_data * lax.rsqrt(mean_square + EPSILON) * gain_row


def rotary_tables(positions, head_dim):
    half_dim = head_dim // 2
    exponent = jnp.arange(half_dim, dtype=F32) * (2.0 / head_dim)
    inverse = jnp.power(F32(THETA), -exponent)
    angles = positions.astype(F32)[:, None] * inverse[None, :]
    return (jnp.cos(angles), jnp.sin(angles))


def row_positions(block_order, first_row, row_count, rows_per_block):
    rows_index = first_row + jnp.arange(row_count, dtype=jnp.int32)
    slot_index = rows_index // rows_per_block
    slots = jnp.arange(block_order.shape[0], dtype=jnp.int32)
    matches = slot_index[:, None] == slots[None, :]
    owners = jnp.sum(jnp.where(matches, block_order[None, :], 0), axis=1)
    return owners * rows_per_block + rows_index % rows_per_block


def after(value, *others):
    return lax.optimization_barrier((value, others))[0]


def rows_call(kernel, out_shapes, *operands):
    return pl.pallas_call(
        kernel,
        out_shape=[jax.ShapeDtypeStruct(shape, kind) for shape, kind in out_shapes],
        compiler_params=pltpu.CompilerParams(vmem_limit_bytes=48 * 1024 * 1024),
    )(*operands)


def join_kernel(*refs):
    *pieces, out_ref = refs
    count = pieces[0].shape[0]
    for slot, piece in enumerate(pieces):
        out_ref[slot * count : (slot + 1) * count, :] = piece[...]


def join(pieces):
    rows, width = pieces[0].shape
    return rows_call(join_kernel, [((len(pieces) * rows, width), pieces[0].dtype)], *pieces)[0]


def prep_kernel(heads, x_ref, gain_ref, cos_ref, sin_ref, out_ref):
    head_dim = gain_ref.shape[1]
    for head in range(x_ref.shape[1] // head_dim):
        at = slice(head * head_dim, (head + 1) * head_dim)
        rows = x_ref[:, at]
        if head < heads:
            mean_square = jnp.mean(rows * rows, axis=-1, keepdims=True)
            rows = rows * lax.rsqrt(mean_square + EPSILON) * gain_ref[...]
            rows = rows * cos_ref[...] + pltpu.roll(rows, head_dim // 2, 1) * sin_ref[...]
        out_ref[:, at] = rows.astype(BF)


def prep_heads(projected, heads, gain, tables):
    kernel = functools.partial(prep_kernel, heads)
    return rows_call(kernel, [(projected.shape, BF)], projected, gain, *tables)[0]


def prep_back_kernel(heads, x_ref, gain_ref, cos_ref, sin_ref, *refs):
    grads, (out_ref, gain_grad_ref) = refs[:-2], refs[-2:]
    head_dim = gain_ref.shape[1]
    gain_grad = jnp.zeros((1, head_dim), F32)
    for head in range(x_ref.shape[1] // head_dim):
        at = slice(head * head_dim, (head + 1) * head_dim)
        grad = grads[0][:, at].astype(F32)
        for piece in grads[1:]:
            grad = grad + piece[:, at].astype(F32)
        if head < heads:
            rows = x_ref[:, at]
            mean_square = jnp.mean(rows * rows, axis=-1, keepdims=True)
            scale = lax.rsqrt(mean_square + EPSILON)
            unit = rows * scale
            grad = grad * cos_ref[...] + pltpu.roll(grad * sin_ref[...], head_dim // 2, 1)
            gain_grad = gain_grad + jnp.sum(grad * unit, axis=0, keepdims=True)
            grad = grad * gain_ref[...]
            grad = scale * (grad - unit * jnp.mean(grad * unit, axis=-1, keepdims=True))
        out_ref[:, at] = grad.astype(BF)
    gain_grad_ref[...] = gain_grad


def prep_heads_back(projected, heads, gain, tables, grads):
    kernel = functools.partial(prep_back_kernel, heads)
    shapes = [(projected.shape, BF), (gain.shape, F32)]
    return rows_call(kernel, shapes, projected, gain, *tables, *grads)


def dot_nt(a, b):
    return lax.dot_general(a, b, (((1,), (1,)), ((), ())), preferred_element_type=F32)


def dot_tn(a, b):
    return lax.dot_general(a, b, (((0,), (0,)), ((), ())), preferred_element_type=F32)


def stack_heads(ref, first, groups, head_dim):
    return jnp.concatenate(
        [ref[:, (first + i) * head_dim : (first + i + 1) * head_dim] for i in range(groups)], axis=0
    )


def attend_kernel(head_dim, query_ref, query_pos_ref, key_pos_ref, *refs):
    pairs, (out_ref, log_ref) = refs[:-2], refs[-2:]
    count = query_ref.shape[0]
    kv_heads = pairs[0].shape[1] // (2 * head_dim)
    groups = query_ref.shape[1] // (kv_heads * head_dim)
    query_pos = jnp.concatenate([query_pos_ref[...]] * groups, axis=0)
    for kv_head in range(kv_heads):
        queries = stack_heads(query_ref, kv_head * groups, groups, head_dim)
        totals = jnp.zeros((groups * count, 1), F32)
        summed = jnp.zeros((groups * count, head_dim), F32)
        for slot, pair in enumerate(pairs):
            keys = pair[:, kv_head * head_dim : (kv_head + 1) * head_dim]
            values = pair[:, (kv_heads + kv_head) * head_dim : (kv_heads + kv_head + 1) * head_dim]
            scores = dot_nt(queries, keys) * head_dim ** (-0.5)
            causal = key_pos_ref[slot : slot + 1, :] <= query_pos
            weights = jnp.where(causal, jnp.exp(scores), 0.0)
            totals = totals + jnp.sum(weights, axis=-1, keepdims=True)
            summed = summed + jnp.dot(weights.astype(BF), values, preferred_element_type=F32)
        outputs = summed / totals
        logs = jnp.log(totals)
        for group in range(groups):
            head = kv_head * groups + group
            at = slice(group * count, (group + 1) * count)
            out_ref[:, head * head_dim : (head + 1) * head_dim] = outputs[at].astype(BF)
            log_ref[:, head : head + 1] = logs[at]


def attend(queries, pairs, query_pos, key_pos, head_dim):
    heads = queries.shape[1] // head_dim
    shapes = [(queries.shape, BF), ((queries.shape[0], heads), F32)]
    kernel = functools.partial(attend_kernel, head_dim)
    return rows_call(kernel, shapes, queries, query_pos, key_pos, *pairs)


def attend_back_kernel(
    head_dim, query_ref, query_pos_ref, key_pos_ref, out_ref, log_ref, grad_ref, *refs
):
    slots = (len(refs) - 1) // 2
    pairs, query_grad_ref, pair_grads = refs[:slots], refs[slots], refs[slots + 1 :]
    count = query_ref.shape[0]
    scale = head_dim ** (-0.5)
    kv_heads = pairs[0].shape[1] // (2 * head_dim)
    groups = query_ref.shape[1] // (kv_heads * head_dim)
    query_pos = jnp.concatenate([query_pos_ref[...]] * groups, axis=0)
    for kv_head in range(kv_heads):
        first = kv_head * groups
        queries = stack_heads(query_ref, first, groups, head_dim)
        grads = stack_heads(grad_ref, first, groups, head_dim)
        outputs = stack_heads(out_ref, first, groups, head_dim)
        logs = jnp.concatenate(
            [log_ref[:, first + i : first + i + 1] for i in range(groups)], axis=0
        )
        deltas = jnp.sum(grads.astype(F32) * outputs.astype(F32), axis=-1, keepdims=True)
        query_grad = jnp.zeros((groups * count, head_dim), F32)
        key_at = slice(kv_head * head_dim, (kv_head + 1) * head_dim)
        value_at = slice((kv_heads + kv_head) * head_dim, (kv_heads + kv_head + 1) * head_dim)
        for slot in range(slots):
            keys, values = pairs[slot][:, key_at], pairs[slot][:, value_at]
            scores = dot_nt(queries, keys) * scale
            causal = key_pos_ref[slot : slot + 1, :] <= query_pos
            probs = jnp.where(causal, jnp.exp(scores - logs), 0.0)
            value_grad = dot_tn(probs.astype(BF), grads)
            grad_probs = dot_nt(grads, values)
            grad_scores = (probs * (grad_probs - deltas) * scale).astype(BF)
            query_grad = query_grad + jnp.dot(grad_scores, keys, preferred_element_type=F32)
            key_grad = dot_tn(grad_scores, queries)
            pair_grads[slot][:, key_at] = key_grad.astype(pair_grads[slot].dtype)
            pair_grads[slot][:, value_at] = value_grad.astype(pair_grads[slot].dtype)
        for group in range(groups):
            head = first + group
            query_grad_ref[:, head * head_dim : (head + 1) * head_dim] = query_grad[
                group * count : (group + 1) * count
            ]


def attend_back(queries, pairs, query_pos, key_pos, outputs, logs, grads, head_dim):
    kernel = functools.partial(attend_back_kernel, head_dim)
    shapes = [(queries.shape, F32)]
    shapes += [(pair.shape, BF if slot else F32) for slot, pair in enumerate(pairs)]
    query_grad, *pair_grads = rows_call(
        kernel, shapes, queries, query_pos, key_pos, outputs, logs, grads, *pairs
    )
    return query_grad, pair_grads


class Links:
    def __init__(self, contexts, tensors):
        self.contexts, self.tensors = contexts, tensors
        self.count = contexts * tensors
        self.near = 4
        self.rows = tensors // 2
        self.half = contexts // 2
        self.far_half = self.half * tensors
        self.half_groups = [
            [(part * self.half + member) * tensors + tensor for member in range(self.half)]
            for part in range(2)
            for tensor in range(tensors)
        ]
        self.context = lax.axis_index("context")
        self.upper = self.context >= self.half

    def swap(self, value, mask):
        return lax.ppermute(value, AXES, [(i, i ^ mask) for i in range(self.count)])

    def far_masks(self):
        return [far * self.near * self.tensors for far in range(self.contexts // self.near)]

    def half_masks(self):
        return [member * self.tensors for member in range(self.half)]

    def by_part(self, mine, theirs):
        return jnp.where(self.upper, theirs, mine), jnp.where(self.upper, mine, theirs)

    def spread(self, value, masks):
        return [value] + [self.swap(value, mask) for mask in masks[1:]]

    def cube_masks(self):
        return [
            near * self.tensors + row * 2
            for near in range(self.near)
            for row in range(self.rows)
        ]

    def collect(self, chunks, masks):
        total = chunks[0].astype(F32)
        for chunk, mask in zip(chunks[1:], masks[1:]):
            total = total + self.swap(chunk.astype(BF), mask).astype(F32)
        return total

    def exchange_context(self, chunks):
        return lax.all_to_all(chunks, "context", 0, 0)

    def spread_context(self, value):
        return self.exchange_context(
            jnp.broadcast_to(value[None], (self.contexts, *value.shape))
        )

    def relative(self, slots, index):
        count, shape = slots.shape[0], slots.shape[1:]
        bit = 1
        while bit < count:
            pairs = slots.reshape(count // (2 * bit), 2, bit, *shape)
            flipped = jnp.concatenate([pairs[:, 1:], pairs[:, :1]], axis=1)
            odd = (index // bit) % 2 == 1
            slots = jnp.where(odd, flipped, pairs).reshape(count, *shape)
            bit *= 2
        return slots

    def gather_rows(self, rows):
        line = join(self.spread(rows, self.far_masks()))
        own = join(self.spread(line, self.cube_masks()))
        return own, self.swap(own, 1)

    def reduce_rows(self, own, other):
        half = own + self.swap(other.astype(BF), 1).astype(F32)
        masks = self.cube_masks()
        line = self.collect(jnp.split(half, len(masks), axis=0), masks)
        masks = self.far_masks()
        return self.collect(jnp.split(line, len(masks), axis=0), masks)

    def spread_rows(self, rows):
        for mask in (self.far_half, 2, 1):
            rows = join([rows, self.swap(rows, mask)])
        return rows

    def return_rows(self, partial):
        for mask in (1, 2, self.far_half):
            own, other = jnp.split(partial, 2, axis=0)
            partial = own + self.swap(other.astype(BF), mask).astype(F32)
        return partial

    def gather_half(self, mine, theirs):
        got = self.swap(theirs, self.far_half)
        low, high = self.by_part(mine, got)
        return jnp.stack([low, high])

    def scatter_half(self, partial):
        rows, columns = partial.shape
        shard = lax.psum_scatter(
            partial.astype(BF).reshape(2, rows // 2, columns),
            AXES,
            scatter_dimension=1,
            axis_index_groups=self.half_groups,
            tiled=True,
        )
        mine = jnp.where(self.upper, shard[1], shard[0])
        theirs = jnp.where(self.upper, shard[0], shard[1])
        got = self.swap(theirs, self.far_half)
        return [part.astype(F32) for part in self.by_part(mine, got)]


def body(
    residual_in,
    grad_output,
    block_order,
    w_query,
    key_weight,
    value_weight,
    w_out,
    w_gate,
    w_up,
    w_down,
    attn_gain,
    mlp_gain,
    query_gain,
    key_gain,
):
    contexts, tensors = lax.axis_size("context"), lax.axis_size("tensor")
    links = Links(contexts, tensors)
    masks = links.half_masks()
    layers = w_query.shape[0]
    head_dim = query_gain.shape[1]
    local_rows, width = residual_in.shape
    context_rows = local_rows * tensors
    rows_per_block = context_rows // 2
    all_rows = context_rows * contexts
    key_pos = row_positions(block_order, jnp.int32(0), all_rows, rows_per_block)
    key_pos = links.relative(key_pos.reshape(contexts, context_rows), links.context)
    key_pos = key_pos.reshape(contexts, tensors, local_rows)
    tensor = lax.axis_index("tensor")
    key_pos = links.relative(key_pos.transpose(1, 0, 2), tensor)
    key_pos = key_pos.reshape(2, 2, 2, links.half, local_rows).transpose(3, 1, 0, 2, 4)
    key_pos = key_pos.reshape(links.half, 2 * context_rows)
    query_pos = key_pos[0]
    cosine, sine = rotary_tables(query_pos, head_dim)
    tables = (
        jnp.concatenate([cosine, cosine], axis=1),
        jnp.concatenate([-sine, sine], axis=1),
    )
    query_pos = query_pos[:, None]
    query_width, kv_width = w_query.shape[2] // 2, key_weight.shape[2] // 2
    query_heads = query_width // head_dim
    kv_heads = kv_width // head_dim
    units = w_gate.shape[2] // contexts
    shard = w_query.shape[1]
    query_gains = [query_gain[layer][None] for layer in range(layers)]
    key_gains = [key_gain[layer][None] for layer in range(layers)]

    gains = jnp.concatenate([attn_gain, mlp_gain], axis=0)
    gains = links.spread_context(gains).transpose(1, 0, 2).reshape(2 * layers, width)
    gains = gains.astype(F32)

    def ffn_parts(layer):
        parts = [w_gate[layer], w_up[layer], w_down[layer].T]
        parts = [part.reshape(shard, contexts, units) for part in parts]
        return jnp.concatenate(parts, axis=2).transpose(1, 0, 2)

    attn_weights, out_weights, ffn_weights = [], [], []
    for layer in range(layers):
        parts = []
        for part in range(2):
            query_at = slice(part * query_width, (part + 1) * query_width)
            kv_at = slice(part * kv_width, (part + 1) * kv_width)
            columns = [
                w_query[layer][:, query_at],
                key_weight[layer][:, kv_at],
                value_weight[layer][:, kv_at],
                w_out[layer].T[:, query_at],
            ]
            parts.append(jnp.concatenate(columns, axis=1))
        mine, theirs = links.by_part(*parts)
        shards = links.gather_half(mine, theirs)
        gathered = []
        for columns in (
            shards[:, :, : query_width + 2 * kv_width], shards[:, :, query_width + 2 * kv_width :]
        ):
            gathered.append(
                lax.all_gather(
                    columns,
                    AXES,
                    axis=1,
                    tiled=True,
                    axis_index_groups=links.half_groups,
                )
            )
        if layer == 0:
            gathered_0 = gathered[0]
        attn_weights.append(gathered[0].reshape(width, -1))
        out_weights.append(gathered[1].reshape(width, -1))

    current = residual_in
    stored = []
    for layer in range(layers):
        gain_attn, gain_mlp = gains[layer], gains[layers + layer]
        normed_in = links.spread_rows(rms_scale(current, gain_attn).astype(BF))
        parts = ffn_parts(layer)
        parts = after(parts, gathered_0 if layer == 0 else stored[0][9][0])
        ffn_weights.append(links.exchange_context(parts).reshape(width, 3 * units))
        projected = mm(normed_in, attn_weights[layer])
        pair_proj, query_proj = projected[:, query_width:], projected[:, :query_width]
        pairs = prep_heads(pair_proj, kv_heads, key_gains[layer], tables)
        pairs = links.spread(pairs, masks)
        queries = prep_heads(query_proj, query_heads, query_gains[layer], tables)
        if layer + 1 == layers:
            top_gradient = links.gather_rows(after(grad_output, query_proj).astype(BF))
            queries = after(queries, top_gradient[0])
        output_rows, log_totals = attend(queries, pairs, query_pos, key_pos, head_dim)
        partial = mm_nt(output_rows, out_weights[layer])
        middle = current + links.return_rows(partial)
        normed_mid = links.gather_rows(rms_scale(middle, gain_mlp).astype(BF))
        inner, partial = [], []
        weights = ffn_weights[layer]
        for rows in normed_mid:
            both = mm(rows, weights[:, : 2 * units])
            gate, up = both[:, :units], both[:, units:]
            hidden = (jax.nn.silu(gate) * up).astype(BF)
            inner.append((gate, up, hidden))
            partial.append(mm_nt(hidden, weights[:, 2 * units :]))
        if layer + 1 < layers:
            block_out = middle + links.reduce_rows(*partial)
        else:
            last = (middle, partial)
        stored.append(
            (
                current,
                normed_in,
                query_proj,
                pair_proj,
                queries,
                pairs,
                output_rows,
                log_totals,
                middle,
                normed_mid,
                inner,
            )
        )
        if layer + 1 < layers:
            current = block_out

    grad_res = grad_output
    weight_grads, gain_grads = [None] * layers, [None] * layers
    for layer in reversed(range(layers)):
        (
            layer_in,
            normed_in,
            query_proj,
            pair_proj,
            queries,
            pairs,
            output_rows,
            log_totals,
            middle,
            normed_mid,
            inner,
        ) = stored[layer]
        gain_attn, gain_mlp = gains[layer], gains[layers + layer]
        if layer + 1 == layers:
            grad_all = top_gradient
        else:
            grad_all = links.gather_rows(grad_res.astype(BF))
        partial, d_in, d_down = [], 0.0, 0.0
        weights = ffn_weights[layer]
        for rows, grad_rows, (gate, up, hidden) in zip(normed_mid, grad_all, inner):
            grad_hidden = mm(grad_rows, weights[:, 2 * units :])
            sigmoid = jax.nn.sigmoid(gate)
            grad_up = (grad_hidden * gate * sigmoid).astype(BF)
            grad_gate = (
                grad_hidden * up * sigmoid * (1.0 + gate * (1.0 - sigmoid))
            ).astype(BF)
            both = jnp.concatenate([grad_gate, grad_up], axis=1)
            partial.append(mm_nt(both, weights[:, : 2 * units]))
            d_in = d_in + mm_tn(rows, both)
            d_down = d_down + mm_tn(grad_rows, hidden)
        grad_normed_mid = links.reduce_rows(*partial)
        unused, norm_back = jax.vjp(rms_scale, middle, gain_mlp)
        grad_mid_part, d_mlp_gain = norm_back(grad_normed_mid)
        grad_mid = grad_res + grad_mid_part
        pieces = jnp.concatenate([d_in, d_down], axis=1).astype(BF)
        if layer + 1 < layers:
            pieces = after(pieces, moved)
        pieces = links.exchange_context(pieces.reshape(contexts, shard, 3 * units))
        moved = pieces
        pieces = pieces.transpose(1, 0, 2)
        d_gate = pieces[:, :, :units].reshape(shard, contexts * units).astype(F32)
        d_up = pieces[:, :, units : 2 * units].reshape(shard, contexts * units).astype(F32)
        d_down = pieces[:, :, 2 * units :].reshape(shard, contexts * units).T.astype(F32)
        if layer + 1 == layers:
            middle_last, partial_last = last
            partial_last = after(partial_last, grad_mid)
            final_out = middle_last + links.reduce_rows(*partial_last)
        grad_mid_all = links.spread_rows(grad_mid.astype(BF))
        d_out = links.scatter_half(mm_tn(grad_mid_all, output_rows))
        d_out = jnp.concatenate(d_out, axis=1).T
        attention_gradient = mm(grad_mid_all, out_weights[layer]).astype(BF)
        query_grad, pair_grads = attend_back(
            queries,
            pairs,
            query_pos,
            key_pos,
            output_rows,
            log_totals,
            attention_gradient,
            head_dim,
        )
        pair_grads = [pair_grads[0]] + [
            links.swap(grad, mask) for grad, mask in zip(pair_grads[1:], masks[1:])
        ]
        grad_queries, d_query_gain = prep_heads_back(
            query_proj, query_heads, query_gains[layer], tables, [query_grad]
        )
        grad_pairs, d_key_gain = prep_heads_back(
            pair_proj, kv_heads, key_gains[layer], tables, pair_grads
        )
        grad_projected = jnp.concatenate([grad_queries, grad_pairs], axis=1)
        partial = mm_nt(grad_projected, attn_weights[layer])
        if layer + 1 == layers:
            partial = after(partial, final_out)
        grad_normed_in = links.return_rows(partial)
        unused, input_back = jax.vjp(rms_scale, layer_in, gain_attn)
        grad_in_part, d_attn_gain = input_back(grad_normed_in)
        grad_res = grad_mid + grad_in_part
        halves = links.scatter_half(mm_tn(normed_in, grad_projected))
        cuts = [query_width, query_width + kv_width]
        d_query, d_key, d_value = [
            jnp.concatenate(pair, axis=1)
            for pair in zip(*[jnp.split(half, cuts, axis=1) for half in halves])
        ]
        weight_grads[layer] = (
            d_query,
            d_key,
            d_value,
            d_out,
            d_gate,
            d_up,
            d_down,
        )
        gain_grads[layer] = (d_attn_gain, d_mlp_gain, d_query_gain[0], d_key_gain[0])

    wide = jnp.stack([g[0] for g in gain_grads] + [g[1] for g in gain_grads])
    wide = wide.reshape(2 * layers, contexts, shard).transpose(1, 0, 2)
    narrow = jnp.stack([g[2] for g in gain_grads] + [g[3] for g in gain_grads])
    wide = wide.reshape(contexts, 1, 2 * layers * shard)
    narrow = jnp.broadcast_to(
        narrow.reshape(1, 1, 2 * layers * head_dim), (contexts, 1, 2 * layers * head_dim)
    )
    pieces = jnp.concatenate([wide, narrow], axis=2)
    pieces = jnp.broadcast_to(pieces, (contexts, tensors, pieces.shape[2]))
    pieces = after(pieces.reshape(contexts * tensors, -1), moved)
    sums = jnp.sum(lax.all_to_all(pieces, AXES, 0, 0, tiled=True), axis=0)
    wide = sums[: 2 * layers * shard].reshape(2, layers, shard)
    narrow = sums[2 * layers * shard :].reshape(2, layers, head_dim)
    stacked = [jnp.stack([grads[member] for grads in weight_grads]) for member in range(7)]
    return (final_out, grad_res, *stacked, wide[0], wide[1], narrow[0], narrow[1])


def solution(mesh):
    rows = P(("context", "tensor"), None)
    in_split = P(None, "context", "tensor")
    out_split = P(None, "tensor", "context")
    gain = P(None, "context")
    weights = (in_split, in_split, in_split, out_split, in_split, in_split, out_split)
    return jax.shard_map(
        body,
        mesh=mesh,
        in_specs=(rows, rows, P(), *weights, gain, gain, P(), P()),
        out_specs=(rows, rows, *weights, gain, gain, P(), P()),
        check_vma=False,
    )
```

profile of v0, /device:TPU:0, one launch (start us, length us, event | category | flops | bytes accessed | tf_op | source)
XLA Modules:
  0.0 1042.1 jit_solution(12762319839858959805)
XLA Ops:
  8.6 7.3 all-to-all-start
  25.5 16.6 %collective-permute-done.3 = bf16[256,768]{1,0:T(8,128)(2,1)S(1)} collective-permute-done((bf16[256,768]{1,0:T(8,128)(2,1)S(1)}, bf16[256,768]{1,0:T(8,128)(2,1)S(1)}, u32[]{:S(2)}, u32[]{:S(2)}) %collective-permute-start.3) | collective-permute-done | bytes 393248 | tf_op jit(solution)/shard_map/ppermute | solution.py:236
  46.2 8.0 collective-permute-done.refs_1_
  63.5 25.0 %all-gather.5.cloned.1.call-done = bf16[2,1024,512]{2,1,0:T(8,128)(2,1)} async-done(((bf16[2,256,512]{2,1,0:T(8,128)(2,1)}), bf16[2,1024,512]{2,1,0:T(8,128)(2,1)}) %all-gather.5.cloned.1.call-update) | async-done | bytes 2097168 | tf_op jit(solution)/shard_map/all_gather | solution.py:401
  107.7 10.1 all-gather.7.cloned.1.call-done
  132.3 5.4 all-to-all-start.1
  140.9 56.4 %collective-permute-done.9 = bf16[32,2048]{1,0:T(8,128)(2,1)S(1)} collective-permute-done((bf16[32,2048]{1,0:T(8,128)(2,1)S(1)}, bf16[32,2048]{1,0:T(8,128)(2,1)S(1)}, u32[]{:S(2)}, u32[]{:S(2)}) %collective-permute-start.9) | collective-permute-done | bytes 131104 | tf_op jit(solution)/shard_map/ppermute | solution.py:236
  197.6 7.9 collective-permute-done.10.refs_1_
  222.8 8.0 collective-permute-done.15.refs_5_
  250.8 19.8 %collective-permute-done.31 = bf16[256,768]{1,0:T(8,128)(2,1)S(1)} collective-permute-done((bf16[256,768]{1,0:T(8,128)(2,1)S(1)}, bf16[256,768]{1,0:T(8,128)(2,1)S(1)}, u32[]{:S(2)}, u32[]{:S(2)}) %collective-permute-start.31) | collective-permute-done | bytes 393248 | tf_op jit(solution)/shard_map/ppermute | solution.py:236
  300.7 8.8 collective-permute-done.24
  309.5 6.9 collective-permute-done.23
  316.8 16.0 %collective-permute-done.21 = bf16[64,2048]{1,0:T(8,128)(2,1)S(1)} collective-permute-done((bf16[64,2048]{1,0:T(8,128)(2,1)S(1)}, bf16[64,2048]{1,0:T(8,128)(2,1)S(1)}, u32[]{:S(2)}, u32[]{:S(2)}) %collective-permute-start.21) | collective-permute-done | bytes 262176 | tf_op jit(solution)/shard_map/ppermute | solution.py:236
  335.6 6.9 collective-permute-done.27
  343.4 8.5 collective-permute-done.28.refs_1_
  353.3 6.5 collective-permute-done.29.refs_1_
  364.8 8.7 collective-permute-done.32.refs_1_
  379.5 6.1 collective-permute-done.39.refs_7_
  385.6 4.9 collective-permute-done.38.refs_6_
  391.9 4.8 collective-permute-done.37.refs_5_
  398.8 5.9 collective-permute-done.36.refs_4_
  406.3 5.5 collective-permute-done.34.refs_2_
  438.2 55.1 %collective-permute-done.45 = bf16[32,2048]{1,0:T(8,128)(2,1)S(1)} collective-permute-done((bf16[32,2048]{1,0:T(8,128)(2,1)S(1)}, bf16[32,2048]{1,0:T(8,128)(2,1)S(1)}, u32[]{:S(2)}, u32[]{:S(2)}) %collective-permute-start.45) | collective-permute-done | bytes 131104 | tf_op jit(solution)/shard_map/ppermute | solution.py:236
  494.3 7.9 collective-permute-done.46.refs_1_
  519.5 8.0 collective-permute-done.51.refs_5_
  556.5 7.5 collective-permute-done.57
  567.3 8.5 collective-permute-done.61
  582.9 6.5 collective-permute-done.64
  591.0 8.6 collective-permute-done.74.refs_1_
  600.7 7.3 collective-permute-done.75.refs_1_
  622.2 6.0 collective-permute-done.77.refs_1_
  638.5 9.0 collective-permute-done.70
  655.0 7.3 collective-permute-done.73
  666.5 7.3 collective-permute-done.81
  674.0 7.4 collective-permute-done.82
  683.0 8.7 collective-permute-done.83.refs_1_
  708.9 8.2 collective-permute-done.88.refs_5_
  779.3 26.7 %collective-permute-done.99 = bf16[64,2048]{1,0:T(8,128)(2,1)S(1)} collective-permute-done((bf16[64,2048]{1,0:T(8,128)(2,1)S(1)}, bf16[64,2048]{1,0:T(8,128)(2,1)S(1)}, u32[]{:S(2)}, u32[]{:S(2)}) %collective-permute-start.99) | collective-permute-done | bytes 262176 | tf_op jit(solution)/shard_map/ppermute | solution.py:236
  806.0 12.2 %collective-permute-start.94 = (bf16[64,2048]{1,0:T(8,128)(2,1)S(1)}, bf16[64,2048]{1,0:T(8,128)(2,1)S(1)}, u32[]{:S(2)}, u32[]{:S(2)}) collective-permute-start(bf16[64,2048]{1,0:T(8,128)(2,1)S(1)} %get-tuple-element.174), channel_id=1, source_target_pairs={{0,4},{1,5},{2,6},{3,7},{4,0},{5,1},{6,2},{7,3},{8,12},{9,13},{10,... | collective-permute-start | bytes 786440 | tf_op jit(solution)/shard_map/ppermute | solution.py:236
  823.5 9.1 collective-permute-done.96
  836.0 6.9 collective-permute-start.100
  859.8 51.9 %collective-permute-done.101.refs_1_ = bf16[32,2048]{1,0:T(8,128)(2,1)S(1)} collective-permute-done((bf16[32,2048]{1,0:T(8,128)(2,1)S(1)}, bf16[32,2048]{1,0:T(8,128)(2,1)S(1)}, u32[]{:S(2)}, u32[]{:S(2)}) %collective-permute-start.101) | collective-permute-done | bytes 131104 | tf_op jit(solution)/shard_map/ppermute | solution.py:236
  919.0 8.8 collective-permute-done.113
  948.6 9.6 collective-permute-done.104.refs_1_
  983.5 5.7 all-to-all-start.5
  990.1 9.3 all-to-all-done.5
  1003.7 12.3 %reduce-scatter.5.cloned.1.call-done = bf16[2,256,512]{2,1,0:T(8,128)(2,1)} async-done(((bf16[2,1024,512]{2,1,0:T(8,128)(2,1)}), bf16[2,256,512]{2,1,0:T(8,128)(2,1)}) %reduce-scatter.5.cloned.1.call-update) | async-done | bytes 524304 | tf_op jit(solution)/shard_map/reduce_scatter | solution.py:312
  1021.7 10.0 collective-permute-done.110
  (752 shorter events, 445.0 us)
Async XLA Ops:
  8.6 35.7 %all-to-all-start = ((bf16[8,4,256]{2,1,0:T(4,128)(2,1)}), bf16[8,4,256]{2,1,0:T(4,128)(2,1)S(1)}, u32[]{:S(2)}, u32[]{:S(2)}) async-start(bf16[8,4,256]{2,1,0:T(4,128)(2,1)} %broadcast_in_dim.30), calls=%async_computation | async-start | bytes 32768 | tf_op jit(solution)/shard_map/all_to_all | solution.py:264
  15.8 72.7 %all-gather.5.cloned.1.call-start = ((), (), s32[]{:S(2)}) async-start(), calls=%async_computation.10 | async-start | bytes 2621440 | tf_op jit(solution)/shard_map/all_gather | solution.py:401
  22.1 20.0 %collective-permute-start.3 = (bf16[256,768]{1,0:T(8,128)(2,1)S(1)}, bf16[256,768]{1,0:T(8,128)(2,1)S(1)}, u32[]{:S(2)}, u32[]{:S(2)}) collective-permute-start(bf16[256,768]{1,0:T(8,128)(2,1)S(1)} %broadcast_select_fusion.3), channel_id=1, source_target_pairs={{0,16},{1,17},{2,18},{3,19},{4,20},{5,21},{6,22},{7,23},{8,24},{9,... | collective-permute-start | bytes 1179656 | tf_op jit(solution)/shard_map/ppermute | solution.py:236
  43.1 74.7 %all-gather.7.cloned.1.call-start = ((), (), s32[]{:S(2)}) async-start(), calls=%async_computation.11 | async-start | bytes 1310720 | tf_op jit(solution)/shard_map/all_gather | solution.py:401
  132.3 104.2 %all-to-all-start.1 = ((bf16[8,256,576]{1,2,0:T(8,128)(2,1)}), bf16[8,256,576]{1,2,0:T(8,128)(2,1)}, u32[]{:S(2)}, u32[]{:S(2)}) async-start(bf16[8,256,576]{1,2,0:T(8,128)(2,1)} %maximum_bitcast_fusion), calls=%async_computation.1 | async-start | bytes 4718592 | tf_op jit(solution)/shard_map/all_to_all | solution.py:264
  137.8 224.2 %all-gather.9.cloned.1.call-start = ((), (), s32[]{:S(2)}) async-start(), calls=%async_computation.12 | async-start | bytes 2621440 | tf_op jit(solution)/shard_map/all_gather | solution.py:401
  137.9 59.4 %collective-permute-start.9 = (bf16[32,2048]{1,0:T(8,128)(2,1)S(1)}, bf16[32,2048]{1,0:T(8,128)(2,1)S(1)}, u32[]{:S(2)}, u32[]{:S(2)}) collective-permute-start(bf16[32,2048]{1,0:T(8,128)(2,1)S(1)} %split.554), channel_id=1, source_target_pairs={{0,16},{1,17},{2,18},{3,19},{4,20},{5,21},{6,22},{7,23},{8,24},{9,... | collective-permute-start | bytes 393224 | tf_op jit(solution)/shard_map/ppermute | solution.py:236
  209.7 21.1 %collective-permute-start.15 = (bf16[64,2048]{1,0:T(8,128)(2,1)S(1)}, bf16[64,2048]{1,0:T(8,128)(2,1)S(1)}, u32[]{:S(2)}, u32[]{:S(2)}) collective-permute-start(bf16[64,2048]{1,0:T(8,128)(2,1)S(1)} %shard_map.243.refs_0_), channel_id=1, source_target_pairs={{0,10},{1,11},{2,8},{3,9},{4,14},{5,15},{6,12},{7,13},{8,2},{9,3},... | collective-permute-start | bytes 786440 | tf_op jit(solution)/shard_map/ppermute | solution.py:236
  209.7 25.3 %collective-permute-start.14 = (bf16[64,2048]{1,0:T(8,128)(2,1)S(1)}, bf16[64,2048]{1,0:T(8,128)(2,1)S(1)}, u32[]{:S(2)}, u32[]{:S(2)}) collective-permute-start(bf16[64,2048]{1,0:T(8,128)(2,1)S(1)} %shard_map.243.refs_0_), channel_id=1, source_target_pairs={{0,8},{1,9},{2,10},{3,11},{4,12},{5,13},{6,14},{7,15},{8,0},{9,1},... | collective-permute-start | bytes 786440 | tf_op jit(solution)/shard_map/ppermute | solution.py:236
  211.4 23.6 %collective-permute-start.13 = (bf16[64,2048]{1,0:T(8,128)(2,1)S(1)}, bf16[64,2048]{1,0:T(8,128)(2,1)S(1)}, u32[]{:S(2)}, u32[]{:S(2)}) collective-permute-start(bf16[64,2048]{1,0:T(8,128)(2,1)S(1)} %shard_map.243.refs_0_), channel_id=1, source_target_pairs={{0,6},{1,7},{2,4},{3,5},{4,2},{5,3},{6,0},{7,1},{8,14},{9,15},{10,... | collective-permute-start | bytes 786440 | tf_op jit(solution)/shard_map/ppermute | solution.py:236
  245.6 31.6 %collective-permute-start.19 = (bf16[512,2048]{1,0:T(8,128)(2,1)}, bf16[512,2048]{1,0:T(8,128)(2,1)}, u32[]{:S(2)}, u32[]{:S(2)}) collective-permute-start(bf16[512,2048]{1,0:T(8,128)(2,1)} %convolution_convert_fusion.2), channel_id=1, source_target_pairs={{0,1},{1,0},{2,3},{3,2},{4,5},{5,4},{6,7},{7,6},{8,9},{9,8},{10,11... | collective-permute-start | bytes 6291464 | tf_op jit(solution)/shard_map/ppermute | solution.py:236
  249.8 20.8 %collective-permute-start.31 = (bf16[256,768]{1,0:T(8,128)(2,1)S(1)}, bf16[256,768]{1,0:T(8,128)(2,1)S(1)}, u32[]{:S(2)}, u32[]{:S(2)}) collective-permute-start(bf16[256,768]{1,0:T(8,128)(2,1)S(1)} %broadcast_select_fusion.1), channel_id=1, source_target_pairs={{0,16},{1,17},{2,18},{3,19},{4,20},{5,21},{6,22},{7,23},{8,24},{9,... | collective-permute-start | bytes 1179656 | tf_op jit(solution)/shard_map/ppermute | solution.py:236
  273.6 142.6 %all-gather.11.cloned.1.call-start = ((), (), s32[]{:S(2)}) async-start(), calls=%async_computation.13 | async-start | bytes 1310720 | tf_op jit(solution)/shard_map/all_gather | solution.py:401
  284.7 24.8 %collective-permute-start.24 = (bf16[64,2048]{1,0:T(8,128)(2,1)S(1)}, bf16[64,2048]{1,0:T(8,128)(2,1)S(1)}, u32[]{:S(2)}, u32[]{:S(2)}) collective-permute-start(bf16[64,2048]{1,0:T(8,128)(2,1)S(1)} %get-tuple-element.192), channel_id=1, source_target_pairs={{0,10},{1,11},{2,8},{3,9},{4,14},{5,15},{6,12},{7,13},{8,2},{9,3},... | collective-permute-start | bytes 786440 | tf_op jit(solution)/shard_map/ppermute | solution.py:236
  284.8 31.7 %collective-permute-start.23 = (bf16[64,2048]{1,0:T(8,128)(2,1)S(1)}, bf16[64,2048]{1,0:T(8,128)(2,1)S(1)}, u32[]{:S(2)}, u32[]{:S(2)}) collective-permute-start(bf16[64,2048]{1,0:T(8,128)(2,1)S(1)} %get-tuple-element.193), channel_id=1, source_target_pairs={{0,8},{1,9},{2,10},{3,11},{4,12},{5,13},{6,14},{7,15},{8,0},{9,1},... | collective-permute-start | bytes 786440 | tf_op jit(solution)/shard_map/ppermute | solution.py:236
  290.7 26.0 %collective-permute-start.22 = (bf16[64,2048]{1,0:T(8,128)(2,1)S(1)}, bf16[64,2048]{1,0:T(8,128)(2,1)S(1)}, u32[]{:S(2)}, u32[]{:S(2)}) collective-permute-start(bf16[64,2048]{1,0:T(8,128)(2,1)S(1)} %get-tuple-element.194), channel_id=1, source_target_pairs={{0,6},{1,7},{2,4},{3,5},{4,2},{5,3},{6,0},{7,1},{8,14},{9,15},{10,... | collective-permute-start | bytes 786440 | tf_op jit(solution)/shard_map/ppermute | solution.py:236
  296.0 36.7 %collective-permute-start.21 = (bf16[64,2048]{1,0:T(8,128)(2,1)S(1)}, bf16[64,2048]{1,0:T(8,128)(2,1)S(1)}, u32[]{:S(2)}, u32[]{:S(2)}) collective-permute-start(bf16[64,2048]{1,0:T(8,128)(2,1)S(1)} %get-tuple-element.195), channel_id=1, source_target_pairs={{0,4},{1,5},{2,6},{3,7},{4,0},{5,1},{6,2},{7,3},{8,12},{9,13},{10,... | collective-permute-start | bytes 786440 | tf_op jit(solution)/shard_map/ppermute | solution.py:236
  377.7 26.9 %collective-permute-start.36 = (bf16[64,2048]{1,0:T(8,128)(2,1)S(1)}, bf16[64,2048]{1,0:T(8,128)(2,1)S(1)}, u32[]{:S(2)}, u32[]{:S(2)}) collective-permute-start(bf16[64,2048]{1,0:T(8,128)(2,1)S(1)} %shard_map.249.refs_0_), channel_id=1, source_target_pairs={{0,8},{1,9},{2,10},{3,11},{4,12},{5,13},{6,14},{7,15},{8,0},{9,1},... | collective-permute-start | bytes 786440 | tf_op jit(solution)/shard_map/ppermute | solution.py:236
  379.5 25.8 %collective-permute-start.35 = (bf16[64,2048]{1,0:T(8,128)(2,1)S(1)}, bf16[64,2048]{1,0:T(8,128)(2,1)S(1)}, u32[]{:S(2)}, u32[]{:S(2)}) collective-permute-start(bf16[64,2048]{1,0:T(8,128)(2,1)S(1)} %shard_map.249.refs_0_), channel_id=1, source_target_pairs={{0,6},{1,7},{2,4},{3,5},{4,2},{5,3},{6,0},{7,1},{8,14},{9,15},{10,... | collective-permute-start | bytes 786440 | tf_op jit(solution)/shard_map/ppermute | solution.py:236
  385.6 26.2 %collective-permute-start.34 = (bf16[64,2048]{1,0:T(8,128)(2,1)S(1)}, bf16[64,2048]{1,0:T(8,128)(2,1)S(1)}, u32[]{:S(2)}, u32[]{:S(2)}) collective-permute-start(bf16[64,2048]{1,0:T(8,128)(2,1)S(1)} %shard_map.249.refs_0_), channel_id=1, source_target_pairs={{0,4},{1,5},{2,6},{3,7},{4,0},{5,1},{6,2},{7,3},{8,12},{9,13},{10,... | collective-permute-start | bytes 786440 | tf_op jit(solution)/shard_map/ppermute | solution.py:236
  390.5 21.2 %collective-permute-start.33 = (bf16[64,2048]{1,0:T(8,128)(2,1)S(1)}, bf16[64,2048]{1,0:T(8,128)(2,1)S(1)}, u32[]{:S(2)}, u32[]{:S(2)}) collective-permute-start(bf16[64,2048]{1,0:T(8,128)(2,1)S(1)} %shard_map.249.refs_0_), channel_id=1, source_target_pairs={{0,2},{1,3},{2,0},{3,1},{4,6},{5,7},{6,4},{7,5},{8,10},{9,11},{10,... | collective-permute-start | bytes 786440 | tf_op jit(solution)/shard_map/ppermute | solution.py:236
  429.1 104.6 %all-to-all-start.2 = ((bf16[8,256,576]{1,2,0:T(8,128)(2,1)}), bf16[8,256,576]{1,2,0:T(8,128)(2,1)}, u32[]{:S(2)}, u32[]{:S(2)}) async-start(bf16[8,256,576]{1,2,0:T(8,128)(2,1)} %maximum_bitcast_fusion.1), calls=%async_computation.2 | async-start | bytes 4718592 | tf_op jit(solution)/shard_map/all_to_all | solution.py:264
  433.8 478.8 %reduce-scatter.11.cloned.1.call-start = ((), (), s32[]{:S(2)}) async-start(), calls=%async_computation.17 | async-start | bytes 1310720 | tf_op jit(solution)/shard_map/reduce_scatter | solution.py:312
  435.3 58.0 %collective-permute-start.45 = (bf16[32,2048]{1,0:T(8,128)(2,1)S(1)}, bf16[32,2048]{1,0:T(8,128)(2,1)S(1)}, u32[]{:S(2)}, u32[]{:S(2)}) collective-permute-start(bf16[32,2048]{1,0:T(8,128)(2,1)S(1)} %split.552), channel_id=1, source_target_pairs={{0,16},{1,17},{2,18},{3,19},{4,20},{5,21},{6,22},{7,23},{8,24},{9,... | collective-permute-start | bytes 393224 | tf_op jit(solution)/shard_map/ppermute | solution.py:236
  505.2 22.3 %collective-permute-start.51 = (bf16[64,2048]{1,0:T(8,128)(2,1)S(1)}, bf16[64,2048]{1,0:T(8,128)(2,1)S(1)}, u32[]{:S(2)}, u32[]{:S(2)}) collective-permute-start(bf16[64,2048]{1,0:T(8,128)(2,1)S(1)} %shard_map.253.refs_0_), channel_id=1, source_target_pairs={{0,10},{1,11},{2,8},{3,9},{4,14},{5,15},{6,12},{7,13},{8,2},{9,3},... | collective-permute-start | bytes 786440 | tf_op jit(solution)/shard_map/ppermute | solution.py:236
  506.2 25.0 %collective-permute-start.50 = (bf16[64,2048]{1,0:T(8,128)(2,1)S(1)}, bf16[64,2048]{1,0:T(8,128)(2,1)S(1)}, u32[]{:S(2)}, u32[]{:S(2)}) collective-permute-start(bf16[64,2048]{1,0:T(8,128)(2,1)S(1)} %shard_map.253.refs_0_), channel_id=1, source_target_pairs={{0,8},{1,9},{2,10},{3,11},{4,12},{5,13},{6,14},{7,15},{8,0},{9,1},... | collective-permute-start | bytes 786440 | tf_op jit(solution)/shard_map/ppermute | solution.py:236
  508.1 23.1 %collective-permute-start.49 = (bf16[64,2048]{1,0:T(8,128)(2,1)S(1)}, bf16[64,2048]{1,0:T(8,128)(2,1)S(1)}, u32[]{:S(2)}, u32[]{:S(2)}) collective-permute-start(bf16[64,2048]{1,0:T(8,128)(2,1)S(1)} %shard_map.253.refs_0_), channel_id=1, source_target_pairs={{0,6},{1,7},{2,4},{3,5},{4,2},{5,3},{6,0},{7,1},{8,14},{9,15},{10,... | collective-permute-start | bytes 786440 | tf_op jit(solution)/shard_map/ppermute | solution.py:236
  554.5 21.3 %collective-permute-start.61 = (bf16[64,2048]{1,0:T(8,128)(2,1)S(1)}, bf16[64,2048]{1,0:T(8,128)(2,1)S(1)}, u32[]{:S(2)}, u32[]{:S(2)}) collective-permute-start(bf16[64,2048]{1,0:T(8,128)(2,1)S(1)} %get-tuple-element.185), channel_id=1, source_target_pairs={{0,10},{1,11},{2,8},{3,9},{4,14},{5,15},{6,12},{7,13},{8,2},{9,3},... | collective-permute-start | bytes 786440 | tf_op jit(solution)/shard_map/ppermute | solution.py:236
  554.8 24.4 %collective-permute-start.60 = (bf16[64,2048]{1,0:T(8,128)(2,1)S(1)}, bf16[64,2048]{1,0:T(8,128)(2,1)S(1)}, u32[]{:S(2)}, u32[]{:S(2)}) collective-permute-start(bf16[64,2048]{1,0:T(8,128)(2,1)S(1)} %get-tuple-element.186), channel_id=1, source_target_pairs={{0,8},{1,9},{2,10},{3,11},{4,12},{5,13},{6,14},{7,15},{8,0},{9,1},... | collective-permute-start | bytes 786440 | tf_op jit(solution)/shard_map/ppermute | solution.py:236
  631.1 19.5 %collective-permute-start.69 = (bf16[64,2048]{1,0:T(8,128)(2,1)}, bf16[64,2048]{1,0:T(8,128)(2,1)S(1)}, u32[]{:S(2)}, u32[]{:S(2)}) collective-permute-start(bf16[64,2048]{1,0:T(8,128)(2,1)} %get-tuple-element.179), channel_id=1, source_target_pairs={{0,8},{1,9},{2,10},{3,11},{4,12},{5,13},{6,14},{7,15},{8,0},{9,1},... | collective-permute-start | bytes 786440 | tf_op jit(solution)/shard_map/ppermute | solution.py:236
  631.1 19.5 %collective-permute-start.68 = (bf16[64,2048]{1,0:T(8,128)(2,1)S(1)}, bf16[64,2048]{1,0:T(8,128)(2,1)S(1)}, u32[]{:S(2)}, u32[]{:S(2)}) collective-permute-start(bf16[64,2048]{1,0:T(8,128)(2,1)S(1)} %get-tuple-element.180), channel_id=1, source_target_pairs={{0,6},{1,7},{2,4},{3,5},{4,2},{5,3},{6,0},{7,1},{8,14},{9,15},{10,... | collective-permute-start | bytes 786440 | tf_op jit(solution)/shard_map/ppermute | solution.py:236
  632.7 19.6 %collective-permute-start.67 = (bf16[64,2048]{1,0:T(8,128)(2,1)S(1)}, bf16[64,2048]{1,0:T(8,128)(2,1)S(1)}, u32[]{:S(2)}, u32[]{:S(2)}) collective-permute-start(bf16[64,2048]{1,0:T(8,128)(2,1)S(1)} %get-tuple-element.181), channel_id=1, source_target_pairs={{0,4},{1,5},{2,6},{3,7},{4,0},{5,1},{6,2},{7,3},{8,12},{9,13},{10,... | collective-permute-start | bytes 786440 | tf_op jit(solution)/shard_map/ppermute | solution.py:236
  695.1 22.1 %collective-permute-start.88 = (bf16[64,2048]{1,0:T(8,128)(2,1)S(1)}, bf16[64,2048]{1,0:T(8,128)(2,1)S(1)}, u32[]{:S(2)}, u32[]{:S(2)}) collective-permute-start(bf16[64,2048]{1,0:T(8,128)(2,1)S(1)} %shard_map.261.refs_0_), channel_id=1, source_target_pairs={{0,10},{1,11},{2,8},{3,9},{4,14},{5,15},{6,12},{7,13},{8,2},{9,3},... | collective-permute-start | bytes 786440 | tf_op jit(solution)/shard_map/ppermute | solution.py:236
  695.1 25.3 %collective-permute-start.87 = (bf16[64,2048]{1,0:T(8,128)(2,1)S(1)}, bf16[64,2048]{1,0:T(8,128)(2,1)S(1)}, u32[]{:S(2)}, u32[]{:S(2)}) collective-permute-start(bf16[64,2048]{1,0:T(8,128)(2,1)S(1)} %shard_map.261.refs_0_), channel_id=1, source_target_pairs={{0,8},{1,9},{2,10},{3,11},{4,12},{5,13},{6,14},{7,15},{8,0},{9,1},... | collective-permute-start | bytes 786440 | tf_op jit(solution)/shard_map/ppermute | solution.py:236
  697.6 22.9 %collective-permute-start.86 = (bf16[64,2048]{1,0:T(8,128)(2,1)S(1)}, bf16[64,2048]{1,0:T(8,128)(2,1)S(1)}, u32[]{:S(2)}, u32[]{:S(2)}) collective-permute-start(bf16[64,2048]{1,0:T(8,128)(2,1)S(1)} %shard_map.261.refs_0_), channel_id=1, source_target_pairs={{0,6},{1,7},{2,4},{3,5},{4,2},{5,3},{6,0},{7,1},{8,14},{9,15},{10,... | collective-permute-start | bytes 786440 | tf_op jit(solution)/shard_map/ppermute | solution.py:236
  742.3 21.8 %collective-permute-start.92 = (bf16[512,2048]{1,0:T(8,128)(2,1)}, bf16[512,2048]{1,0:T(8,128)(2,1)}, u32[]{:S(2)}, u32[]{:S(2)}) collective-permute-start(bf16[512,2048]{1,0:T(8,128)(2,1)} %convolution_convert_fusion.3), channel_id=1, source_target_pairs={{0,1},{1,0},{2,3},{3,2},{4,5},{5,4},{6,7},{7,6},{8,9},{9,8},{10,11... | collective-permute-start | bytes 6291464 | tf_op jit(solution)/shard_map/ppermute | solution.py:236
  749.8 94.7 %all-to-all-start.3 = ((bf16[8,256,576]{1,2,0:T(8,128)(2,1)}), bf16[8,256,576]{1,2,0:T(8,128)(2,1)}, u32[]{:S(2)}, u32[]{:S(2)}) async-start(bf16[8,256,576]{1,2,0:T(8,128)(2,1)} %pad_maximum_fusion.1), calls=%async_computation.7 | async-start | bytes 4718592 | tf_op jit(solution)/shard_map/all_to_all | solution.py:264
  754.3 159.4 %reduce-scatter.7.cloned.1.call-start = ((), (), s32[]{:S(2)}) async-start(), calls=%async_computation.15 | async-start | bytes 2621440 | tf_op jit(solution)/shard_map/reduce_scatter | solution.py:312
  768.8 37.2 %collective-permute-start.99 = (bf16[64,2048]{1,0:T(8,128)(2,1)S(1)}, bf16[64,2048]{1,0:T(8,128)(2,1)S(1)}, u32[]{:S(2)}, u32[]{:S(2)}) collective-permute-start(bf16[64,2048]{1,0:T(8,128)(2,1)S(1)} %get-tuple-element.169), channel_id=1, source_target_pairs={{0,14},{1,15},{2,12},{3,13},{4,10},{5,11},{6,8},{7,9},{8,6},{9,7},... | collective-permute-start | bytes 786440 | tf_op jit(solution)/shard_map/ppermute | solution.py:236
  774.3 46.2 %collective-permute-start.98 = (bf16[64,2048]{1,0:T(8,128)(2,1)S(1)}, bf16[64,2048]{1,0:T(8,128)(2,1)S(1)}, u32[]{:S(2)}, u32[]{:S(2)}) collective-permute-start(bf16[64,2048]{1,0:T(8,128)(2,1)S(1)} %get-tuple-element.170), channel_id=1, source_target_pairs={{0,12},{1,13},{2,14},{3,15},{4,8},{5,9},{6,10},{7,11},{8,4},{9,5},... | collective-permute-start | bytes 786440 | tf_op jit(solution)/shard_map/ppermute | solution.py:236
  774.6 48.9 %collective-permute-start.97 = (bf16[64,2048]{1,0:T(8,128)(2,1)S(1)}, bf16[64,2048]{1,0:T(8,128)(2,1)S(1)}, u32[]{:S(2)}, u32[]{:S(2)}) collective-permute-start(bf16[64,2048]{1,0:T(8,128)(2,1)S(1)} %get-tuple-element.171), channel_id=1, source_target_pairs={{0,10},{1,11},{2,8},{3,9},{4,14},{5,15},{6,12},{7,13},{8,2},{9,3},... | collective-permute-start | bytes 786440 | tf_op jit(solution)/shard_map/ppermute | solution.py:236
  776.8 55.8 %collective-permute-start.96 = (bf16[64,2048]{1,0:T(8,128)(2,1)S(1)}, bf16[64,2048]{1,0:T(8,128)(2,1)S(1)}, u32[]{:S(2)}, u32[]{:S(2)}) collective-permute-start(bf16[64,2048]{1,0:T(8,128)(2,1)S(1)} %get-tuple-element.172), channel_id=1, source_target_pairs={{0,8},{1,9},{2,10},{3,11},{4,12},{5,13},{6,14},{7,15},{8,0},{9,1},... | collective-permute-start | bytes 786440 | tf_op jit(solution)/shard_map/ppermute | solution.py:236
  776.9 55.7 %collective-permute-start.95 = (bf16[64,2048]{1,0:T(8,128)(2,1)S(1)}, bf16[64,2048]{1,0:T(8,128)(2,1)S(1)}, u32[]{:S(2)}, u32[]{:S(2)}) collective-permute-start(bf16[64,2048]{1,0:T(8,128)(2,1)S(1)} %get-tuple-element.173), channel_id=1, source_target_pairs={{0,6},{1,7},{2,4},{3,5},{4,2},{5,3},{6,0},{7,1},{8,14},{9,15},{10,... | collective-permute-start | bytes 786440 | tf_op jit(solution)/shard_map/ppermute | solution.py:236
  806.0 29.7 %collective-permute-start.94 = (bf16[64,2048]{1,0:T(8,128)(2,1)S(1)}, bf16[64,2048]{1,0:T(8,128)(2,1)S(1)}, u32[]{:S(2)}, u32[]{:S(2)}) collective-permute-start(bf16[64,2048]{1,0:T(8,128)(2,1)S(1)} %get-tuple-element.174), channel_id=1, source_target_pairs={{0,4},{1,5},{2,6},{3,7},{4,0},{5,1},{6,2},{7,3},{8,12},{9,13},{10,... | collective-permute-start | bytes 786440 | tf_op jit(solution)/shard_map/ppermute | solution.py:236
  847.7 118.6 %all-to-all-start.4 = ((bf16[8,256,576]{1,2,0:T(8,128)(2,1)}), bf16[8,256,576]{1,2,0:T(8,128)(2,1)}, u32[]{:S(2)}, u32[]{:S(2)}) async-start(bf16[8,256,576]{1,2,0:T(8,128)(2,1)} %bitcast.246), calls=%async_computation.8 | async-start | bytes 4718592 | tf_op jit(solution)/shard_map/all_to_all | solution.py:264
  852.5 148.7 %reduce-scatter.9.cloned.1.call-start = ((), (), s32[]{:S(2)}) async-start(), calls=%async_computation.16 | async-start | bytes 1310720 | tf_op jit(solution)/shard_map/reduce_scatter | solution.py:312
  854.2 57.5 %collective-permute-start.101 = (bf16[32,2048]{1,0:T(8,128)(2,1)S(1)}, bf16[32,2048]{1,0:T(8,128)(2,1)S(1)}, u32[]{:S(2)}, u32[]{:S(2)}) collective-permute-start(bf16[32,2048]{1,0:T(8,128)(2,1)S(1)} %get-tuple-element.148.refs_0_), channel_id=1, source_target_pairs={{0,16},{1,17},{2,18},{3,19},{4,20},{5,21},{6,22},{7,23},{8,24},{9,... | collective-permute-start | bytes 393224 | tf_op jit(solution)/shard_map/ppermute | solution.py:236
  938.0 78.0 %reduce-scatter.5.cloned.1.call-start = ((), (), s32[]{:S(2)}) async-start(), calls=%async_computation.14 | async-start | bytes 2621440 | tf_op jit(solution)/shard_map/reduce_scatter | solution.py:312
  (219 other events, 2642.8 us)
Sparse Core Ops, SparseCore 0:
  43.3 45.2 all-gather.4
  90.7 27.0 all-gather.6
  273.7 65.4 all-gather.8
  360.8 42.3 all-gather.10
  734.0 31.5 reduce-scatter.10
  767.7 80.1 reduce-scatter.6
  938.1 30.3 reduce-scatter.8
  970.7 45.2 reduce-scatter.4
where the time goes:
time: 1050 us; the launch traced here: 1040 us
  waiting for transfers between devices  644 us (61%)
  starting transfers between devices  175 us (17%)
  local copies, waits for them, and re-layouts  71 us (7%)
  matrix products  69.8 us (7%)
  other arithmetic  52.5 us (5%)
  between operations  17.4 us (2%)
  Pallas kernels  12.5 us (1%)
    ppermute x114, waiting for transfers between devices, swap(): return lax.ppermute(value, AXES, [(i, i ^ mask) for i in range(self.count)])  587 us
    ppermute x114, starting transfers between devices, swap(): return lax.ppermute(value, AXES, [(i, i ^ mask) for i in range(self.count)])  142 us
    all_gather x4, waiting for transfers between devices, body(): lax.all_gather(columns, AXES, axis=1, tiled=True, axis_index_groups=links...  35.2 us
    unnamed x288, local copies, waits for them, and re-layouts  27.6 us
    all_to_all x5, starting transfers between devices, exchange_context(): return lax.all_to_all(chunks, 'context', 0, 0)  26.7 us
    dot_general x12, matrix products, mm_tn(): lax.dot_general(a, b, (((0,), (0,)), ((), ())), preferred_element_type=F32)  25.4 us
    dot_general x12, matrix products, mm(): return jnp.dot(a, b, preferred_element_type=F32)  24.9 us
  transfers between devices with their start and end apart: 128, of which 86 were waited for; matrix products, arithmetic and copies ran while one was open for 15% of the time, Pallas kernels for 1%

commit v1 on v0

--- a/solution.py
+++ b/solution.py
@@ -9,7 +9,7 @@
 
 EPSILON = 1e-06
 THETA = 1000000.0
-AXES = ("context", "tensor")
+CONTEXT, TENSOR = AXES = ("context", "tensor")
 BF = jnp.bfloat16
 F32 = jnp.float32
 
@@ -70,6 +70,45 @@
 def join(pieces):
     rows, width = pieces[0].shape
     return rows_call(join_kernel, [((len(pieces) * rows, width), pieces[0].dtype)], *pieces)[0]
+
+
+def index_call(kernel, out_shapes, index, *operands):
+    vmem = pl.BlockSpec(memory_space=pltpu.VMEM)
+    return pl.pallas_call(
+        kernel,
+        in_specs=[pl.BlockSpec(memory_space=pltpu.SMEM)] + [vmem] * len(operands),
+        out_specs=[vmem] * len(out_shapes),
+        out_shape=[jax.ShapeDtypeStruct(shape, kind) for shape, kind in out_shapes],
+        compiler_params=pltpu.CompilerParams(vmem_limit_bytes=48 * 1024 * 1024),
+    )(index.reshape(1), *operands)
+
+
+def join_at_kernel(index_ref, *refs):
+    *pieces, out_ref = refs
+    count = pieces[0].shape[1]
+    for slot, piece in enumerate(pieces):
+        first = pl.multiple_of((index_ref[0] ^ slot) * count, count)
+        out_ref[:, pl.ds(first, count), :] = piece[...]
+
+
+def join_at(pieces, index):
+    parts, rows, width = pieces[0].shape
+    shape = (parts, len(pieces) * rows, width)
+    return index_call(join_at_kernel, [(shape, pieces[0].dtype)], index, *pieces)[0]
+
+
+def split_at_kernel(index_ref, x_ref, *outs):
+    count = outs[0].shape[1]
+    for slot, out in enumerate(outs):
+        first = pl.multiple_of((index_ref[0] ^ slot) * count, count)
+        out[...] = x_ref[:, pl.ds(first, count), :].astype(out.dtype)
+
+
+def split_at(x, places, index, own=F32):
+    parts, rows, width = x.shape
+    shape = (parts, rows // places, width)
+    shapes = [(shape, BF if slot else own) for slot in range(places)]
+    return index_call(split_at_kernel, shapes, index, x)
 
 
 def prep_kernel(heads, x_ref, gain_ref, cos_ref, sin_ref, out_ref):
@@ -220,8 +259,6 @@
     def __init__(self, contexts, tensors):
         self.contexts, self.tensors = contexts, tensors
         self.count = contexts * tensors
-        self.near = 4
-        self.rows = tensors // 2
         self.half = contexts // 2
         self.far_half = self.half * tensors
         self.half_groups = [
@@ -229,14 +266,20 @@
             for part in range(2)
             for tensor in range(tensors)
         ]
-        self.context = lax.axis_index("context")
+        self.context = lax.axis_index(CONTEXT)
         self.upper = self.context >= self.half
+        self.place = self.context % self.half
 
     def swap(self, value, mask):
         return lax.ppermute(value, AXES, [(i, i ^ mask) for i in range(self.count)])
 
-    def far_masks(self):
-        return [far * self.near * self.tensors for far in range(self.contexts // self.near)]
+    def line_masks(self):
+        return [2 * place * self.tensors for place in range(self.half)]
+
+    def square_masks(self):
+        return [
+            side * self.tensors + row * 2 for side in range(2) for row in range(self.tensors // 2)
+        ]
 
     def half_masks(self):
         return [member * self.tensors for member in range(self.half)]
@@ -247,21 +290,22 @@
     def spread(self, value, masks):
         return [value] + [self.swap(value, mask) for mask in masks[1:]]
 
-    def cube_masks(self):
-        return [
-            near * self.tensors + row * 2
-            for near in range(self.near)
-            for row in range(self.rows)
+    def collect(self, chunks, masks):
+        return self.total(self.fetch(chunks, masks))
+
+    def fetch(self, chunks, masks):
+        return [chunks[0]] + [
+            self.swap(chunk.astype(BF), mask) for chunk, mask in zip(chunks[1:], masks[1:])
         ]
 
-    def collect(self, chunks, masks):
-        total = chunks[0].astype(F32)
-        for chunk, mask in zip(chunks[1:], masks[1:]):
-            total = total + self.swap(chunk.astype(BF), mask).astype(F32)
+    def total(self, pieces):
+        total = pieces[0].astype(F32)
+        for piece in pieces[1:]:
+            total = total + piece.astype(F32)
         return total
 
     def exchange_context(self, chunks):
-        return lax.all_to_all(chunks, "context", 0, 0)
+        return lax.all_to_all(chunks, CONTEXT, 0, 0)
 
     def spread_context(self, value):
         return self.exchange_context(
@@ -280,21 +324,37 @@
         return slots
 
     def gather_rows(self, rows):
-        line = join(self.spread(rows, self.far_masks()))
-        own = join(self.spread(line, self.cube_masks()))
+        return self.gather_square(self.gather_line(rows))
+
+    def gather_line(self, rows):
+        return join(self.spread(rows, self.line_masks()))
+
+    def gather_square(self, line):
+        own = join(self.spread(line, self.square_masks()))
         return own, self.swap(own, 1)
 
+    def move_start(self, chunks):
+        return self.exchange_context(chunks)
+
+    def reduce_start(self, own, other):
+        half = own + self.swap(other.astype(BF), 1).astype(F32)
+        masks = self.square_masks()
+        return self.fetch(jnp.split(half, len(masks), axis=0), masks)
+
+    def reduce_end(self, pieces):
+        line = self.total(pieces)
+        masks = self.line_masks()
+        return self.collect(jnp.split(line, len(masks), axis=0), masks)
+
     def reduce_rows(self, own, other):
-        half = own + self.swap(other.astype(BF), 1).astype(F32)
-        masks = self.cube_masks()
-        line = self.collect(jnp.split(half, len(masks), axis=0), masks)
-        masks = self.far_masks()
-        return self.collect(jnp.split(line, len(masks), axis=0), masks)
+        return self.reduce_end(self.reduce_start(own, other))
 
     def spread_rows(self, rows):
+        stages = []
         for mask in (self.far_half, 2, 1):
             rows = join([rows, self.swap(rows, mask)])
-        return rows
+            stages.append(rows)
+        return rows, stages[0]
 
     def return_rows(self, partial):
         for mask in (1, 2, self.far_half):
@@ -302,20 +362,35 @@
             partial = own + self.swap(other.astype(BF), mask).astype(F32)
         return partial
 
-    def gather_half(self, mine, theirs):
+    def both_parts(self, mine, theirs):
         got = self.swap(theirs, self.far_half)
-        low, high = self.by_part(mine, got)
-        return jnp.stack([low, high])
-
-    def scatter_half(self, partial):
+        joined = join_at([mine[None], got[None]], self.upper.astype(jnp.int32))
+        return joined.reshape(2, *mine.shape)
+
+    def gather_half(self, shard, behind):
+        if not behind and self.half <= 4:
+            return join_at(self.spread(shard, self.half_masks()), self.place)
+        return lax.all_gather(
+            shard, AXES, axis=1, tiled=True, axis_index_groups=self.half_groups
+        )
+
+    def scatter_start(self, partial):
         rows, columns = partial.shape
-        shard = lax.psum_scatter(
-            partial.astype(BF).reshape(2, rows // 2, columns),
-            AXES,
-            scatter_dimension=1,
-            axis_index_groups=self.half_groups,
-            tiled=True,
-        )
+        partial = partial.reshape(2, rows // 2, columns)
+        if self.half > 4:
+            return [
+                lax.psum_scatter(
+                    partial.astype(BF),
+                    AXES,
+                    scatter_dimension=1,
+                    axis_index_groups=self.half_groups,
+                    tiled=True,
+                )
+            ]
+        return self.fetch(split_at(partial, self.half, self.place), self.half_masks())
+
+    def scatter_end(self, pieces):
+        shard = self.total(pieces).astype(BF)
         mine = jnp.where(self.upper, shard[1], shard[0])
         theirs = jnp.where(self.upper, shard[0], shard[1])
         got = self.swap(theirs, self.far_half)
@@ -338,7 +413,7 @@
     query_gain,
     key_gain,
 ):
-    contexts, tensors = lax.axis_size("context"), lax.axis_size("tensor")
+    contexts, tensors = lax.axis_size(CONTEXT), lax.axis_size(TENSOR)
     links = Links(contexts, tensors)
     masks = links.half_masks()
     layers = w_query.shape[0]
@@ -350,7 +425,7 @@
     key_pos = row_positions(block_order, jnp.int32(0), all_rows, rows_per_block)
     key_pos = links.relative(key_pos.reshape(contexts, context_rows), links.context)
     key_pos = key_pos.reshape(contexts, tensors, local_rows)
-    tensor = lax.axis_index("tensor")
+    tensor = lax.axis_index(TENSOR)
     key_pos = links.relative(key_pos.transpose(1, 0, 2), tensor)
     key_pos = key_pos.reshape(2, 2, 2, links.half, local_rows).transpose(3, 1, 0, 2, 4)
     key_pos = key_pos.reshape(links.half, 2 * context_rows)
@@ -376,9 +451,26 @@
     def ffn_parts(layer):
         parts = [w_gate[layer], w_up[layer], w_down[layer].T]
         parts = [part.reshape(shard, contexts, units) for part in parts]
-        return jnp.concatenate(parts, axis=2).transpose(1, 0, 2)
-
-    attn_weights, out_weights, ffn_weights = [], [], []
+        parts = [jnp.concatenate(parts[:2], axis=2), parts[2]]
+        return [part.transpose(1, 0, 2) for part in parts]
+
+    def move(piece, *others):
+        if moves:
+            others = (*others, moves[-1])
+        piece = after(piece, *others) if others else piece
+        moves.append(links.move_start(piece))
+        return moves[-1]
+
+    moves = []
+    packed = []
+    for layer in range(layers):
+        packed.append(ffn_parts(layer))
+    attn_weights, out_weights = [], []
+    ffn_weights = [[None] * 2 for _ in range(layers)]
+
+    def fetch(layer, at, *others):
+        ffn_weights[layer][at] = move(packed[layer][at], *others).reshape(width, -1)
+
     for layer in range(layers):
         parts = []
         for part in range(2):
@@ -392,55 +484,55 @@
             ]
             parts.append(jnp.concatenate(columns, axis=1))
         mine, theirs = links.by_part(*parts)
-        shards = links.gather_half(mine, theirs)
-        gathered = []
-        for columns in (
-            shards[:, :, : query_width + 2 * kv_width], shards[:, :, query_width + 2 * kv_width :]
-        ):
-            gathered.append(
-                lax.all_gather(
-                    columns,
-                    AXES,
-                    axis=1,
-                    tiled=True,
-                    axis_index_groups=links.half_groups,
-                )
-            )
-        if layer == 0:
-            gathered_0 = gathered[0]
-        attn_weights.append(gathered[0].reshape(width, -1))
-        out_weights.append(gathered[1].reshape(width, -1))
+        cuts = [query_width + 2 * kv_width]
+        mine, theirs = jnp.split(mine, cuts, axis=1), jnp.split(theirs, cuts, axis=1)
+        if layer:
+            held = [links.both_parts(a, b) for a, b in zip(mine, theirs)]
+        else:
+            taken = links.both_parts(mine[0], theirs[0])
+            taken = links.gather_half(taken, False)
+            attn_weights.append(taken.reshape(width, -1))
+        if not layer:
+            taken = links.both_parts(mine[1], theirs[1])
+            out_weights.append(links.gather_half(taken, False).reshape(width, -1))
 
     current = residual_in
     stored = []
     for layer in range(layers):
         gain_attn, gain_mlp = gains[layer], gains[layers + layer]
-        normed_in = links.spread_rows(rms_scale(current, gain_attn).astype(BF))
-        parts = ffn_parts(layer)
-        parts = after(parts, gathered_0 if layer == 0 else stored[0][9][0])
-        ffn_weights.append(links.exchange_context(parts).reshape(width, 3 * units))
+        normed_in = links.spread_rows(rms_scale(current, gain_attn).astype(BF))[0]
         projected = mm(normed_in, attn_weights[layer])
         pair_proj, query_proj = projected[:, query_width:], projected[:, :query_width]
         pairs = prep_heads(pair_proj, kv_heads, key_gains[layer], tables)
         pairs = links.spread(pairs, masks)
         queries = prep_heads(query_proj, query_heads, query_gains[layer], tables)
-        if layer + 1 == layers:
-            top_gradient = links.gather_rows(after(grad_output, query_proj).astype(BF))
-            queries = after(queries, top_gradient[0])
+        if layer == 0:
+            top_gradient = links.gather_rows(after(grad_output, *pairs).astype(BF))
+        if layer == 0:
+            shards = after(held, *pairs)
+            attn_weights.append(links.gather_half(shards[0], True).reshape(width, -1))
+        fetch(layer, layer, *pairs)
         output_rows, log_totals = attend(queries, pairs, query_pos, key_pos, head_dim)
         partial = mm_nt(output_rows, out_weights[layer])
         middle = current + links.return_rows(partial)
-        normed_mid = links.gather_rows(rms_scale(middle, gain_mlp).astype(BF))
+        line = links.gather_line(rms_scale(middle, gain_mlp).astype(BF))
+        if layer == 0:
+            fetch(layer, 1, line)
+        normed_mid = links.gather_square(line)
+        if layer + 1 < layers:
+            fetch(layer + 1, 0, normed_mid[0])
         inner, partial = [], []
         weights = ffn_weights[layer]
         for rows in normed_mid:
-            both = mm(rows, weights[:, : 2 * units])
+            both = mm(rows, weights[0])
             gate, up = both[:, :units], both[:, units:]
             hidden = (jax.nn.silu(gate) * up).astype(BF)
             inner.append((gate, up, hidden))
-            partial.append(mm_nt(hidden, weights[:, 2 * units :]))
+            partial.append(mm_nt(hidden, weights[1]))
         if layer + 1 < layers:
             block_out = middle + links.reduce_rows(*partial)
+            taken = links.gather_half(after(shards[1], block_out), True)
+            out_weights.append(taken.reshape(width, -1))
         else:
             last = (middle, partial)
         stored.append(
@@ -461,7 +553,23 @@
         if layer + 1 < layers:
             current = block_out
 
-    grad_res = grad_output
+    def finish_ffn(pieces, late):
+        parts = [
+            piece.transpose(1, 0, 2).reshape(shard, -1).astype(F32)
+            for piece in after(pieces, late)
+        ]
+        return parts[0], parts[1], parts[2].T
+
+    def finish_attn(left, lates):
+        out_pieces, query_pieces, pair_pieces = [after(a, b) for a, b in zip(left, lates)]
+        d_out = jnp.concatenate(links.scatter_end(out_pieces), axis=1).T
+        d_query = jnp.concatenate(links.scatter_end(query_pieces), axis=1)
+        halves = links.scatter_end(pair_pieces)
+        d_key = jnp.concatenate([half[:, :kv_width] for half in halves], axis=1)
+        d_value = jnp.concatenate([half[:, kv_width:] for half in halves], axis=1)
+        return d_query, d_key, d_value, d_out
+
+    grad_res, moved = grad_output, None
     weight_grads, gain_grads = [None] * layers, [None] * layers
     for layer in reversed(range(layers)):
         (
@@ -481,41 +589,45 @@
         if layer + 1 == layers:
             grad_all = top_gradient
         else:
-            grad_all = links.gather_rows(grad_res.astype(BF))
+            line = links.gather_line(grad_res.astype(BF))
+            moved[1] = move(held_grads[1], line)
+            grad_all = links.gather_square(line)
+            final_pieces = after(final_pieces, grad_all[0])
+            final_out = middle_last + links.reduce_end(final_pieces)
+            weight_grads[layer + 1] = finish_attn(left, [grad_all[0]] * 3)
         partial, d_in, d_down = [], 0.0, 0.0
         weights = ffn_weights[layer]
         for rows, grad_rows, (gate, up, hidden) in zip(normed_mid, grad_all, inner):
-            grad_hidden = mm(grad_rows, weights[:, 2 * units :])
+            grad_hidden = mm(grad_rows, weights[1])
             sigmoid = jax.nn.sigmoid(gate)
             grad_up = (grad_hidden * gate * sigmoid).astype(BF)
             grad_gate = (
                 grad_hidden * up * sigmoid * (1.0 + gate * (1.0 - sigmoid))
             ).astype(BF)
             both = jnp.concatenate([grad_gate, grad_up], axis=1)
-            partial.append(mm_nt(both, weights[:, : 2 * units]))
+            partial.append(mm_nt(both, weights[0]))
             d_in = d_in + mm_tn(rows, both)
             d_down = d_down + mm_tn(grad_rows, hidden)
-        grad_normed_mid = links.reduce_rows(*partial)
+        held_grads = [
+            grads.astype(BF).reshape(contexts, shard, units)
+            for grads in (d_in[:, :units], d_in[:, units:], d_down)
+        ]
+        last_moved, moved = moved, [None] * 3
+        pieces = links.reduce_start(*partial)
+        if layer == 0:
+            moved[2] = move(held_grads[2], partial[1])
+        grad_normed_mid = links.reduce_end(pieces)
         unused, norm_back = jax.vjp(rms_scale, middle, gain_mlp)
         grad_mid_part, d_mlp_gain = norm_back(grad_normed_mid)
         grad_mid = grad_res + grad_mid_part
-        pieces = jnp.concatenate([d_in, d_down], axis=1).astype(BF)
-        if layer + 1 < layers:
-            pieces = after(pieces, moved)
-        pieces = links.exchange_context(pieces.reshape(contexts, shard, 3 * units))
-        moved = pieces
-        pieces = pieces.transpose(1, 0, 2)
-        d_gate = pieces[:, :, :units].reshape(shard, contexts * units).astype(F32)
-        d_up = pieces[:, :, units : 2 * units].reshape(shard, contexts * units).astype(F32)
-        d_down = pieces[:, :, 2 * units :].reshape(shard, contexts * units).T.astype(F32)
+        grad_mid_all, far_rows = links.spread_rows(grad_mid.astype(BF))
+        at = 0 if layer == 0 else 2
+        moved[at] = move(held_grads[at], far_rows)
+        out_pieces = links.scatter_start(mm_tn(grad_mid_all, output_rows))
+        attention_gradient = mm(grad_mid_all, out_weights[layer]).astype(BF)
         if layer + 1 == layers:
             middle_last, partial_last = last
-            partial_last = after(partial_last, grad_mid)
-            final_out = middle_last + links.reduce_rows(*partial_last)
-        grad_mid_all = links.spread_rows(grad_mid.astype(BF))
-        d_out = links.scatter_half(mm_tn(grad_mid_all, output_rows))
-        d_out = jnp.concatenate(d_out, axis=1).T
-        attention_gradient = mm(grad_mid_all, out_weights[layer]).astype(BF)
+            final_pieces = links.reduce_start(*after(partial_last, grad_mid_all))
         query_grad, pair_grads = attend_back(
             queries,
             pairs,
@@ -529,6 +641,10 @@
         pair_grads = [pair_grads[0]] + [
             links.swap(grad, mask) for grad, mask in zip(pair_grads[1:], masks[1:])
         ]
+        at = 1 if layer == 0 else 0
+        moved[at] = move(held_grads[at], *pair_grads)
+        if layer == 0:
+            weight_grads[1] = (*weight_grads[1], *finish_ffn(last_moved, query_grad))
         grad_queries, d_query_gain = prep_heads_back(
             query_proj, query_heads, query_gains[layer], tables, [query_grad]
         )
@@ -537,27 +653,15 @@
         )
         grad_projected = jnp.concatenate([grad_queries, grad_pairs], axis=1)
         partial = mm_nt(grad_projected, attn_weights[layer])
-        if layer + 1 == layers:
-            partial = after(partial, final_out)
         grad_normed_in = links.return_rows(partial)
         unused, input_back = jax.vjp(rms_scale, layer_in, gain_attn)
         grad_in_part, d_attn_gain = input_back(grad_normed_in)
         grad_res = grad_mid + grad_in_part
-        halves = links.scatter_half(mm_tn(normed_in, grad_projected))
-        cuts = [query_width, query_width + kv_width]
-        d_query, d_key, d_value = [
-            jnp.concatenate(pair, axis=1)
-            for pair in zip(*[jnp.split(half, cuts, axis=1) for half in halves])
-        ]
-        weight_grads[layer] = (
-            d_query,
-            d_key,
-            d_value,
-            d_out,
-            d_gate,
-            d_up,
-            d_down,
-        )
+        query_pieces = links.scatter_start(mm_tn(normed_in, grad_queries))
+        pair_pieces = links.scatter_start(mm_tn(normed_in, grad_pairs))
+        left = (out_pieces, query_pieces, pair_pieces)
+        if layer == 0:
+            weight_grads[0] = (*finish_attn(left, [grad_res] * 3), *finish_ffn(moved, partial))
         gain_grads[layer] = (d_attn_gain, d_mlp_gain, d_query_gain[0], d_key_gain[0])
 
     wide = jnp.stack([g[0] for g in gain_grads] + [g[1] for g in gain_grads])
@@ -569,7 +673,7 @@
     )
     pieces = jnp.concatenate([wide, narrow], axis=2)
     pieces = jnp.broadcast_to(pieces, (contexts, tensors, pieces.shape[2]))
-    pieces = after(pieces.reshape(contexts * tensors, -1), moved)
+    pieces = after(pieces.reshape(contexts * tensors, -1), moves[-1])
     sums = jnp.sum(lax.all_to_all(pieces, AXES, 0, 0, tiled=True), axis=0)
     wide = sums[: 2 * layers * shard].reshape(2, layers, shard)
     narrow = sums[2 * layers * shard :].reshape(2, layers, head_dim)
@@ -578,10 +682,10 @@
 
 
 def solution(mesh):
-    rows = P(("context", "tensor"), None)
-    in_split = P(None, "context", "tensor")
-    out_split = P(None, "tensor", "context")
-    gain = P(None, "context")
+    rows = P(AXES, None)
+    in_split = P(None, CONTEXT, TENSOR)
+    out_split = P(None, TENSOR, CONTEXT)
+    gain = P(None, CONTEXT)
     weights = (in_split, in_split, in_split, out_split, in_split, in_split, out_split)
     return jax.shard_map(
         body,

time: 1050 us -> 1020 us (0.971)
  waiting for transfers between devices: 644 us -> 553 us
  local copies, waits for them, and re-layouts: 71 us -> 96 us
  starting transfers between devices: 175 us -> 200 us
    ppermute x114 -> x126, waiting for transfers between devices: 587 us -> 517 us  [swap(): return lax.ppermute(value, AXES, [(i, i ^ mask) for i in range(self.count)])]
    all_to_all x5 -> x11, waiting for transfers between devices: 0.01 us -> 35.4 us  [exchange_context(): return lax.all_to_all(chunks, CONTEXT, 0, 0)]
    all_gather x4 -> x2, waiting for transfers between devices: 35.2 us -> 0.02 us  [gather_half(): lax.all_gather(shard, AXES, axis=1, tiled=True, axis_index_groups=self.ha...]
    all_to_all x5 -> x11, starting transfers between devices: 26.7 us -> 52.6 us  [exchange_context(): return lax.all_to_all(chunks, CONTEXT, 0, 0)]
    unnamed x288 -> x371, local copies, waits for them, and re-layouts: 27.6 us -> 50.4 us
    reduce_scatter x4 -> x0, waiting for transfers between devices: 12.3 us -> none  [scatter_half(): lax.psum_scatter(partial.astype(BF).reshape(2, rows // 2, columns), AXES,...]
    dot_general x12 -> x14, matrix products: 25.4 us -> 19.5 us  [mm_tn(): lax.dot_general(a, b, (((0,), (0,)), ((), ())), preferred_element_type=F32)]
    ppermute x114 -> x126, starting transfers between devices: 142 us -> 144 us  [swap(): return lax.ppermute(value, AXES, [(i, i ^ mask) for i in range(self.count)])]
  transfers between devices with their start and end apart: 128 -> 140, of which waited for: 86 -> 78; matrix products, arithmetic and copies ran while one was open for 15% -> 17% of each run, Pallas kernels for 1% -> 2%
where the time goes in v1:
time: 1020 us; the launch traced here: 1010 us
  waiting for transfers between devices  553 us (54%)
  starting transfers between devices  200 us (20%)
  local copies, waits for them, and re-layouts  96 us (9%)
  matrix products  66.4 us (7%)
  other arithmetic  56.5 us (6%)
  Pallas kernels  21.4 us (2%)
  between operations  17.7 us (2%)
    ppermute x126, waiting for transfers between devices, swap(): return lax.ppermute(value, AXES, [(i, i ^ mask) for i in range(self.count)])  517 us
    ppermute x126, starting transfers between devices, swap(): return lax.ppermute(value, AXES, [(i, i ^ mask) for i in range(self.count)])  144 us
    all_to_all x11, starting transfers between devices, exchange_context(): return lax.all_to_all(chunks, CONTEXT, 0, 0)  52.6 us
    unnamed x371, local copies, waits for them, and re-layouts  50.4 us
    all_to_all x11, waiting for transfers between devices, exchange_context(): return lax.all_to_all(chunks, CONTEXT, 0, 0)  35.4 us
    dot_general x12, matrix products, mm(): return jnp.dot(a, b, preferred_element_type=F32)  24.5 us
    dot_general x12, matrix products, mm_nt(): lax.dot_general(a, b, (((1,), (1,)), ((), ())), preferred_element_type=F32)  22.5 us
  transfers between devices with their start and end apart: 140, of which 78 were waited for; matrix products, arithmetic and copies ran while one was open for 17% of the time, Pallas kernels for 2%

profile of v1, /device:TPU:0, one launch (start us, length us, event | category | flops | bytes accessed | tf_op | source)
XLA Modules:
  0.0 1011.0 jit_solution(7676230639254653717)
XLA Ops:
  8.6 7.3 all-to-all-start
  31.2 17.4 %collective-permute-done.refs_1_ = bf16[32,2048]{1,0:T(8,128)(2,1)S(1)} collective-permute-done((bf16[32,2048]{1,0:T(8,128)(2,1)S(1)}, bf16[32,2048]{1,0:T(8,128)(2,1)S(1)}, u32[]{:S(2)}, u32[]{:S(2)}) %collective-permute-start) | collective-permute-done | bytes 131104 | tf_op jit(solution)/shard_map/ppermute | solution.py:274
  62.5 4.8 collective-permute-done.6.refs_3_
  68.0 10.8 %collective-permute-done.5.refs_2_ = bf16[2,256,512]{2,1,0:T(8,128)(2,1)S(1)} collective-permute-done((bf16[2,256,512]{2,1,0:T(8,128)(2,1)S(1)}, bf16[2,256,512]{2,1,0:T(8,128)(2,1)S(1)}, u32[]{:S(2)}, u32[]{:S(2)}) %collective-permute-start.5) | collective-permute-done | bytes 524320 | tf_op jit(solution)/shard_map/ppermute | solution.py:274
  123.0 27.0 %collective-permute-done.19.refs_3_ = bf16[32,2048]{1,0:T(8,128)(2,1)S(1)} collective-permute-done((bf16[32,2048]{1,0:T(8,128)(2,1)S(1)}, bf16[32,2048]{1,0:T(8,128)(2,1)S(1)}, u32[]{:S(2)}, u32[]{:S(2)}) %collective-permute-start.19) | collective-permute-done | bytes 131104 | tf_op jit(solution)/shard_map/ppermute | solution.py:274
  150.0 13.9 %collective-permute-done.18.refs_2_ = bf16[32,2048]{1,0:T(8,128)(2,1)S(1)} collective-permute-done((bf16[32,2048]{1,0:T(8,128)(2,1)S(1)}, bf16[32,2048]{1,0:T(8,128)(2,1)S(1)}, u32[]{:S(2)}, u32[]{:S(2)}) %collective-permute-start.18) | collective-permute-done | bytes 131104 | tf_op jit(solution)/shard_map/ppermute | solution.py:274
  167.5 12.2 %collective-permute-done.22.refs_3_ = bf16[128,2048]{1,0:T(8,128)(2,1)S(1)} collective-permute-done((bf16[128,2048]{1,0:T(8,128)(2,1)S(1)}, bf16[128,2048]{1,0:T(8,128)(2,1)S(1)}, u32[]{:S(2)}, u32[]{:S(2)}) %collective-permute-start.22) | collective-permute-done | bytes 524320 | tf_op jit(solution)/shard_map/ppermute | solution.py:274
  179.8 8.2 collective-permute-done.21.refs_2_
  190.7 5.7 all-to-all-start.2
  203.8 13.4 %all-to-all-done.2 = bf16[8,256,192]{1,2,0:T(8,128)(2,1)S(1)} async-done(((bf16[8,256,192]{1,2,0:T(8,128)(2,1)}), bf16[8,256,192]{1,2,0:T(8,128)(2,1)S(1)}, u32[]{:S(2)}, u32[]{:S(2)}) %all-to-all-start.2) | async-done | bytes 786464 | tf_op jit(solution)/shard_map/all_to_all | solution.py:308
  229.7 11.7 %collective-permute-done.35 = bf16[256,256]{1,0:T(8,128)(2,1)S(1)} collective-permute-done((bf16[256,256]{1,0:T(8,128)(2,1)S(1)}, bf16[256,256]{1,0:T(8,128)(2,1)S(1)}, u32[]{:S(2)}, u32[]{:S(2)}) %collective-permute-start.35) | collective-permute-done | bytes 131104 | tf_op jit(solution)/shard_map/ppermute | solution.py:274
  242.1 4.9 collective-permute-done.34
  258.4 13.7 %collective-permute-done.25 = bf16[128,2048]{1,0:T(8,128)(2,1)S(1)} collective-permute-done((bf16[128,2048]{1,0:T(8,128)(2,1)S(1)}, bf16[128,2048]{1,0:T(8,128)(2,1)S(1)}, u32[]{:S(2)}, u32[]{:S(2)}) %collective-permute-start.25) | collective-permute-done | bytes 524320 | tf_op jit(solution)/shard_map/ppermute | solution.py:274
  272.1 23.9 %collective-permute-done.27 = bf16[128,2048]{1,0:T(8,128)(2,1)S(1)} collective-permute-done((bf16[128,2048]{1,0:T(8,128)(2,1)S(1)}, bf16[128,2048]{1,0:T(8,128)(2,1)S(1)}, u32[]{:S(2)}, u32[]{:S(2)}) %collective-permute-start.27) | collective-permute-done | bytes 524320 | tf_op jit(solution)/shard_map/ppermute | solution.py:274
  296.0 16.7 %collective-permute-done.26 = bf16[128,2048]{1,0:T(8,128)(2,1)S(1)} collective-permute-done((bf16[128,2048]{1,0:T(8,128)(2,1)S(1)}, bf16[128,2048]{1,0:T(8,128)(2,1)S(1)}, u32[]{:S(2)}, u32[]{:S(2)}) %collective-permute-start.26) | collective-permute-done | bytes 524320 | tf_op jit(solution)/shard_map/ppermute | solution.py:274
  318.6 4.9 collective-permute-done.30
  323.5 5.1 collective-permute-done.29
  329.7 8.3 collective-permute-done.31.refs_1_
  339.6 6.7 collective-permute-done.32.refs_1_
  381.2 4.7 all-to-all-start.3
  390.1 38.4 %collective-permute-done.41 = bf16[32,2048]{1,0:T(8,128)(2,1)S(1)} collective-permute-done((bf16[32,2048]{1,0:T(8,128)(2,1)S(1)}, bf16[32,2048]{1,0:T(8,128)(2,1)S(1)}, u32[]{:S(2)}, u32[]{:S(2)}) %collective-permute-start.41) | collective-permute-done | bytes 131104 | tf_op jit(solution)/shard_map/ppermute | solution.py:274
  448.9 5.0 collective-permute-done.51.refs_3_
  453.9 4.6 collective-permute-start.49
  471.7 9.8 collective-permute-done.54.refs_3_
  481.5 8.6 collective-permute-done.53.refs_2_
  492.3 4.7 all-to-all-start.4
  500.1 17.9 %all-to-all-done.4 = bf16[8,256,192]{1,2,0:T(8,128)(2,1)} async-done(((bf16[8,256,192]{1,2,0:T(8,128)(2,1)}), bf16[8,256,192]{1,2,0:T(8,128)(2,1)}, u32[]{:S(2)}, u32[]{:S(2)}) %all-to-all-start.4) | async-done | bytes 786464 | tf_op jit(solution)/shard_map/all_to_all | solution.py:308
  537.7 22.1 %collective-permute-done.57 = bf16[128,2048]{1,0:T(8,128)(2,1)S(1)} collective-permute-done((bf16[128,2048]{1,0:T(8,128)(2,1)S(1)}, bf16[128,2048]{1,0:T(8,128)(2,1)S(1)}, u32[]{:S(2)}, u32[]{:S(2)}) %collective-permute-start.57) | collective-permute-done | bytes 524320 | tf_op jit(solution)/shard_map/ppermute | solution.py:274
  569.8 6.0 collective-permute-done.61
  577.4 6.9 collective-permute-done.63.refs_1_
  585.1 7.2 collective-permute-done.64.refs_1_
  618.0 5.7 collective-permute-done.74
  646.6 7.7 collective-permute-done.78.refs_3_
  654.3 10.1 collective-permute-done.77.refs_2_
  673.0 20.9 %collective-permute-done.106 = bf16[2,256,256]{2,1,0:T(8,128)(2,1)S(1)} collective-permute-done((bf16[2,256,256]{2,1,0:T(8,128)(2,1)S(1)}, bf16[2,256,256]{2,1,0:T(8,128)(2,1)S(1)}, u32[]{:S(2)}, u32[]{:S(2)}) %collective-permute-start.106) | collective-permute-done | bytes 262176 | tf_op jit(solution)/shard_map/ppermute | solution.py:274
  719.6 5.7 collective-permute-done.122
  729.3 9.0 collective-permute-done.123
  744.2 5.4 collective-permute-done.117
  771.8 5.1 collective-permute-done.69
  777.0 14.5 %collective-permute-done.68 = bf16[128,2048]{1,0:T(8,128)(2,1)} collective-permute-done((bf16[128,2048]{1,0:T(8,128)(2,1)}, bf16[128,2048]{1,0:T(8,128)(2,1)}, u32[]{:S(2)}, u32[]{:S(2)}) %collective-permute-start.68) | collective-permute-done | bytes 524320 | tf_op jit(solution)/shard_map/ppermute | solution.py:274
  800.2 18.9 %collective-permute-done.87 = bf16[128,2048]{1,0:T(8,128)(2,1)S(1)} collective-permute-done((bf16[128,2048]{1,0:T(8,128)(2,1)S(1)}, bf16[128,2048]{1,0:T(8,128)(2,1)S(1)}, u32[]{:S(2)}, u32[]{:S(2)}) %collective-permute-start.87) | collective-permute-done | bytes 524320 | tf_op jit(solution)/shard_map/ppermute | solution.py:274
  830.3 12.7 %collective-permute-done.91 = bf16[32,2048]{1,0:T(8,128)(2,1)S(1)} collective-permute-done((bf16[32,2048]{1,0:T(8,128)(2,1)S(1)}, bf16[32,2048]{1,0:T(8,128)(2,1)S(1)}, u32[]{:S(2)}, u32[]{:S(2)}) %collective-permute-start.91) | collective-permute-done | bytes 131104 | tf_op jit(solution)/shard_map/ppermute | solution.py:274
  844.7 5.0 collective-permute-done.83
  883.9 5.6 collective-permute-done.98.refs_3_
  941.1 9.0 collective-permute-done.103
  951.2 8.1 collective-permute-done.104
  964.1 5.7 collective-permute-done.112
  972.7 5.6 collective-permute-done.113
  (875 shorter events, 486.4 us)
Async XLA Ops:
  22.9 36.7 %collective-permute-start.10 = (bf16[256,256]{1,0:T(8,128)(2,1)}, bf16[256,256]{1,0:T(8,128)(2,1)S(1)}, u32[]{:S(2)}, u32[]{:S(2)}) collective-permute-start(bf16[256,256]{1,0:T(8,128)(2,1)} %split.295), channel_id=1, source_target_pairs={{0,16},{1,17},{2,18},{3,19},{4,20},{5,21},{6,22},{7,23},{8,24},{9,... | collective-permute-start | bytes 393224 | tf_op jit(solution)/shard_map/ppermute | solution.py:274
  25.8 25.6 %collective-permute-start.3 = (bf16[256,512]{1,0:T(8,128)(2,1)S(1)}, bf16[256,512]{1,0:T(8,128)(2,1)S(1)}, u32[]{:S(2)}, u32[]{:S(2)}) collective-permute-start(bf16[256,512]{1,0:T(8,128)(2,1)S(1)} %split.293), channel_id=1, source_target_pairs={{0,16},{1,17},{2,18},{3,19},{4,20},{5,21},{6,22},{7,23},{8,24},{9,... | collective-permute-start | bytes 786440 | tf_op jit(solution)/shard_map/ppermute | solution.py:274
  53.2 25.6 %collective-permute-start.5 = (bf16[2,256,512]{2,1,0:T(8,128)(2,1)S(1)}, bf16[2,256,512]{2,1,0:T(8,128)(2,1)S(1)}, u32[]{:S(2)}, u32[]{:S(2)}) collective-permute-start(bf16[2,256,512]{2,1,0:T(8,128)(2,1)S(1)} %bitcast.309), channel_id=1, source_target_pairs={{0,8},{1,9},{2,10},{3,11},{4,12},{5,13},{6,14},{7,15},{8,0},{9,1},... | collective-permute-start | bytes 1572872 | tf_op jit(solution)/shard_map/ppermute | solution.py:274
  59.7 26.4 %collective-permute-start.13 = (bf16[2,256,256]{2,1,0:T(8,128)(2,1)S(1)}, bf16[2,256,256]{2,1,0:T(8,128)(2,1)S(1)}, u32[]{:S(2)}, u32[]{:S(2)}) collective-permute-start(bf16[2,256,256]{2,1,0:T(8,128)(2,1)S(1)} %bitcast.312), channel_id=1, source_target_pairs={{0,12},{1,13},{2,14},{3,15},{4,8},{5,9},{6,10},{7,11},{8,4},{9,5},... | collective-permute-start | bytes 786440 | tf_op jit(solution)/shard_map/ppermute | solution.py:274
  112.2 78.5 %all-to-all-start.1 = ((bf16[8,256,384]{1,2,0:T(8,128)(2,1)}), bf16[8,256,384]{1,2,0:T(8,128)(2,1)}, u32[]{:S(2)}, u32[]{:S(2)}) async-start(bf16[8,256,384]{1,2,0:T(8,128)(2,1)} %maximum_bitcast_fusion), calls=%async_computation.1 | async-start | bytes 3145728 | tf_op jit(solution)/shard_map/all_to_all | solution.py:308
  118.6 31.4 %collective-permute-start.19 = (bf16[32,2048]{1,0:T(8,128)(2,1)S(1)}, bf16[32,2048]{1,0:T(8,128)(2,1)S(1)}, u32[]{:S(2)}, u32[]{:S(2)}) collective-permute-start(bf16[32,2048]{1,0:T(8,128)(2,1)S(1)} %multiply_convert_fusion.14.refs_0_), channel_id=1, source_target_pairs={{0,24},{1,25},{2,26},{3,27},{4,28},{5,29},{6,30},{7,31},{8,16},{9,... | collective-permute-start | bytes 393224 | tf_op jit(solution)/shard_map/ppermute | solution.py:274
  122.2 41.7 %collective-permute-start.18 = (bf16[32,2048]{1,0:T(8,128)(2,1)S(1)}, bf16[32,2048]{1,0:T(8,128)(2,1)S(1)}, u32[]{:S(2)}, u32[]{:S(2)}) collective-permute-start(bf16[32,2048]{1,0:T(8,128)(2,1)S(1)} %multiply_convert_fusion.14.refs_0_), channel_id=1, source_target_pairs={{0,16},{1,17},{2,18},{3,19},{4,20},{5,21},{6,22},{7,23},{8,24},{9,... | collective-permute-start | bytes 393224 | tf_op jit(solution)/shard_map/ppermute | solution.py:274
  122.2 41.7 %collective-permute-start.17 = (bf16[32,2048]{1,0:T(8,128)(2,1)S(1)}, bf16[32,2048]{1,0:T(8,128)(2,1)S(1)}, u32[]{:S(2)}, u32[]{:S(2)}) collective-permute-start(bf16[32,2048]{1,0:T(8,128)(2,1)S(1)} %multiply_convert_fusion.14.refs_0_), channel_id=1, source_target_pairs={{0,8},{1,9},{2,10},{3,11},{4,12},{5,13},{6,14},{7,15},{8,0},{9,1},... | collective-permute-start | bytes 393224 | tf_op jit(solution)/shard_map/ppermute | solution.py:274
  190.7 26.5 %all-to-all-start.2 = ((bf16[8,256,192]{1,2,0:T(8,128)(2,1)}), bf16[8,256,192]{1,2,0:T(8,128)(2,1)S(1)}, u32[]{:S(2)}, u32[]{:S(2)}) async-start(bf16[8,256,192]{1,2,0:T(8,128)(2,1)} %bitcast.350), calls=%async_computation.2 | async-start | bytes 1572864 | tf_op jit(solution)/shard_map/all_to_all | solution.py:308
  196.3 152.0 %all-gather.3.cloned.1.call-start = ((), (), s32[]{:S(2)}) async-start(), calls=%async_computation.12 | async-start | bytes 2621440 | tf_op jit(solution)/shard_map/all_gather | solution.py:373
  222.5 29.7 %collective-permute-start.24 = (bf16[512,2048]{1,0:T(8,128)(2,1)}, bf16[512,2048]{1,0:T(8,128)(2,1)}, u32[]{:S(2)}, u32[]{:S(2)}) collective-permute-start(bf16[512,2048]{1,0:T(8,128)(2,1)} %convolution_convert_fusion), channel_id=1, source_target_pairs={{0,1},{1,0},{2,3},{3,2},{4,5},{5,4},{6,7},{7,6},{8,9},{9,8},{10,11... | collective-permute-start | bytes 6291464 | tf_op jit(solution)/shard_map/ppermute | solution.py:274
  247.8 119.0 %all-gather.5.cloned.1.call-start = ((), (), s32[]{:S(2)}) async-start(), calls=%async_computation.13 | async-start | bytes 1310720 | tf_op jit(solution)/shard_map/all_gather | solution.py:373
  255.5 40.5 %collective-permute-start.27 = (bf16[128,2048]{1,0:T(8,128)(2,1)S(1)}, bf16[128,2048]{1,0:T(8,128)(2,1)S(1)}, u32[]{:S(2)}, u32[]{:S(2)}) collective-permute-start(bf16[128,2048]{1,0:T(8,128)(2,1)S(1)} %get-tuple-element.329), channel_id=1, source_target_pairs={{0,6},{1,7},{2,4},{3,5},{4,2},{5,3},{6,0},{7,1},{8,14},{9,15},{10,... | collective-permute-start | bytes 1572872 | tf_op jit(solution)/shard_map/ppermute | solution.py:274
  257.1 55.5 %collective-permute-start.26 = (bf16[128,2048]{1,0:T(8,128)(2,1)S(1)}, bf16[128,2048]{1,0:T(8,128)(2,1)S(1)}, u32[]{:S(2)}, u32[]{:S(2)}) collective-permute-start(bf16[128,2048]{1,0:T(8,128)(2,1)S(1)} %get-tuple-element.330), channel_id=1, source_target_pairs={{0,4},{1,5},{2,6},{3,7},{4,0},{5,1},{6,2},{7,3},{8,12},{9,13},{10,... | collective-permute-start | bytes 1572872 | tf_op jit(solution)/shard_map/ppermute | solution.py:274
  381.2 111.1 %all-to-all-start.3 = ((bf16[8,256,384]{1,2,0:T(8,128)(2,1)}), bf16[8,256,384]{1,2,0:T(8,128)(2,1)}, u32[]{:S(2)}, u32[]{:S(2)}) async-start(bf16[8,256,384]{1,2,0:T(8,128)(2,1)} %maximum_bitcast_fusion.1), calls=%async_computation.3 | async-start | bytes 3145728 | tf_op jit(solution)/shard_map/all_to_all | solution.py:308
  387.1 41.4 %collective-permute-start.41 = (bf16[32,2048]{1,0:T(8,128)(2,1)S(1)}, bf16[32,2048]{1,0:T(8,128)(2,1)S(1)}, u32[]{:S(2)}, u32[]{:S(2)}) collective-permute-start(bf16[32,2048]{1,0:T(8,128)(2,1)S(1)} %split.449), channel_id=1, source_target_pairs={{0,16},{1,17},{2,18},{3,19},{4,20},{5,21},{6,22},{7,23},{8,24},{9,... | collective-permute-start | bytes 393224 | tf_op jit(solution)/shard_map/ppermute | solution.py:274
  444.0 25.3 %collective-permute-start.46 = (bf16[128,2048]{1,0:T(8,128)(2,1)S(1)}, bf16[128,2048]{1,0:T(8,128)(2,1)S(1)}, u32[]{:S(2)}, u32[]{:S(2)}) collective-permute-start(bf16[128,2048]{1,0:T(8,128)(2,1)S(1)} %shard_map.257.refs_0_), channel_id=1, source_target_pairs={{0,4},{1,5},{2,6},{3,7},{4,0},{5,1},{6,2},{7,3},{8,12},{9,13},{10,... | collective-permute-start | bytes 1572872 | tf_op jit(solution)/shard_map/ppermute | solution.py:274
  445.2 25.0 %collective-permute-start.45 = (bf16[128,2048]{1,0:T(8,128)(2,1)S(1)}, bf16[128,2048]{1,0:T(8,128)(2,1)S(1)}, u32[]{:S(2)}, u32[]{:S(2)}) collective-permute-start(bf16[128,2048]{1,0:T(8,128)(2,1)S(1)} %shard_map.257.refs_0_), channel_id=1, source_target_pairs={{0,2},{1,3},{2,0},{3,1},{4,6},{5,7},{6,4},{7,5},{8,10},{9,11},{10,... | collective-permute-start | bytes 1572872 | tf_op jit(solution)/shard_map/ppermute | solution.py:274
  463.1 26.9 %collective-permute-start.53 = (bf16[128,2048]{1,0:T(8,128)(2,1)S(1)}, bf16[128,2048]{1,0:T(8,128)(2,1)S(1)}, u32[]{:S(2)}, u32[]{:S(2)}) collective-permute-start(bf16[128,2048]{1,0:T(8,128)(2,1)S(1)} %shard_map.259.refs_0_), channel_id=1, source_target_pairs={{0,4},{1,5},{2,6},{3,7},{4,0},{5,1},{6,2},{7,3},{8,12},{9,13},{10,... | collective-permute-start | bytes 1572872 | tf_op jit(solution)/shard_map/ppermute | solution.py:274
  463.6 27.3 %collective-permute-start.52 = (bf16[128,2048]{1,0:T(8,128)(2,1)S(1)}, bf16[128,2048]{1,0:T(8,128)(2,1)S(1)}, u32[]{:S(2)}, u32[]{:S(2)}) collective-permute-start(bf16[128,2048]{1,0:T(8,128)(2,1)S(1)} %shard_map.259.refs_0_), channel_id=1, source_target_pairs={{0,2},{1,3},{2,0},{3,1},{4,6},{5,7},{6,4},{7,5},{8,10},{9,11},{10,... | collective-permute-start | bytes 1572872 | tf_op jit(solution)/shard_map/ppermute | solution.py:274
  471.7 47.5 %collective-permute-start.48 = (bf16[512,2048]{1,0:T(8,128)(2,1)}, bf16[512,2048]{1,0:T(8,128)(2,1)}, u32[]{:S(2)}, u32[]{:S(2)}) collective-permute-start(bf16[512,2048]{1,0:T(8,128)(2,1)} %shard_map.258), channel_id=1, source_target_pairs={{0,1},{1,0},{2,3},{3,2},{4,5},{5,4},{6,7},{7,6},{8,9},{9,8},{10,11... | collective-permute-start | bytes 6291464 | tf_op jit(solution)/shard_map/ppermute | solution.py:274
  492.3 30.2 %collective-permute-start.55 = (bf16[512,2048]{1,0:T(8,128)(2,1)}, bf16[512,2048]{1,0:T(8,128)(2,1)}, u32[]{:S(2)}, u32[]{:S(2)}) collective-permute-start(bf16[512,2048]{1,0:T(8,128)(2,1)} %shard_map.260), channel_id=1, source_target_pairs={{0,1},{1,0},{2,3},{3,2},{4,5},{5,4},{6,7},{7,6},{8,9},{9,8},{10,11... | collective-permute-start | bytes 6291464 | tf_op jit(solution)/shard_map/ppermute | solution.py:274
  492.3 25.6 %all-to-all-start.4 = ((bf16[8,256,192]{1,2,0:T(8,128)(2,1)}), bf16[8,256,192]{1,2,0:T(8,128)(2,1)}, u32[]{:S(2)}, u32[]{:S(2)}) async-start(bf16[8,256,192]{1,2,0:T(8,128)(2,1)} %bitcast.347), calls=%async_computation.4 | async-start | bytes 1572864 | tf_op jit(solution)/shard_map/all_to_all | solution.py:308
  534.1 25.6 %collective-permute-start.57 = (bf16[128,2048]{1,0:T(8,128)(2,1)S(1)}, bf16[128,2048]{1,0:T(8,128)(2,1)S(1)}, u32[]{:S(2)}, u32[]{:S(2)}) collective-permute-start(bf16[128,2048]{1,0:T(8,128)(2,1)S(1)} %get-tuple-element.325), channel_id=1, source_target_pairs={{0,2},{1,3},{2,0},{3,1},{4,6},{5,7},{6,4},{7,5},{8,10},{9,11},{10,... | collective-permute-start | bytes 1572872 | tf_op jit(solution)/shard_map/ppermute | solution.py:274
  534.9 24.9 %collective-permute-start.59 = (bf16[128,2048]{1,0:T(8,128)(2,1)S(1)}, bf16[128,2048]{1,0:T(8,128)(2,1)S(1)}, u32[]{:S(2)}, u32[]{:S(2)}) collective-permute-start(bf16[128,2048]{1,0:T(8,128)(2,1)S(1)} %get-tuple-element.326), channel_id=1, source_target_pairs={{0,6},{1,7},{2,4},{3,5},{4,2},{5,3},{6,0},{7,1},{8,14},{9,15},{10,... | collective-permute-start | bytes 1572872 | tf_op jit(solution)/shard_map/ppermute | solution.py:274
  629.1 73.3 %all-to-all-start.5 = ((bf16[8,256,192]{1,2,0:T(8,128)(2,1)}), bf16[8,256,192]{1,2,0:T(8,128)(2,1)}, u32[]{:S(2)}, u32[]{:S(2)}) async-start(bf16[8,256,192]{1,2,0:T(8,128)(2,1)} %copy.197), calls=%async_computation.5 | async-start | bytes 1572864 | tf_op jit(solution)/shard_map/all_to_all | solution.py:308
  664.5 30.3 %collective-permute-start.81 = (bf16[128,2048]{1,0:T(8,128)(2,1)S(1)}, bf16[128,2048]{1,0:T(8,128)(2,1)S(1)}, u32[]{:S(2)}, u32[]{:S(2)}) collective-permute-start(bf16[128,2048]{1,0:T(8,128)(2,1)S(1)} %shard_map.267.refs_0_), channel_id=1, source_target_pairs={{0,6},{1,7},{2,4},{3,5},{4,2},{5,3},{6,0},{7,1},{8,14},{9,15},{10,... | collective-permute-start | bytes 1572872 | tf_op jit(solution)/shard_map/ppermute | solution.py:274
  665.9 29.9 %collective-permute-start.80 = (bf16[128,2048]{1,0:T(8,128)(2,1)S(1)}, bf16[128,2048]{1,0:T(8,128)(2,1)S(1)}, u32[]{:S(2)}, u32[]{:S(2)}) collective-permute-start(bf16[128,2048]{1,0:T(8,128)(2,1)S(1)} %shard_map.267.refs_0_), channel_id=1, source_target_pairs={{0,4},{1,5},{2,6},{3,7},{4,0},{5,1},{6,2},{7,3},{8,12},{9,13},{10,... | collective-permute-start | bytes 1572872 | tf_op jit(solution)/shard_map/ppermute | solution.py:274
  666.6 30.8 %collective-permute-start.79 = (bf16[128,2048]{1,0:T(8,128)(2,1)S(1)}, bf16[128,2048]{1,0:T(8,128)(2,1)S(1)}, u32[]{:S(2)}, u32[]{:S(2)}) collective-permute-start(bf16[128,2048]{1,0:T(8,128)(2,1)S(1)} %shard_map.267.refs_0_), channel_id=1, source_target_pairs={{0,2},{1,3},{2,0},{3,1},{4,6},{5,7},{6,4},{7,5},{8,10},{9,11},{10,... | collective-permute-start | bytes 1572872 | tf_op jit(solution)/shard_map/ppermute | solution.py:274
  671.6 40.8 %collective-permute-start.107 = (bf16[2,256,256]{2,1,0:T(8,128)(2,1)}, bf16[2,256,256]{2,1,0:T(8,128)(2,1)}, u32[]{:S(2)}, u32[]{:S(2)}) collective-permute-start(bf16[2,256,256]{2,1,0:T(8,128)(2,1)} %get-tuple-element.152), channel_id=1, source_target_pairs={{0,8},{1,9},{2,10},{3,11},{4,12},{5,13},{6,14},{7,15},{8,0},{9,1},... | collective-permute-start | bytes 786440 | tf_op jit(solution)/shard_map/ppermute | solution.py:274
  704.6 60.4 %all-to-all-start.6 = ((bf16[8,256,192]{1,2,0:T(8,128)(2,1)}), bf16[8,256,192]{1,2,0:T(8,128)(2,1)}, u32[]{:S(2)}, u32[]{:S(2)}) async-start(bf16[8,256,192]{1,2,0:T(8,128)(2,1)} %copy.198), calls=%async_computation.6 | async-start | bytes 1572864 | tf_op jit(solution)/shard_map/all_to_all | solution.py:308
  716.7 38.5 %collective-permute-start.66 = (bf16[512,2048]{1,0:T(8,128)(2,1)S(1)}, bf16[512,2048]{1,0:T(8,128)(2,1)S(1)}, u32[]{:S(2)}, u32[]{:S(2)}) collective-permute-start(bf16[512,2048]{1,0:T(8,128)(2,1)S(1)} %copy-done.109), channel_id=1, source_target_pairs={{0,1},{1,0},{2,3},{3,2},{4,5},{5,4},{6,7},{7,6},{8,9},{9,8},{10,11... | collective-permute-start | bytes 6291464 | tf_op jit(solution)/shard_map/ppermute | solution.py:274
  716.7 33.0 %collective-permute-start.85 = (bf16[512,2048]{1,0:T(8,128)(2,1)S(1)}, bf16[512,2048]{1,0:T(8,128)(2,1)S(1)}, u32[]{:S(2)}, u32[]{:S(2)}) collective-permute-start(bf16[512,2048]{1,0:T(8,128)(2,1)S(1)} %shard_map.268), channel_id=1, source_target_pairs={{0,1},{1,0},{2,3},{3,2},{4,5},{5,4},{6,7},{7,6},{8,9},{9,8},{10,11... | collective-permute-start | bytes 6291464 | tf_op jit(solution)/shard_map/ppermute | solution.py:274
  754.4 37.1 %collective-permute-start.86 = (bf16[512,2048]{1,0:T(8,128)(2,1)}, bf16[512,2048]{1,0:T(8,128)(2,1)}, u32[]{:S(2)}, u32[]{:S(2)}) collective-permute-start(bf16[512,2048]{1,0:T(8,128)(2,1)} %fusion.33), channel_id=1, source_target_pairs={{0,1},{1,0},{2,3},{3,2},{4,5},{5,4},{6,7},{7,6},{8,9},{9,8},{10,11... | collective-permute-start | bytes 6291464 | tf_op jit(solution)/shard_map/ppermute | solution.py:274
  761.3 30.2 %collective-permute-start.68 = (bf16[128,2048]{1,0:T(8,128)(2,1)}, bf16[128,2048]{1,0:T(8,128)(2,1)}, u32[]{:S(2)}, u32[]{:S(2)}) collective-permute-start(bf16[128,2048]{1,0:T(8,128)(2,1)} %get-tuple-element.323), channel_id=1, source_target_pairs={{0,4},{1,5},{2,6},{3,7},{4,0},{5,1},{6,2},{7,3},{8,12},{9,13},{10,... | collective-permute-start | bytes 1572872 | tf_op jit(solution)/shard_map/ppermute | solution.py:274
  761.3 30.2 %collective-permute-start.67 = (bf16[128,2048]{1,0:T(8,128)(2,1)}, bf16[128,2048]{1,0:T(8,128)(2,1)}, u32[]{:S(2)}, u32[]{:S(2)}) collective-permute-start(bf16[128,2048]{1,0:T(8,128)(2,1)} %get-tuple-element.324), channel_id=1, source_target_pairs={{0,2},{1,3},{2,0},{3,1},{4,6},{5,7},{6,4},{7,5},{8,10},{9,11},{10,... | collective-permute-start | bytes 1572872 | tf_op jit(solution)/shard_map/ppermute | solution.py:274
  766.1 93.7 %all-to-all-start.7 = ((bf16[8,256,192]{1,2,0:T(8,128)(2,1)}), bf16[8,256,192]{1,2,0:T(8,128)(2,1)}, u32[]{:S(2)}, u32[]{:S(2)}) async-start(bf16[8,256,192]{1,2,0:T(8,128)(2,1)} %copy.199), calls=%async_computation.7 | async-start | bytes 1572864 | tf_op jit(solution)/shard_map/all_to_all | solution.py:308
  861.9 31.3 %all-to-all-start.8 = ((bf16[8,256,192]{1,2,0:T(8,128)(2,1)}), bf16[8,256,192]{1,2,0:T(8,128)(2,1)}, u32[]{:S(2)}, u32[]{:S(2)}) async-start(bf16[8,256,192]{1,2,0:T(8,128)(2,1)} %copy.200), calls=%async_computation.8 | async-start | bytes 1572864 | tf_op jit(solution)/shard_map/all_to_all | solution.py:308
  894.3 26.1 %all-to-all-start.9 = ((bf16[8,256,192]{1,2,0:T(8,128)(2,1)}), bf16[8,256,192]{1,2,0:T(8,128)(2,1)}, u32[]{:S(2)}, u32[]{:S(2)}) async-start(bf16[8,256,192]{1,2,0:T(8,128)(2,1)} %copy.201), calls=%async_computation.9 | async-start | bytes 1572864 | tf_op jit(solution)/shard_map/all_to_all | solution.py:308
  900.1 34.3 %collective-permute-start.118 = (bf16[2,256,256]{2,1,0:T(8,128)(2,1)}, bf16[2,256,256]{2,1,0:T(8,128)(2,1)}, u32[]{:S(2)}, u32[]{:S(2)}) collective-permute-start(bf16[2,256,256]{2,1,0:T(8,128)(2,1)} %get-tuple-element.175), channel_id=1, source_target_pairs={{0,4},{1,5},{2,6},{3,7},{4,0},{5,1},{6,2},{7,3},{8,12},{9,13},{10,... | collective-permute-start | bytes 786440 | tf_op jit(solution)/shard_map/ppermute | solution.py:274
  902.2 33.3 %collective-permute-start.119 = (bf16[2,256,256]{2,1,0:T(8,128)(2,1)}, bf16[2,256,256]{2,1,0:T(8,128)(2,1)}, u32[]{:S(2)}, u32[]{:S(2)}) collective-permute-start(bf16[2,256,256]{2,1,0:T(8,128)(2,1)} %get-tuple-element.176), channel_id=1, source_target_pairs={{0,8},{1,9},{2,10},{3,11},{4,12},{5,13},{6,14},{7,15},{8,0},{9,1},... | collective-permute-start | bytes 786440 | tf_op jit(solution)/shard_map/ppermute | solution.py:274
  903.6 32.5 %collective-permute-start.120 = (bf16[2,256,256]{2,1,0:T(8,128)(2,1)}, bf16[2,256,256]{2,1,0:T(8,128)(2,1)}, u32[]{:S(2)}, u32[]{:S(2)}) collective-permute-start(bf16[2,256,256]{2,1,0:T(8,128)(2,1)} %get-tuple-element.177), channel_id=1, source_target_pairs={{0,12},{1,13},{2,14},{3,15},{4,8},{5,9},{6,10},{7,11},{8,4},{9,5},... | collective-permute-start | bytes 786440 | tf_op jit(solution)/shard_map/ppermute | solution.py:274
  906.8 33.3 %collective-permute-start.102 = (bf16[2,256,256]{2,1,0:T(8,128)(2,1)S(1)}, bf16[2,256,256]{2,1,0:T(8,128)(2,1)}, u32[]{:S(2)}, u32[]{:S(2)}) collective-permute-start(bf16[2,256,256]{2,1,0:T(8,128)(2,1)S(1)} %get-tuple-element.143), channel_id=1, source_target_pairs={{0,4},{1,5},{2,6},{3,7},{4,0},{5,1},{6,2},{7,3},{8,12},{9,13},{10,... | collective-permute-start | bytes 786440 | tf_op jit(solution)/shard_map/ppermute | solution.py:274
  922.6 58.6 %all-to-all-start.10 = ((bf16[8,256,192]{1,2,0:T(8,128)(2,1)}), bf16[8,256,192]{1,2,0:T(8,128)(2,1)}, u32[]{:S(2)}, u32[]{:S(2)}) async-start(bf16[8,256,192]{1,2,0:T(8,128)(2,1)} %copy.202), calls=%async_computation.10 | async-start | bytes 1572864 | tf_op jit(solution)/shard_map/all_to_all | solution.py:308
  934.5 24.9 %collective-permute-start.104 = (bf16[2,256,256]{2,1,0:T(8,128)(2,1)S(1)}, bf16[2,256,256]{2,1,0:T(8,128)(2,1)}, u32[]{:S(2)}, u32[]{:S(2)}) collective-permute-start(bf16[2,256,256]{2,1,0:T(8,128)(2,1)S(1)} %get-tuple-element.145), channel_id=1, source_target_pairs={{0,12},{1,13},{2,14},{3,15},{4,8},{5,9},{6,10},{7,11},{8,4},{9,5},... | collective-permute-start | bytes 786440 | tf_op jit(solution)/shard_map/ppermute | solution.py:274
  935.5 25.2 %collective-permute-start.110 = (bf16[2,256,256]{2,1,0:T(8,128)(2,1)S(1)}, bf16[2,256,256]{2,1,0:T(8,128)(2,1)}, u32[]{:S(2)}, u32[]{:S(2)}) collective-permute-start(bf16[2,256,256]{2,1,0:T(8,128)(2,1)S(1)} %get-tuple-element.159), channel_id=1, source_target_pairs={{0,4},{1,5},{2,6},{3,7},{4,0},{5,1},{6,2},{7,3},{8,12},{9,13},{10,... | collective-permute-start | bytes 786440 | tf_op jit(solution)/shard_map/ppermute | solution.py:274
  936.1 28.0 %collective-permute-start.111 = (bf16[2,256,256]{2,1,0:T(8,128)(2,1)S(1)}, bf16[2,256,256]{2,1,0:T(8,128)(2,1)}, u32[]{:S(2)}, u32[]{:S(2)}) collective-permute-start(bf16[2,256,256]{2,1,0:T(8,128)(2,1)S(1)} %get-tuple-element.160), channel_id=1, source_target_pairs={{0,8},{1,9},{2,10},{3,11},{4,12},{5,13},{6,14},{7,15},{8,0},{9,1},... | collective-permute-start | bytes 786440 | tf_op jit(solution)/shard_map/ppermute | solution.py:274
  940.0 29.8 %collective-permute-start.112 = (bf16[2,256,256]{2,1,0:T(8,128)(2,1)S(1)}, bf16[2,256,256]{2,1,0:T(8,128)(2,1)S(1)}, u32[]{:S(2)}, u32[]{:S(2)}) collective-permute-start(bf16[2,256,256]{2,1,0:T(8,128)(2,1)S(1)} %get-tuple-element.161), channel_id=1, source_target_pairs={{0,12},{1,13},{2,14},{3,15},{4,8},{5,9},{6,10},{7,11},{8,4},{9,5},... | collective-permute-start | bytes 786440 | tf_op jit(solution)/shard_map/ppermute | solution.py:274
  (270 other events, 3070.0 us)
Sparse Core Ops, SparseCore 0:
  247.9 58.8 all-gather.2
  329.8 30.7 all-gather.4

commit v2 on v1

--- a/solution.py
+++ b/solution.py
@@ -350,11 +350,9 @@
         return self.reduce_end(self.reduce_start(own, other))
 
     def spread_rows(self, rows):
-        stages = []
         for mask in (self.far_half, 2, 1):
             rows = join([rows, self.swap(rows, mask)])
-            stages.append(rows)
-        return rows, stages[0]
+        return rows
 
     def return_rows(self, partial):
         for mask in (1, 2, self.far_half):
@@ -451,26 +449,22 @@
     def ffn_parts(layer):
         parts = [w_gate[layer], w_up[layer], w_down[layer].T]
         parts = [part.reshape(shard, contexts, units) for part in parts]
-        parts = [jnp.concatenate(parts[:2], axis=2), parts[2]]
+        if layer:
+            parts = [jnp.concatenate(parts[:2], axis=2), parts[2]]
         return [part.transpose(1, 0, 2) for part in parts]
 
-    def move(piece, *others):
-        if moves:
-            others = (*others, moves[-1])
-        piece = after(piece, *others) if others else piece
-        moves.append(links.move_start(piece))
-        return moves[-1]
-
-    moves = []
     packed = []
     for layer in range(layers):
         packed.append(ffn_parts(layer))
     attn_weights, out_weights = [], []
-    ffn_weights = [[None] * 2 for _ in range(layers)]
-
-    def fetch(layer, at, *others):
-        ffn_weights[layer][at] = move(packed[layer][at], *others).reshape(width, -1)
-
+    ffn_weights = [[] for _ in range(layers)]
+
+    def fetch(layer):
+        at = len(ffn_weights[layer])
+        piece = links.move_start(packed[layer][at])
+        ffn_weights[layer].append(piece.reshape(width, -1))
+
+    fetch(0)
     for layer in range(layers):
         parts = []
         for part in range(2):
@@ -484,7 +478,7 @@
             ]
             parts.append(jnp.concatenate(columns, axis=1))
         mine, theirs = links.by_part(*parts)
-        cuts = [query_width + 2 * kv_width]
+        cuts = [query_width, query_width + 2 * kv_width] if layer else [query_width + 2 * kv_width]
         mine, theirs = jnp.split(mine, cuts, axis=1), jnp.split(theirs, cuts, axis=1)
         if layer:
             held = [links.both_parts(a, b) for a, b in zip(mine, theirs)]
@@ -500,29 +494,33 @@
     stored = []
     for layer in range(layers):
         gain_attn, gain_mlp = gains[layer], gains[layers + layer]
-        normed_in = links.spread_rows(rms_scale(current, gain_attn).astype(BF))[0]
-        projected = mm(normed_in, attn_weights[layer])
-        pair_proj, query_proj = projected[:, query_width:], projected[:, :query_width]
+        normed_in = links.spread_rows(rms_scale(current, gain_attn).astype(BF))
+        if layer:
+            query_proj, pair_proj = [mm(normed_in, w) for w in attn_weights[layer]]
+        else:
+            projected = mm(normed_in, attn_weights[layer])
+            query_proj, pair_proj = projected[:, :query_width], projected[:, query_width:]
         pairs = prep_heads(pair_proj, kv_heads, key_gains[layer], tables)
         pairs = links.spread(pairs, masks)
         queries = prep_heads(query_proj, query_heads, query_gains[layer], tables)
         if layer == 0:
             top_gradient = links.gather_rows(after(grad_output, *pairs).astype(BF))
         if layer == 0:
-            shards = after(held, *pairs)
-            attn_weights.append(links.gather_half(shards[0], True).reshape(width, -1))
-        fetch(layer, layer, *pairs)
+            out_weights.append(links.gather_half(held[2], True).reshape(width, -1))
+        fetch(layer)
         output_rows, log_totals = attend(queries, pairs, query_pos, key_pos, head_dim)
         partial = mm_nt(output_rows, out_weights[layer])
         middle = current + links.return_rows(partial)
         line = links.gather_line(rms_scale(middle, gain_mlp).astype(BF))
         if layer == 0:
-            fetch(layer, 1, line)
+            fetch(0)
         normed_mid = links.gather_square(line)
         if layer + 1 < layers:
-            fetch(layer + 1, 0, normed_mid[0])
+            fetch(layer + 1)
         inner, partial = [], []
         weights = ffn_weights[layer]
+        if len(weights) == 3:
+            weights[:2] = [jnp.concatenate(weights[:2], axis=1)]
         for rows in normed_mid:
             both = mm(rows, weights[0])
             gate, up = both[:, :units], both[:, units:]
@@ -531,10 +529,11 @@
             partial.append(mm_nt(hidden, weights[1]))
         if layer + 1 < layers:
             block_out = middle + links.reduce_rows(*partial)
-            taken = links.gather_half(after(shards[1], block_out), True)
-            out_weights.append(taken.reshape(width, -1))
+            next_pairs = links.gather_half(held[1], True).reshape(width, -1)
+            next_queries = links.gather_half(held[0], True).reshape(width, -1)
+            attn_weights.append((next_queries, next_pairs))
         else:
-            last = (middle, partial)
+            last = (middle, (partial[0], partial[1].astype(BF)))
         stored.append(
             (
                 current,
@@ -560,13 +559,16 @@
         ]
         return parts[0], parts[1], parts[2].T
 
-    def finish_attn(left, lates):
-        out_pieces, query_pieces, pair_pieces = [after(a, b) for a, b in zip(left, lates)]
+    def finish_attn(left, late):
+        out_pieces, *projected = after(left, late)
         d_out = jnp.concatenate(links.scatter_end(out_pieces), axis=1).T
-        d_query = jnp.concatenate(links.scatter_end(query_pieces), axis=1)
-        halves = links.scatter_end(pair_pieces)
-        d_key = jnp.concatenate([half[:, :kv_width] for half in halves], axis=1)
-        d_value = jnp.concatenate([half[:, kv_width:] for half in halves], axis=1)
+        shards = [links.scatter_end(pieces) for pieces in projected]
+        halves = [jnp.concatenate(pair, axis=1) for pair in zip(*shards)]
+        cuts = [query_width, query_width + kv_width]
+        d_query, d_key, d_value = [
+            jnp.concatenate(pair, axis=1)
+            for pair in zip(*[jnp.split(half, cuts, axis=1) for half in halves])
+        ]
         return d_query, d_key, d_value, d_out
 
     grad_res, moved = grad_output, None
@@ -590,11 +592,11 @@
             grad_all = top_gradient
         else:
             line = links.gather_line(grad_res.astype(BF))
-            moved[1] = move(held_grads[1], line)
+            moved[1] = links.move_start(held_grads[1])
             grad_all = links.gather_square(line)
-            final_pieces = after(final_pieces, grad_all[0])
+            final_pieces = after(final_pieces, line)
             final_out = middle_last + links.reduce_end(final_pieces)
-            weight_grads[layer + 1] = finish_attn(left, [grad_all[0]] * 3)
+            weight_grads[layer + 1] = finish_attn(left, line)
         partial, d_in, d_down = [], 0.0, 0.0
         weights = ffn_weights[layer]
         for rows, grad_rows, (gate, up, hidden) in zip(normed_mid, grad_all, inner):
@@ -615,14 +617,14 @@
         last_moved, moved = moved, [None] * 3
         pieces = links.reduce_start(*partial)
         if layer == 0:
-            moved[2] = move(held_grads[2], partial[1])
+            moved[2] = links.move_start(held_grads[2])
         grad_normed_mid = links.reduce_end(pieces)
         unused, norm_back = jax.vjp(rms_scale, middle, gain_mlp)
         grad_mid_part, d_mlp_gain = norm_back(grad_normed_mid)
         grad_mid = grad_res + grad_mid_part
-        grad_mid_all, far_rows = links.spread_rows(grad_mid.astype(BF))
+        grad_mid_all = links.spread_rows(grad_mid.astype(BF))
         at = 0 if layer == 0 else 2
-        moved[at] = move(held_grads[at], far_rows)
+        moved[at] = links.move_start(held_grads[at])
         out_pieces = links.scatter_start(mm_tn(grad_mid_all, output_rows))
         attention_gradient = mm(grad_mid_all, out_weights[layer]).astype(BF)
         if layer + 1 == layers:
@@ -642,7 +644,7 @@
             links.swap(grad, mask) for grad, mask in zip(pair_grads[1:], masks[1:])
         ]
         at = 1 if layer == 0 else 0
-        moved[at] = move(held_grads[at], *pair_grads)
+        moved[at] = links.move_start(held_grads[at])
         if layer == 0:
             weight_grads[1] = (*weight_grads[1], *finish_ffn(last_moved, query_grad))
         grad_queries, d_query_gain = prep_heads_back(
@@ -651,17 +653,22 @@
         grad_pairs, d_key_gain = prep_heads_back(
             pair_proj, kv_heads, key_gains[layer], tables, pair_grads
         )
-        grad_projected = jnp.concatenate([grad_queries, grad_pairs], axis=1)
-        partial = mm_nt(grad_projected, attn_weights[layer])
+        if layer:
+            partial = mm_nt(grad_queries, attn_weights[layer][0])
+            partial = partial + mm_nt(grad_pairs, attn_weights[layer][1])
+        else:
+            grad_projected = jnp.concatenate([grad_queries, grad_pairs], axis=1)
+            partial = mm_nt(grad_projected, attn_weights[layer])
         grad_normed_in = links.return_rows(partial)
         unused, input_back = jax.vjp(rms_scale, layer_in, gain_attn)
         grad_in_part, d_attn_gain = input_back(grad_normed_in)
         grad_res = grad_mid + grad_in_part
-        query_pieces = links.scatter_start(mm_tn(normed_in, grad_queries))
-        pair_pieces = links.scatter_start(mm_tn(normed_in, grad_pairs))
-        left = (out_pieces, query_pieces, pair_pieces)
+        projected = []
+        for grads in (grad_queries, grad_pairs):
+            projected.append(links.scatter_start(mm_tn(normed_in, grads)))
+        left = (out_pieces, *projected)
         if layer == 0:
-            weight_grads[0] = (*finish_attn(left, [grad_res] * 3), *finish_ffn(moved, partial))
+            weight_grads[0] = (*finish_attn(left, grad_res), *finish_ffn(moved, partial))
         gain_grads[layer] = (d_attn_gain, d_mlp_gain, d_query_gain[0], d_key_gain[0])
 
     wide = jnp.stack([g[0] for g in gain_grads] + [g[1] for g in gain_grads])
@@ -673,11 +680,13 @@
     )
     pieces = jnp.concatenate([wide, narrow], axis=2)
     pieces = jnp.broadcast_to(pieces, (contexts, tensors, pieces.shape[2]))
-    pieces = after(pieces.reshape(contexts * tensors, -1), moves[-1])
+    pieces = pieces.reshape(contexts * tensors, -1)
     sums = jnp.sum(lax.all_to_all(pieces, AXES, 0, 0, tiled=True), axis=0)
     wide = sums[: 2 * layers * shard].reshape(2, layers, shard)
     narrow = sums[2 * layers * shard :].reshape(2, layers, head_dim)
-    stacked = [jnp.stack([grads[member] for grads in weight_grads]) for member in range(7)]
+    stacked = []
+    for member in range(7):
+        stacked.append(jnp.stack([grads[member] for grads in weight_grads]))
     return (final_out, grad_res, *stacked, wide[0], wide[1], narrow[0], narrow[1])
 
 

time: 1020 us -> 1020 us (level)
  waiting for transfers between devices: 553 us -> 505 us
  starting transfers between devices: 200 us -> 226 us
  matrix products: 66.4 us -> 78.4 us
    ppermute x126 -> x127, waiting for transfers between devices: 517 us -> 488 us  [swap(): return lax.ppermute(value, AXES, [(i, i ^ mask) for i in range(self.count)])]
    ppermute x126 -> x127, starting transfers between devices: 144 us -> 164 us  [swap(): return lax.ppermute(value, AXES, [(i, i ^ mask) for i in range(self.count)])]
    all_to_all x11 -> x12, waiting for transfers between devices: 35.4 us -> 16.7 us  [exchange_context(): return lax.all_to_all(chunks, CONTEXT, 0, 0)]
    unnamed x371 -> x330, local copies, waits for them, and re-layouts: 50.4 us -> 38.9 us
    all_to_all x11 -> x12, starting transfers between devices: 52.6 us -> 57.8 us  [exchange_context(): return lax.all_to_all(chunks, CONTEXT, 0, 0)]
    dot_general x12 -> x13, matrix products: 22.5 us -> 26 us  [mm_nt(): lax.dot_general(a, b, (((1,), (1,)), ((), ())), preferred_element_type=F32)]
    dot_general x12 -> x13, matrix products: 24.5 us -> 26.5 us  [mm(): return jnp.dot(a, b, preferred_element_type=F32)]
  transfers between devices with their start and end apart: 140 -> 143, of which waited for: 78 -> 78; matrix products, arithmetic and copies ran while one was open for 17% -> 18% of each run, Pallas kernels for 2% -> 2%
where the time goes in v2:
time: 1020 us; the launch traced here: 1010 us
  waiting for transfers between devices  505 us (50%)
  starting transfers between devices  226 us (22%)
  local copies, waits for them, and re-layouts  90.9 us (9%)
  matrix products  78.4 us (8%)
  other arithmetic  60.6 us (6%)
  Pallas kernels  28.8 us (3%)
  between operations  17.1 us (2%)
    ppermute x127, waiting for transfers between devices, swap(): return lax.ppermute(value, AXES, [(i, i ^ mask) for i in range(self.count)])  488 us
    ppermute x127, starting transfers between devices, swap(): return lax.ppermute(value, AXES, [(i, i ^ mask) for i in range(self.count)])  164 us
    all_to_all x12, starting transfers between devices, exchange_context(): return lax.all_to_all(chunks, CONTEXT, 0, 0)  57.8 us
    unnamed x330, local copies, waits for them, and re-layouts  38.9 us
    dot_general x13, matrix products, mm(): return jnp.dot(a, b, preferred_element_type=F32)  26.5 us
    dot_general x13, matrix products, mm_nt(): lax.dot_general(a, b, (((1,), (1,)), ((), ())), preferred_element_type=F32)  26 us
    dot_general x14, matrix products, mm_tn(): lax.dot_general(a, b, (((0,), (0,)), ((), ())), preferred_element_type=F32)  26 us
    pallas_call x32, Pallas kernels, rows_call(): pl.pallas_call(kernel, out_shape=[jax.ShapeDtypeStruct(shape, kind) for s...  22.8 us
  transfers between devices with their start and end apart: 143, of which 78 were waited for; matrix products, arithmetic and copies ran while one was open for 18% of the time, Pallas kernels for 2%

profile of v2, /device:TPU:0, one launch (start us, length us, event | category | flops | bytes accessed | tf_op | source)
XLA Modules:
  0.0 1006.8 jit_solution(9115865390311103353)
XLA Ops:
  8.6 7.3 all-to-all-start
  30.6 18.0 %collective-permute-done.refs_1_ = bf16[32,2048]{1,0:T(8,128)(2,1)S(1)} collective-permute-done((bf16[32,2048]{1,0:T(8,128)(2,1)S(1)}, bf16[32,2048]{1,0:T(8,128)(2,1)S(1)}, u32[]{:S(2)}, u32[]{:S(2)}) %collective-permute-start) | collective-permute-done | bytes 131104 | tf_op jit(solution)/shard_map/ppermute | solution.py:274
  61.1 6.2 collective-permute-done.6.refs_3_
  68.0 10.8 %collective-permute-done.5.refs_2_ = bf16[2,256,512]{2,1,0:T(8,128)(2,1)S(1)} collective-permute-done((bf16[2,256,512]{2,1,0:T(8,128)(2,1)S(1)}, bf16[2,256,512]{2,1,0:T(8,128)(2,1)S(1)}, u32[]{:S(2)}, u32[]{:S(2)}) %collective-permute-start.5) | collective-permute-done | bytes 524320 | tf_op jit(solution)/shard_map/ppermute | solution.py:274
  102.1 6.3 all-to-all-start.1
  116.6 17.6 %collective-permute-done.16 = bf16[32,2048]{1,0:T(8,128)(2,1)} collective-permute-done((bf16[32,2048]{1,0:T(8,128)(2,1)}, bf16[32,2048]{1,0:T(8,128)(2,1)}, u32[]{:S(2)}, u32[]{:S(2)}) %collective-permute-start.16) | collective-permute-done | bytes 131104 | tf_op jit(solution)/shard_map/ppermute | solution.py:274
  144.9 15.7 %collective-permute-done.19.refs_3_ = bf16[32,2048]{1,0:T(8,128)(2,1)S(1)} collective-permute-done((bf16[32,2048]{1,0:T(8,128)(2,1)S(1)}, bf16[32,2048]{1,0:T(8,128)(2,1)S(1)}, u32[]{:S(2)}, u32[]{:S(2)}) %collective-permute-start.19) | collective-permute-done | bytes 131104 | tf_op jit(solution)/shard_map/ppermute | solution.py:274
  160.6 10.1 collective-permute-done.18.refs_2_
  174.3 12.2 %collective-permute-done.22.refs_3_ = bf16[128,2048]{1,0:T(8,128)(2,1)S(1)} collective-permute-done((bf16[128,2048]{1,0:T(8,128)(2,1)S(1)}, bf16[128,2048]{1,0:T(8,128)(2,1)S(1)}, u32[]{:S(2)}, u32[]{:S(2)}) %collective-permute-start.22) | collective-permute-done | bytes 524320 | tf_op jit(solution)/shard_map/ppermute | solution.py:274
  186.6 8.5 collective-permute-done.21.refs_2_
  198.3 4.9 all-to-all-start.3
  207.4 16.7 %all-to-all-done.3 = bf16[8,256,192]{1,2,0:T(8,128)(2,1)} async-done(((bf16[8,256,192]{1,2,0:T(8,128)(2,1)}), bf16[8,256,192]{1,2,0:T(8,128)(2,1)}, u32[]{:S(2)}, u32[]{:S(2)}) %all-to-all-start.3) | async-done | bytes 786464 | tf_op jit(solution)/shard_map/all_to_all | solution.py:308
  237.2 9.0 collective-permute-done.35
  261.3 14.5 %collective-permute-done.25 = bf16[128,2048]{1,0:T(8,128)(2,1)} collective-permute-done((bf16[128,2048]{1,0:T(8,128)(2,1)}, bf16[128,2048]{1,0:T(8,128)(2,1)}, u32[]{:S(2)}, u32[]{:S(2)}) %collective-permute-start.25) | collective-permute-done | bytes 524320 | tf_op jit(solution)/shard_map/ppermute | solution.py:274
  275.8 9.7 collective-permute-done.27
  285.5 16.8 %collective-permute-done.26 = bf16[128,2048]{1,0:T(8,128)(2,1)} collective-permute-done((bf16[128,2048]{1,0:T(8,128)(2,1)}, bf16[128,2048]{1,0:T(8,128)(2,1)}, u32[]{:S(2)}, u32[]{:S(2)}) %collective-permute-start.26) | collective-permute-done | bytes 524320 | tf_op jit(solution)/shard_map/ppermute | solution.py:274
  310.7 7.8 collective-permute-done.28
  324.0 6.9 collective-permute-done.31.refs_1_
  332.3 5.1 collective-permute-done.32.refs_1_
  372.7 20.7 %collective-permute-done.42 = bf16[32,2048]{1,0:T(8,128)(2,1)S(1)} collective-permute-done((bf16[32,2048]{1,0:T(8,128)(2,1)S(1)}, bf16[32,2048]{1,0:T(8,128)(2,1)S(1)}, u32[]{:S(2)}, u32[]{:S(2)}) %collective-permute-start.42) | collective-permute-done | bytes 131104 | tf_op jit(solution)/shard_map/ppermute | solution.py:274
  427.0 26.2 %collective-permute-done.52.refs_3_ = bf16[32,2048]{1,0:T(8,128)(2,1)S(1)} collective-permute-done((bf16[32,2048]{1,0:T(8,128)(2,1)S(1)}, bf16[32,2048]{1,0:T(8,128)(2,1)S(1)}, u32[]{:S(2)}, u32[]{:S(2)}) %collective-permute-start.52) | collective-permute-done | bytes 131104 | tf_op jit(solution)/shard_map/ppermute | solution.py:274
  453.2 13.5 %collective-permute-start.50 = (bf16[32,2048]{1,0:T(8,128)(2,1)S(1)}, bf16[32,2048]{1,0:T(8,128)(2,1)S(1)}, u32[]{:S(2)}, u32[]{:S(2)}) collective-permute-start(bf16[32,2048]{1,0:T(8,128)(2,1)S(1)} %convert_element_type.455.refs_0_), channel_id=1, source_target_pairs={{0,8},{1,9},{2,10},{3,11},{4,12},{5,13},{6,14},{7,15},{8,0},{9,1},... | collective-permute-start | bytes 393224 | tf_op jit(solution)/shard_map/ppermute | solution.py:274
  476.4 9.6 collective-permute-done.55.refs_3_
  486.0 9.3 collective-permute-done.54.refs_2_
  520.9 21.6 %collective-permute-done.58 = bf16[128,2048]{1,0:T(8,128)(2,1)S(1)} collective-permute-done((bf16[128,2048]{1,0:T(8,128)(2,1)S(1)}, bf16[128,2048]{1,0:T(8,128)(2,1)S(1)}, u32[]{:S(2)}, u32[]{:S(2)}) %collective-permute-start.58) | collective-permute-done | bytes 524320 | tf_op jit(solution)/shard_map/ppermute | solution.py:274
  549.8 4.6 collective-permute-done.63
  554.4 4.5 collective-permute-done.62
  560.5 7.9 collective-permute-done.64.refs_1_
  569.8 6.4 collective-permute-done.65.refs_1_
  614.7 6.6 collective-permute-done.75
  667.7 6.1 collective-permute-done.121
  675.2 6.1 collective-permute-done.85.refs_3_
  681.3 9.9 collective-permute-done.84.refs_2_
  696.0 11.8 %collective-permute-done.126 = bf16[256,256]{1,0:T(8,128)(2,1)S(1)} collective-permute-done((bf16[256,256]{1,0:T(8,128)(2,1)S(1)}, bf16[256,256]{1,0:T(8,128)(2,1)S(1)}, u32[]{:S(2)}, u32[]{:S(2)}) %collective-permute-start.126) | collective-permute-done | bytes 131104 | tf_op jit(solution)/shard_map/ppermute | solution.py:274
  732.8 6.4 collective-permute-done.70
  739.2 13.2 %collective-permute-done.69 = bf16[128,2048]{1,0:T(8,128)(2,1)} collective-permute-done((bf16[128,2048]{1,0:T(8,128)(2,1)}, bf16[128,2048]{1,0:T(8,128)(2,1)}, u32[]{:S(2)}, u32[]{:S(2)}) %collective-permute-start.69) | collective-permute-done | bytes 524320 | tf_op jit(solution)/shard_map/ppermute | solution.py:274
  758.6 5.6 fusion.127
  780.1 13.7 %collective-permute-done.88 = bf16[128,2048]{1,0:T(8,128)(2,1)S(1)} collective-permute-done((bf16[128,2048]{1,0:T(8,128)(2,1)S(1)}, bf16[128,2048]{1,0:T(8,128)(2,1)S(1)}, u32[]{:S(2)}, u32[]{:S(2)}) %collective-permute-start.88) | collective-permute-done | bytes 524320 | tf_op jit(solution)/shard_map/ppermute | solution.py:274
  793.8 7.8 collective-permute-done.89
  817.7 7.8 collective-permute-done.91
  825.5 6.9 collective-permute-done.93
  832.4 7.5 collective-permute-done.92
  852.5 18.7 %collective-permute-done.94.refs_1_ = bf16[32,2048]{1,0:T(8,128)(2,1)S(1)} collective-permute-done((bf16[32,2048]{1,0:T(8,128)(2,1)S(1)}, bf16[32,2048]{1,0:T(8,128)(2,1)S(1)}, u32[]{:S(2)}, u32[]{:S(2)}) %collective-permute-start.94) | collective-permute-done | bytes 131104 | tf_op jit(solution)/shard_map/ppermute | solution.py:274
  879.8 5.3 all-to-all-start.7
  921.6 4.8 collective-permute-done.101
  956.0 4.9 collective-permute-done.108
  965.7 5.9 collective-permute-done.111
  979.7 10.6 %collective-permute-done.123 = bf16[256,256]{1,0:T(8,128)(2,1)S(1)} collective-permute-done((bf16[256,256]{1,0:T(8,128)(2,1)S(1)}, bf16[256,256]{1,0:T(8,128)(2,1)S(1)}, u32[]{:S(2)}, u32[]{:S(2)}) %collective-permute-start.123) | collective-permute-done | bytes 131104 | tf_op jit(solution)/shard_map/ppermute | solution.py:274
  (841 shorter events, 502.1 us)
Async XLA Ops:
  22.8 35.3 %collective-permute-start.10 = (bf16[256,256]{1,0:T(8,128)(2,1)}, bf16[256,256]{1,0:T(8,128)(2,1)S(1)}, u32[]{:S(2)}, u32[]{:S(2)}) collective-permute-start(bf16[256,256]{1,0:T(8,128)(2,1)} %split.335), channel_id=1, source_target_pairs={{0,16},{1,17},{2,18},{3,19},{4,20},{5,21},{6,22},{7,23},{8,24},{9,... | collective-permute-start | bytes 393224 | tf_op jit(solution)/shard_map/ppermute | solution.py:274
  25.8 25.6 %collective-permute-start.3 = (bf16[256,512]{1,0:T(8,128)(2,1)S(1)}, bf16[256,512]{1,0:T(8,128)(2,1)S(1)}, u32[]{:S(2)}, u32[]{:S(2)}) collective-permute-start(bf16[256,512]{1,0:T(8,128)(2,1)S(1)} %split.333), channel_id=1, source_target_pairs={{0,16},{1,17},{2,18},{3,19},{4,20},{5,21},{6,22},{7,23},{8,24},{9,... | collective-permute-start | bytes 786440 | tf_op jit(solution)/shard_map/ppermute | solution.py:274
  53.2 25.6 %collective-permute-start.5 = (bf16[2,256,512]{2,1,0:T(8,128)(2,1)S(1)}, bf16[2,256,512]{2,1,0:T(8,128)(2,1)S(1)}, u32[]{:S(2)}, u32[]{:S(2)}) collective-permute-start(bf16[2,256,512]{2,1,0:T(8,128)(2,1)S(1)} %bitcast.324), channel_id=1, source_target_pairs={{0,8},{1,9},{2,10},{3,11},{4,12},{5,13},{6,14},{7,15},{8,0},{9,1},... | collective-permute-start | bytes 1572872 | tf_op jit(solution)/shard_map/ppermute | solution.py:274
  55.7 24.5 %collective-permute-start.2 = (bf16[128,2048]{1,0:T(8,128)(2,1)S(1)}, bf16[128,2048]{1,0:T(8,128)(2,1)}, u32[]{:S(2)}, u32[]{:S(2)}) collective-permute-start(bf16[128,2048]{1,0:T(8,128)(2,1)S(1)} %shard_map.238.refs_0_), channel_id=1, source_target_pairs={{0,1},{1,0},{2,3},{3,2},{4,5},{5,4},{6,7},{7,6},{8,9},{9,8},{10,11... | collective-permute-start | bytes 1572872 | tf_op jit(solution)/shard_map/ppermute | solution.py:274
  58.2 27.8 %collective-permute-start.13 = (bf16[2,256,256]{2,1,0:T(8,128)(2,1)S(1)}, bf16[2,256,256]{2,1,0:T(8,128)(2,1)S(1)}, u32[]{:S(2)}, u32[]{:S(2)}) collective-permute-start(bf16[2,256,256]{2,1,0:T(8,128)(2,1)S(1)} %bitcast.327), channel_id=1, source_target_pairs={{0,12},{1,13},{2,14},{3,15},{4,8},{5,9},{6,10},{7,11},{8,4},{9,5},... | collective-permute-start | bytes 786440 | tf_op jit(solution)/shard_map/ppermute | solution.py:274
  102.1 33.4 %all-to-all-start.1 = ((bf16[8,256,192]{1,2,0:T(8,128)(2,1)}), bf16[8,256,192]{1,2,0:T(8,128)(2,1)}, u32[]{:S(2)}, u32[]{:S(2)}) async-start(bf16[8,256,192]{1,2,0:T(8,128)(2,1)} %bitcast.363), calls=%async_computation.1 | async-start | bytes 1572864 | tf_op jit(solution)/shard_map/all_to_all | solution.py:308
  135.4 62.8 %all-to-all-start.2 = ((bf16[8,256,192]{1,2,0:T(8,128)(2,1)}), bf16[8,256,192]{1,2,0:T(8,128)(2,1)}, u32[]{:S(2)}, u32[]{:S(2)}) async-start(bf16[8,256,192]{1,2,0:T(8,128)(2,1)} %bitcast.362), calls=%async_computation.2 | async-start | bytes 1572864 | tf_op jit(solution)/shard_map/all_to_all | solution.py:308
  144.3 26.4 %collective-permute-start.18 = (bf16[32,2048]{1,0:T(8,128)(2,1)S(1)}, bf16[32,2048]{1,0:T(8,128)(2,1)S(1)}, u32[]{:S(2)}, u32[]{:S(2)}) collective-permute-start(bf16[32,2048]{1,0:T(8,128)(2,1)S(1)} %multiply_convert_fusion.14.refs_0_), channel_id=1, source_target_pairs={{0,16},{1,17},{2,18},{3,19},{4,20},{5,21},{6,22},{7,23},{8,24},{9,... | collective-permute-start | bytes 393224 | tf_op jit(solution)/shard_map/ppermute | solution.py:274
  144.3 26.4 %collective-permute-start.17 = (bf16[32,2048]{1,0:T(8,128)(2,1)S(1)}, bf16[32,2048]{1,0:T(8,128)(2,1)S(1)}, u32[]{:S(2)}, u32[]{:S(2)}) collective-permute-start(bf16[32,2048]{1,0:T(8,128)(2,1)S(1)} %multiply_convert_fusion.14.refs_0_), channel_id=1, source_target_pairs={{0,8},{1,9},{2,10},{3,11},{4,12},{5,13},{6,14},{7,15},{8,0},{9,1},... | collective-permute-start | bytes 393224 | tf_op jit(solution)/shard_map/ppermute | solution.py:274
  197.0 28.7 %collective-permute-start.23 = (bf16[512,2048]{1,0:T(8,128)(2,1)}, bf16[512,2048]{1,0:T(8,128)(2,1)}, u32[]{:S(2)}, u32[]{:S(2)}) collective-permute-start(bf16[512,2048]{1,0:T(8,128)(2,1)} %shard_map.248), channel_id=1, source_target_pairs={{0,1},{1,0},{2,3},{3,2},{4,5},{5,4},{6,7},{7,6},{8,9},{9,8},{10,11... | collective-permute-start | bytes 6291464 | tf_op jit(solution)/shard_map/ppermute | solution.py:274
  198.3 25.8 %all-to-all-start.3 = ((bf16[8,256,192]{1,2,0:T(8,128)(2,1)}), bf16[8,256,192]{1,2,0:T(8,128)(2,1)}, u32[]{:S(2)}, u32[]{:S(2)}) async-start(bf16[8,256,192]{1,2,0:T(8,128)(2,1)} %bitcast.370), calls=%async_computation.3 | async-start | bytes 1572864 | tf_op jit(solution)/shard_map/all_to_all | solution.py:308
  203.1 136.3 %all-gather.6.cloned.1.call-start = ((), (), s32[]{:S(2)}) async-start(), calls=%async_computation.14 | async-start | bytes 1310720 | tf_op jit(solution)/shard_map/all_gather | solution.py:371
  234.2 26.2 %collective-permute-start.34 = (bf16[256,256]{1,0:T(8,128)(2,1)}, bf16[256,256]{1,0:T(8,128)(2,1)S(1)}, u32[]{:S(2)}, u32[]{:S(2)}) collective-permute-start(bf16[256,256]{1,0:T(8,128)(2,1)} %get-tuple-element.359), channel_id=1, source_target_pairs={{0,16},{1,17},{2,18},{3,19},{4,20},{5,21},{6,22},{7,23},{8,24},{9,... | collective-permute-start | bytes 393224 | tf_op jit(solution)/shard_map/ppermute | solution.py:274
  247.0 99.2 %all-gather.4.cloned.1.call-start = ((), (), s32[]{:S(2)}) async-start(), calls=%async_computation.13 | async-start | bytes 1310720 | tf_op jit(solution)/shard_map/all_gather | solution.py:371
  258.3 27.1 %collective-permute-start.27 = (bf16[128,2048]{1,0:T(8,128)(2,1)}, bf16[128,2048]{1,0:T(8,128)(2,1)}, u32[]{:S(2)}, u32[]{:S(2)}) collective-permute-start(bf16[128,2048]{1,0:T(8,128)(2,1)} %get-tuple-element.301), channel_id=1, source_target_pairs={{0,6},{1,7},{2,4},{3,5},{4,2},{5,3},{6,0},{7,1},{8,14},{9,15},{10,... | collective-permute-start | bytes 1572872 | tf_op jit(solution)/shard_map/ppermute | solution.py:274
  259.1 43.2 %collective-permute-start.26 = (bf16[128,2048]{1,0:T(8,128)(2,1)}, bf16[128,2048]{1,0:T(8,128)(2,1)}, u32[]{:S(2)}, u32[]{:S(2)}) collective-permute-start(bf16[128,2048]{1,0:T(8,128)(2,1)} %get-tuple-element.302), channel_id=1, source_target_pairs={{0,4},{1,5},{2,6},{3,7},{4,0},{5,1},{6,2},{7,3},{8,12},{9,13},{10,... | collective-permute-start | bytes 1572872 | tf_op jit(solution)/shard_map/ppermute | solution.py:274
  261.2 95.1 %all-gather.8.cloned.1.call-start = ((), (), s32[]{:S(2)}) async-start(), calls=%async_computation.15 | async-start | bytes 1310720 | tf_op jit(solution)/shard_map/all_gather | solution.py:371
  261.2 48.7 %collective-permute-start.39 = (bf16[256,256]{1,0:T(8,128)(2,1)S(1)}, bf16[256,256]{1,0:T(8,128)(2,1)S(1)}, u32[]{:S(2)}, u32[]{:S(2)}) collective-permute-start(bf16[256,256]{1,0:T(8,128)(2,1)S(1)} %get-tuple-element.357), channel_id=1, source_target_pairs={{0,16},{1,17},{2,18},{3,19},{4,20},{5,21},{6,22},{7,23},{8,24},{9,... | collective-permute-start | bytes 393224 | tf_op jit(solution)/shard_map/ppermute | solution.py:274
  363.2 51.9 %all-to-all-start.5 = ((bf16[8,256,192]{1,2,0:T(8,128)(2,1)}), bf16[8,256,192]{1,2,0:T(8,128)(2,1)}, u32[]{:S(2)}, u32[]{:S(2)}) async-start(bf16[8,256,192]{1,2,0:T(8,128)(2,1)} %bitcast.366), calls=%async_computation.5 | async-start | bytes 1572864 | tf_op jit(solution)/shard_map/all_to_all | solution.py:308
  410.8 62.3 %collective-permute-start.48 = (bf16[128,2048]{1,0:T(8,128)(2,1)}, bf16[128,2048]{1,0:T(8,128)(2,1)}, u32[]{:S(2)}, u32[]{:S(2)}) collective-permute-start(bf16[128,2048]{1,0:T(8,128)(2,1)} %shard_map.258.refs_0_), channel_id=1, source_target_pairs={{0,6},{1,7},{2,4},{3,5},{4,2},{5,3},{6,0},{7,1},{8,14},{9,15},{10,... | collective-permute-start | bytes 1572872 | tf_op jit(solution)/shard_map/ppermute | solution.py:274
  415.1 84.0 %all-to-all-start.4 = ((bf16[8,256,384]{1,2,0:T(8,128)(2,1)}), bf16[8,256,384]{1,2,0:T(8,128)(2,1)}, u32[]{:S(2)}, u32[]{:S(2)}) async-start(bf16[8,256,384]{1,2,0:T(8,128)(2,1)} %maximum_bitcast_fusion), calls=%async_computation.4 | async-start | bytes 3145728 | tf_op jit(solution)/shard_map/all_to_all | solution.py:308
  419.4 54.3 %collective-permute-start.47 = (bf16[128,2048]{1,0:T(8,128)(2,1)}, bf16[128,2048]{1,0:T(8,128)(2,1)S(1)}, u32[]{:S(2)}, u32[]{:S(2)}) collective-permute-start(bf16[128,2048]{1,0:T(8,128)(2,1)} %shard_map.258.refs_0_), channel_id=1, source_target_pairs={{0,4},{1,5},{2,6},{3,7},{4,0},{5,1},{6,2},{7,3},{8,12},{9,13},{10,... | collective-permute-start | bytes 1572872 | tf_op jit(solution)/shard_map/ppermute | solution.py:274
  421.3 52.4 %collective-permute-start.46 = (bf16[128,2048]{1,0:T(8,128)(2,1)}, bf16[128,2048]{1,0:T(8,128)(2,1)S(1)}, u32[]{:S(2)}, u32[]{:S(2)}) collective-permute-start(bf16[128,2048]{1,0:T(8,128)(2,1)} %shard_map.258.refs_0_), channel_id=1, source_target_pairs={{0,2},{1,3},{2,0},{3,1},{4,6},{5,7},{6,4},{7,5},{8,10},{9,11},{10,... | collective-permute-start | bytes 1572872 | tf_op jit(solution)/shard_map/ppermute | solution.py:274
  423.6 29.6 %collective-permute-start.52 = (bf16[32,2048]{1,0:T(8,128)(2,1)S(1)}, bf16[32,2048]{1,0:T(8,128)(2,1)S(1)}, u32[]{:S(2)}, u32[]{:S(2)}) collective-permute-start(bf16[32,2048]{1,0:T(8,128)(2,1)S(1)} %convert_element_type.455.refs_0_), channel_id=1, source_target_pairs={{0,24},{1,25},{2,26},{3,27},{4,28},{5,29},{6,30},{7,31},{8,16},{9,... | collective-permute-start | bytes 393224 | tf_op jit(solution)/shard_map/ppermute | solution.py:274
  427.0 40.9 %collective-permute-start.51 = (bf16[32,2048]{1,0:T(8,128)(2,1)S(1)}, bf16[32,2048]{1,0:T(8,128)(2,1)S(1)}, u32[]{:S(2)}, u32[]{:S(2)}) collective-permute-start(bf16[32,2048]{1,0:T(8,128)(2,1)S(1)} %convert_element_type.455.refs_0_), channel_id=1, source_target_pairs={{0,16},{1,17},{2,18},{3,19},{4,20},{5,21},{6,22},{7,23},{8,24},{9,... | collective-permute-start | bytes 393224 | tf_op jit(solution)/shard_map/ppermute | solution.py:274
  476.4 25.7 %collective-permute-start.49 = (bf16[512,2048]{1,0:T(8,128)(2,1)}, bf16[512,2048]{1,0:T(8,128)(2,1)}, u32[]{:S(2)}, u32[]{:S(2)}) collective-permute-start(bf16[512,2048]{1,0:T(8,128)(2,1)} %shard_map.259), channel_id=1, source_target_pairs={{0,1},{1,0},{2,3},{3,2},{4,5},{5,4},{6,7},{7,6},{8,9},{9,8},{10,11... | collective-permute-start | bytes 6291464 | tf_op jit(solution)/shard_map/ppermute | solution.py:274
  517.3 25.1 %collective-permute-start.58 = (bf16[128,2048]{1,0:T(8,128)(2,1)S(1)}, bf16[128,2048]{1,0:T(8,128)(2,1)S(1)}, u32[]{:S(2)}, u32[]{:S(2)}) collective-permute-start(bf16[128,2048]{1,0:T(8,128)(2,1)S(1)} %get-tuple-element.297), channel_id=1, source_target_pairs={{0,2},{1,3},{2,0},{3,1},{4,6},{5,7},{6,4},{7,5},{8,10},{9,11},{10,... | collective-permute-start | bytes 1572872 | tf_op jit(solution)/shard_map/ppermute | solution.py:274
  593.5 129.7 %all-to-all-start.11 = ((bf16[8,256,192]{1,2,0:T(8,128)(2,1)}), bf16[8,256,192]{1,2,0:T(8,128)(2,1)}, u32[]{:S(2)}, u32[]{:S(2)}) async-start(bf16[8,256,192]{1,2,0:T(8,128)(2,1)} %bitcast.357), calls=%async_computation.11 | async-start | bytes 1572864 | tf_op jit(solution)/shard_map/all_to_all | solution.py:308
  656.4 24.9 %collective-permute-start.85 = (bf16[128,2048]{1,0:T(8,128)(2,1)S(1)}, bf16[128,2048]{1,0:T(8,128)(2,1)S(1)}, u32[]{:S(2)}, u32[]{:S(2)}) collective-permute-start(bf16[128,2048]{1,0:T(8,128)(2,1)S(1)} %shard_map.268.refs_0_), channel_id=1, source_target_pairs={{0,6},{1,7},{2,4},{3,5},{4,2},{5,3},{6,0},{7,1},{8,14},{9,15},{10,... | collective-permute-start | bytes 1572872 | tf_op jit(solution)/shard_map/ppermute | solution.py:274
  663.0 28.2 %collective-permute-start.84 = (bf16[128,2048]{1,0:T(8,128)(2,1)S(1)}, bf16[128,2048]{1,0:T(8,128)(2,1)S(1)}, u32[]{:S(2)}, u32[]{:S(2)}) collective-permute-start(bf16[128,2048]{1,0:T(8,128)(2,1)S(1)} %shard_map.268.refs_0_), channel_id=1, source_target_pairs={{0,4},{1,5},{2,6},{3,7},{4,0},{5,1},{6,2},{7,3},{8,12},{9,13},{10,... | collective-permute-start | bytes 1572872 | tf_op jit(solution)/shard_map/ppermute | solution.py:274
  663.6 27.6 %collective-permute-start.83 = (bf16[128,2048]{1,0:T(8,128)(2,1)S(1)}, bf16[128,2048]{1,0:T(8,128)(2,1)S(1)}, u32[]{:S(2)}, u32[]{:S(2)}) collective-permute-start(bf16[128,2048]{1,0:T(8,128)(2,1)S(1)} %shard_map.268.refs_0_), channel_id=1, source_target_pairs={{0,2},{1,3},{2,0},{3,1},{4,6},{5,7},{6,4},{7,5},{8,10},{9,11},{10,... | collective-permute-start | bytes 1572872 | tf_op jit(solution)/shard_map/ppermute | solution.py:274
  667.7 47.2 %collective-permute-start.67 = (bf16[512,2048]{1,0:T(8,128)(2,1)S(1)}, bf16[512,2048]{1,0:T(8,128)(2,1)S(1)}, u32[]{:S(2)}, u32[]{:S(2)}) collective-permute-start(bf16[512,2048]{1,0:T(8,128)(2,1)S(1)} %convolution_convert_fusion), channel_id=1, source_target_pairs={{0,1},{1,0},{2,3},{3,2},{4,5},{5,4},{6,7},{7,6},{8,9},{9,8},{10,11... | collective-permute-start | bytes 6291464 | tf_op jit(solution)/shard_map/ppermute | solution.py:274
  714.9 43.7 %collective-permute-start.87 = (bf16[512,2048]{1,0:T(8,128)(2,1)}, bf16[512,2048]{1,0:T(8,128)(2,1)}, u32[]{:S(2)}, u32[]{:S(2)}) collective-permute-start(bf16[512,2048]{1,0:T(8,128)(2,1)} %convolution_convert_fusion.2), channel_id=1, source_target_pairs={{0,1},{1,0},{2,3},{3,2},{4,5},{5,4},{6,7},{7,6},{8,9},{9,8},{10,11... | collective-permute-start | bytes 6291464 | tf_op jit(solution)/shard_map/ppermute | solution.py:274
  720.3 32.2 %collective-permute-start.69 = (bf16[128,2048]{1,0:T(8,128)(2,1)}, bf16[128,2048]{1,0:T(8,128)(2,1)}, u32[]{:S(2)}, u32[]{:S(2)}) collective-permute-start(bf16[128,2048]{1,0:T(8,128)(2,1)} %get-tuple-element.295), channel_id=1, source_target_pairs={{0,4},{1,5},{2,6},{3,7},{4,0},{5,1},{6,2},{7,3},{8,12},{9,13},{10,... | collective-permute-start | bytes 1572872 | tf_op jit(solution)/shard_map/ppermute | solution.py:274
  721.7 30.7 %collective-permute-start.68 = (bf16[128,2048]{1,0:T(8,128)(2,1)}, bf16[128,2048]{1,0:T(8,128)(2,1)}, u32[]{:S(2)}, u32[]{:S(2)}) collective-permute-start(bf16[128,2048]{1,0:T(8,128)(2,1)} %get-tuple-element.296), channel_id=1, source_target_pairs={{0,2},{1,3},{2,0},{3,1},{4,6},{5,7},{6,4},{7,5},{8,10},{9,11},{10,... | collective-permute-start | bytes 1572872 | tf_op jit(solution)/shard_map/ppermute | solution.py:274
  723.2 41.0 %all-to-all-start.9 = ((bf16[8,256,192]{1,2,0:T(8,128)(2,1)}), bf16[8,256,192]{1,2,0:T(8,128)(2,1)}, u32[]{:S(2)}, u32[]{:S(2)}) async-start(bf16[8,256,192]{1,2,0:T(8,128)(2,1)} %bitcast.359), calls=%async_computation.9 | async-start | bytes 1572864 | tf_op jit(solution)/shard_map/all_to_all | solution.py:308
  764.2 40.1 %all-to-all-start.10 = ((bf16[8,256,192]{1,2,0:T(8,128)(2,1)}), bf16[8,256,192]{1,2,0:T(8,128)(2,1)S(1)}, u32[]{:S(2)}, u32[]{:S(2)}) async-start(bf16[8,256,192]{1,2,0:T(8,128)(2,1)} %bitcast.358), calls=%async_computation.10 | async-start | bytes 1572864 | tf_op jit(solution)/shard_map/all_to_all | solution.py:308
  773.2 28.4 %collective-permute-start.89 = (bf16[128,2048]{1,0:T(8,128)(2,1)S(1)}, bf16[128,2048]{1,0:T(8,128)(2,1)S(1)}, u32[]{:S(2)}, u32[]{:S(2)}) collective-permute-start(bf16[128,2048]{1,0:T(8,128)(2,1)S(1)} %get-tuple-element.293), channel_id=1, source_target_pairs={{0,4},{1,5},{2,6},{3,7},{4,0},{5,1},{6,2},{7,3},{8,12},{9,13},{10,... | collective-permute-start | bytes 1572872 | tf_op jit(solution)/shard_map/ppermute | solution.py:274
  804.3 37.3 %all-to-all-start.8 = ((bf16[8,256,192]{1,2,0:T(8,128)(2,1)}), bf16[8,256,192]{1,2,0:T(8,128)(2,1)}, u32[]{:S(2)}, u32[]{:S(2)}) async-start(bf16[8,256,192]{1,2,0:T(8,128)(2,1)} %bitcast.361), calls=%async_computation.8 | async-start | bytes 1572864 | tf_op jit(solution)/shard_map/all_to_all | solution.py:308
  814.3 25.6 %collective-permute-start.92 = (bf16[32,2048]{1,0:T(8,128)(2,1)S(1)}, bf16[32,2048]{1,0:T(8,128)(2,1)S(1)}, u32[]{:S(2)}, u32[]{:S(2)}) collective-permute-start(bf16[32,2048]{1,0:T(8,128)(2,1)S(1)} %get-tuple-element.329), channel_id=1, source_target_pairs={{0,16},{1,17},{2,18},{3,19},{4,20},{5,21},{6,22},{7,23},{8,24},{9,... | collective-permute-start | bytes 393224 | tf_op jit(solution)/shard_map/ppermute | solution.py:274
  841.6 38.2 %all-to-all-start.6 = ((bf16[8,256,192]{1,2,0:T(8,128)(2,1)}), bf16[8,256,192]{1,2,0:T(8,128)(2,1)}, u32[]{:S(2)}, u32[]{:S(2)}) async-start(bf16[8,256,192]{1,2,0:T(8,128)(2,1)} %bitcast.312), calls=%async_computation.6 | async-start | bytes 1572864 | tf_op jit(solution)/shard_map/all_to_all | solution.py:308
  846.7 24.5 %collective-permute-start.94 = (bf16[32,2048]{1,0:T(8,128)(2,1)S(1)}, bf16[32,2048]{1,0:T(8,128)(2,1)S(1)}, u32[]{:S(2)}, u32[]{:S(2)}) collective-permute-start(bf16[32,2048]{1,0:T(8,128)(2,1)S(1)} %get-tuple-element.265.refs_0_), channel_id=1, source_target_pairs={{0,16},{1,17},{2,18},{3,19},{4,20},{5,21},{6,22},{7,23},{8,24},{9,... | collective-permute-start | bytes 393224 | tf_op jit(solution)/shard_map/ppermute | solution.py:274
  879.8 31.1 %all-to-all-start.7 = ((bf16[8,256,192]{1,2,0:T(8,128)(2,1)}), bf16[8,256,192]{1,2,0:T(8,128)(2,1)}, u32[]{:S(2)}, u32[]{:S(2)}) async-start(bf16[8,256,192]{1,2,0:T(8,128)(2,1)} %bitcast.360), calls=%async_computation.7 | async-start | bytes 1572864 | tf_op jit(solution)/shard_map/all_to_all | solution.py:308
  897.3 50.8 %collective-permute-start.103 = (bf16[2,256,256]{2,1,0:T(8,128)(2,1)}, bf16[2,256,256]{2,1,0:T(8,128)(2,1)}, u32[]{:S(2)}, u32[]{:S(2)}) collective-permute-start(bf16[2,256,256]{2,1,0:T(8,128)(2,1)} %get-tuple-element.122), channel_id=1, source_target_pairs={{0,4},{1,5},{2,6},{3,7},{4,0},{5,1},{6,2},{7,3},{8,12},{9,13},{10,... | collective-permute-start | bytes 786440 | tf_op jit(solution)/shard_map/ppermute | solution.py:274
  899.2 51.5 %collective-permute-start.104 = (bf16[2,256,256]{2,1,0:T(8,128)(2,1)}, bf16[2,256,256]{2,1,0:T(8,128)(2,1)}, u32[]{:S(2)}, u32[]{:S(2)}) collective-permute-start(bf16[2,256,256]{2,1,0:T(8,128)(2,1)} %get-tuple-element.123), channel_id=1, source_target_pairs={{0,8},{1,9},{2,10},{3,11},{4,12},{5,13},{6,14},{7,15},{8,0},{9,1},... | collective-permute-start | bytes 786440 | tf_op jit(solution)/shard_map/ppermute | solution.py:274
  900.9 50.3 %collective-permute-start.105 = (bf16[2,256,256]{2,1,0:T(8,128)(2,1)}, bf16[2,256,256]{2,1,0:T(8,128)(2,1)}, u32[]{:S(2)}, u32[]{:S(2)}) collective-permute-start(bf16[2,256,256]{2,1,0:T(8,128)(2,1)} %get-tuple-element.124), channel_id=1, source_target_pairs={{0,12},{1,13},{2,14},{3,15},{4,8},{5,9},{6,10},{7,11},{8,4},{9,5},... | collective-permute-start | bytes 786440 | tf_op jit(solution)/shard_map/ppermute | solution.py:274
  902.4 49.2 %collective-permute-start.106 = (bf16[2,256,256]{2,1,0:T(8,128)(2,1)}, bf16[2,256,256]{2,1,0:T(8,128)(2,1)}, u32[]{:S(2)}, u32[]{:S(2)}) collective-permute-start(bf16[2,256,256]{2,1,0:T(8,128)(2,1)} %get-tuple-element.126), channel_id=1, source_target_pairs={{0,4},{1,5},{2,6},{3,7},{4,0},{5,1},{6,2},{7,3},{8,12},{9,13},{10,... | collective-permute-start | bytes 786440 | tf_op jit(solution)/shard_map/ppermute | solution.py:274
  944.7 52.2 %all-to-all-start.12 = ((f32[32,1,1536]{2,1,0:T(1,128)}), f32[32,1,1536]{2,1,0:T(1,128)}, u32[]{:S(2)}, u32[]{:S(2)}) async-start(f32[32,1,1536]{2,1,0:T(1,128)} %all_to_all.54), calls=%async_computation.12 | async-start | bytes 393216 | tf_op jit(solution)/shard_map/all_to_all | solution.py:684
  (255 other events, 2878.2 us)
Sparse Core Ops, SparseCore 0:
  247.1 32.2 all-gather.5
  281.5 31.0 all-gather.3
  314.7 30.2 all-gather.7

commit v3 on v2

--- a/solution.py
+++ b/solution.py
@@ -109,6 +109,43 @@
     shape = (parts, rows // places, width)
     shapes = [(shape, BF if slot else own) for slot in range(places)]
     return index_call(split_at_kernel, shapes, index, x)
+
+
+def pack_kernel(layer, gate_ref, up_ref, *outs):
+    slots, rows, width = outs[0].shape
+    units = width // 2
+    for part, out in enumerate(outs):
+        row_at = slice(part * rows, (part + 1) * rows)
+        gate = gate_ref[layer, row_at, :].astype(F32)
+        up = up_ref[layer, row_at, :].astype(F32)
+        for slot in range(slots):
+            at = slice(slot * units, (slot + 1) * units)
+            out[slot, :, :units] = gate[:, at].astype(BF)
+            out[slot, :, units:] = up[:, at].astype(BF)
+
+
+def pack(w_gate, w_up, layer, slots, parts):
+    rows, columns = w_gate.shape[1:]
+    shapes = [((slots, rows // parts, 2 * columns // slots), BF)] * parts
+    return rows_call(functools.partial(pack_kernel, layer), shapes, w_gate, w_up)
+
+
+def unpack_kernel(*refs):
+    *layers, gate_ref, up_ref = refs
+    for layer, pieces in enumerate(layers):
+        count, _, width = pieces.shape
+        units = width // 2
+        for slot in range(count):
+            at = slice(slot * units, (slot + 1) * units)
+            both = pieces[slot].astype(F32)
+            gate_ref[layer, :, at] = both[:, :units]
+            up_ref[layer, :, at] = both[:, units:]
+
+
+def unpack(layers):
+    count, rows, width = layers[0].shape
+    shape = (len(layers), rows, count * width // 2)
+    return rows_call(unpack_kernel, [(shape, F32)] * 2, *layers)
 
 
 def prep_kernel(heads, x_ref, gain_ref, cos_ref, sin_ref, out_ref):
@@ -337,7 +374,8 @@
         return self.exchange_context(chunks)
 
     def reduce_start(self, own, other):
-        half = own + self.swap(other.astype(BF), 1).astype(F32)
+        other = self.swap(other.astype(BF), 1)
+        half = lax.optimization_barrier(own.astype(BF)).astype(F32) + other.astype(F32)
         masks = self.square_masks()
         return self.fetch(jnp.split(half, len(masks), axis=0), masks)
 
@@ -447,11 +485,8 @@
     gains = gains.astype(F32)
 
     def ffn_parts(layer):
-        parts = [w_gate[layer], w_up[layer], w_down[layer].T]
-        parts = [part.reshape(shard, contexts, units) for part in parts]
-        if layer:
-            parts = [jnp.concatenate(parts[:2], axis=2), parts[2]]
-        return [part.transpose(1, 0, 2) for part in parts]
+        parts = pack(w_gate, w_up, layer, contexts, 1 if layer else 2)
+        return [*parts, w_down[layer].reshape(contexts, units, shard)]
 
     packed = []
     for layer in range(layers):
@@ -462,7 +497,7 @@
     def fetch(layer):
         at = len(ffn_weights[layer])
         piece = links.move_start(packed[layer][at])
-        ffn_weights[layer].append(piece.reshape(width, -1))
+        ffn_weights[layer].append(piece)
 
     fetch(0)
     for layer in range(layers):
@@ -519,21 +554,22 @@
             fetch(layer + 1)
         inner, partial = [], []
         weights = ffn_weights[layer]
-        if len(weights) == 3:
-            weights[:2] = [jnp.concatenate(weights[:2], axis=1)]
+        *inner_parts, down = weights
+        weights[:] = [jnp.concatenate(inner_parts, axis=1).reshape(width, 2 * units)]
+        weights.append(down.transpose(1, 0, 2).reshape(units, width))
         for rows in normed_mid:
             both = mm(rows, weights[0])
             gate, up = both[:, :units], both[:, units:]
             hidden = (jax.nn.silu(gate) * up).astype(BF)
             inner.append((gate, up, hidden))
-            partial.append(mm_nt(hidden, weights[1]))
+            partial.append(mm(hidden, weights[1]))
         if layer + 1 < layers:
             block_out = middle + links.reduce_rows(*partial)
             next_pairs = links.gather_half(held[1], True).reshape(width, -1)
             next_queries = links.gather_half(held[0], True).reshape(width, -1)
             attn_weights.append((next_queries, next_pairs))
         else:
-            last = (middle, (partial[0], partial[1].astype(BF)))
+            last = (middle, [half.astype(BF) for half in partial])
         stored.append(
             (
                 current,
@@ -551,13 +587,6 @@
         )
         if layer + 1 < layers:
             current = block_out
-
-    def finish_ffn(pieces, late):
-        parts = [
-            piece.transpose(1, 0, 2).reshape(shard, -1).astype(F32)
-            for piece in after(pieces, late)
-        ]
-        return parts[0], parts[1], parts[2].T
 
     def finish_attn(left, late):
         out_pieces, *projected = after(left, late)
@@ -592,7 +621,6 @@
             grad_all = top_gradient
         else:
             line = links.gather_line(grad_res.astype(BF))
-            moved[1] = links.move_start(held_grads[1])
             grad_all = links.gather_square(line)
             final_pieces = after(final_pieces, line)
             final_out = middle_last + links.reduce_end(final_pieces)
@@ -600,7 +628,7 @@
         partial, d_in, d_down = [], 0.0, 0.0
         weights = ffn_weights[layer]
         for rows, grad_rows, (gate, up, hidden) in zip(normed_mid, grad_all, inner):
-            grad_hidden = mm(grad_rows, weights[1])
+            grad_hidden = mm_nt(grad_rows, weights[1])
             sigmoid = jax.nn.sigmoid(gate)
             grad_up = (grad_hidden * gate * sigmoid).astype(BF)
             grad_gate = (
@@ -609,22 +637,18 @@
             both = jnp.concatenate([grad_gate, grad_up], axis=1)
             partial.append(mm_nt(both, weights[0]))
             d_in = d_in + mm_tn(rows, both)
-            d_down = d_down + mm_tn(grad_rows, hidden)
-        held_grads = [
-            grads.astype(BF).reshape(contexts, shard, units)
-            for grads in (d_in[:, :units], d_in[:, units:], d_down)
-        ]
-        last_moved, moved = moved, [None] * 3
+            d_down = d_down + mm_tn(hidden, grad_rows)
+        held_grads = d_in.astype(BF).reshape(contexts, shard, 2 * units)
+        down_grads = d_down.astype(BF).reshape(units, contexts, shard).transpose(1, 0, 2)
+        last_moved, moved = moved, [None] * 2
         pieces = links.reduce_start(*partial)
-        if layer == 0:
-            moved[2] = links.move_start(held_grads[2])
+        moved[1] = links.move_start(down_grads)
         grad_normed_mid = links.reduce_end(pieces)
         unused, norm_back = jax.vjp(rms_scale, middle, gain_mlp)
         grad_mid_part, d_mlp_gain = norm_back(grad_normed_mid)
         grad_mid = grad_res + grad_mid_part
         grad_mid_all = links.spread_rows(grad_mid.astype(BF))
-        at = 0 if layer == 0 else 2
-        moved[at] = links.move_start(held_grads[at])
+        moved[0] = links.move_start(held_grads)
         out_pieces = links.scatter_start(mm_tn(grad_mid_all, output_rows))
         attention_gradient = mm(grad_mid_all, out_weights[layer]).astype(BF)
         if layer + 1 == layers:
@@ -643,10 +667,6 @@
         pair_grads = [pair_grads[0]] + [
             links.swap(grad, mask) for grad, mask in zip(pair_grads[1:], masks[1:])
         ]
-        at = 1 if layer == 0 else 0
-        moved[at] = links.move_start(held_grads[at])
-        if layer == 0:
-            weight_grads[1] = (*weight_grads[1], *finish_ffn(last_moved, query_grad))
         grad_queries, d_query_gain = prep_heads_back(
             query_proj, query_heads, query_gains[layer], tables, [query_grad]
         )
@@ -668,7 +688,11 @@
             projected.append(links.scatter_start(mm_tn(normed_in, grads)))
         left = (out_pieces, *projected)
         if layer == 0:
-            weight_grads[0] = (*finish_attn(left, grad_res), *finish_ffn(moved, partial))
+            weight_grads[0] = finish_attn(left, grad_res)
+            every = after((moved, last_moved), partial)
+            d_gate, d_up = unpack([piece[0] for piece in every])
+            d_down = [piece[1].reshape(contexts * units, shard) for piece in every]
+            d_down = jnp.stack(d_down).astype(F32)
         gain_grads[layer] = (d_attn_gain, d_mlp_gain, d_query_gain[0], d_key_gain[0])
 
     wide = jnp.stack([g[0] for g in gain_grads] + [g[1] for g in gain_grads])
@@ -685,8 +709,9 @@
     wide = sums[: 2 * layers * shard].reshape(2, layers, shard)
     narrow = sums[2 * layers * shard :].reshape(2, layers, head_dim)
     stacked = []
-    for member in range(7):
+    for member in range(4):
         stacked.append(jnp.stack([grads[member] for grads in weight_grads]))
+    stacked.extend((d_gate, d_up, d_down))
     return (final_out, grad_res, *stacked, wide[0], wide[1], narrow[0], narrow[1])
 
 

time: 1020 us -> 982 us (0.963)
  local copies, waits for them, and re-layouts: 90.9 us -> 48.2 us
  waiting for transfers between devices: 505 us -> 536 us
  matrix products: 78.4 us -> 64.2 us
    ppermute x127, waiting for transfers between devices: 488 us -> 516 us  [swap(): return lax.ppermute(value, AXES, [(i, i ^ mask) for i in range(self.count)])]
    unnamed x330 -> x319, local copies, waits for them, and re-layouts: 38.9 us -> 14.4 us
    all_to_all x12 -> x10, starting transfers between devices: 57.8 us -> 49.9 us  [exchange_context(): return lax.all_to_all(chunks, CONTEXT, 0, 0)]
    pallas_call x32 -> x35, Pallas kernels: 22.8 us -> 26 us  [rows_call(): pl.pallas_call(kernel, out_shape=[jax.ShapeDtypeStruct(shape, kind) for s...]
  transfers between devices with their start and end apart: 143 -> 141, of which waited for: 78 -> 83; matrix products, arithmetic and copies ran while one was open for 18% -> 14% of each run, Pallas kernels for 2% -> 3%
where the time goes in v3:
time: 982 us; the launch traced here: 971 us
  waiting for transfers between devices  536 us (55%)
  starting transfers between devices  216 us (22%)
  matrix products  64.2 us (7%)
  other arithmetic  57.8 us (6%)
  local copies, waits for them, and re-layouts  48.2 us (5%)
  Pallas kernels  31.5 us (3%)
  between operations  17.3 us (2%)
    ppermute x127, waiting for transfers between devices, swap(): return lax.ppermute(value, AXES, [(i, i ^ mask) for i in range(self.count)])  516 us
    ppermute x127, starting transfers between devices, swap(): return lax.ppermute(value, AXES, [(i, i ^ mask) for i in range(self.count)])  162 us
    all_to_all x10, starting transfers between devices, exchange_context(): return lax.all_to_all(chunks, CONTEXT, 0, 0)  49.9 us
    pallas_call x35, Pallas kernels, rows_call(): pl.pallas_call(kernel, out_shape=[jax.ShapeDtypeStruct(shape, kind) for s...  26 us
    dot_general x13, matrix products, mm(): return jnp.dot(a, b, preferred_element_type=F32)  23.8 us
    dot_general x14, matrix products, mm_tn(): lax.dot_general(a, b, (((0,), (0,)), ((), ())), preferred_element_type=F32)  21.1 us
    all_to_all x10, waiting for transfers between devices, exchange_context(): return lax.all_to_all(chunks, CONTEXT, 0, 0)  19.6 us
  transfers between devices with their start and end apart: 141, of which 83 were waited for; matrix products, arithmetic and copies ran while one was open for 14% of the time, Pallas kernels for 3%

profile of v3, /device:TPU:0, one launch (start us, length us, event | category | flops | bytes accessed | tf_op | source)
XLA Modules:
  0.0 971.1 jit_solution(3198337726539216053)
XLA Ops:
  8.6 7.3 all-to-all-start
  30.6 18.0 %collective-permute-done.refs_1_ = bf16[32,2048]{1,0:T(8,128)(2,1)S(1)} collective-permute-done((bf16[32,2048]{1,0:T(8,128)(2,1)S(1)}, bf16[32,2048]{1,0:T(8,128)(2,1)S(1)}, u32[]{:S(2)}, u32[]{:S(2)}) %collective-permute-start) | collective-permute-done | bytes 131104 | tf_op jit(solution)/shard_map/ppermute | solution.py:311
  68.1 10.8 %collective-permute-done.5.refs_2_ = bf16[2,256,512]{2,1,0:T(8,128)(2,1)S(1)} collective-permute-done((bf16[2,256,512]{2,1,0:T(8,128)(2,1)S(1)}, bf16[2,256,512]{2,1,0:T(8,128)(2,1)S(1)}, u32[]{:S(2)}, u32[]{:S(2)}) %collective-permute-start.5) | collective-permute-done | bytes 524320 | tf_op jit(solution)/shard_map/ppermute | solution.py:311
  97.4 6.3 all-to-all-start.3
  105.6 7.9 collective-permute-done.15
  117.7 12.3 %collective-permute-done.16 = bf16[32,2048]{1,0:T(8,128)(2,1)S(1)} collective-permute-done((bf16[32,2048]{1,0:T(8,128)(2,1)S(1)}, bf16[32,2048]{1,0:T(8,128)(2,1)S(1)}, u32[]{:S(2)}, u32[]{:S(2)}) %collective-permute-start.16) | collective-permute-done | bytes 131104 | tf_op jit(solution)/shard_map/ppermute | solution.py:311
  139.1 16.4 %collective-permute-done.19.refs_3_ = bf16[32,2048]{1,0:T(8,128)(2,1)S(1)} collective-permute-done((bf16[32,2048]{1,0:T(8,128)(2,1)S(1)}, bf16[32,2048]{1,0:T(8,128)(2,1)S(1)}, u32[]{:S(2)}, u32[]{:S(2)}) %collective-permute-start.19) | collective-permute-done | bytes 131104 | tf_op jit(solution)/shard_map/ppermute | solution.py:311
  155.4 10.2 %collective-permute-done.18.refs_2_ = bf16[32,2048]{1,0:T(8,128)(2,1)S(1)} collective-permute-done((bf16[32,2048]{1,0:T(8,128)(2,1)S(1)}, bf16[32,2048]{1,0:T(8,128)(2,1)S(1)}, u32[]{:S(2)}, u32[]{:S(2)}) %collective-permute-start.18) | collective-permute-done | bytes 131104 | tf_op jit(solution)/shard_map/ppermute | solution.py:311
  169.3 12.2 %collective-permute-done.22.refs_3_ = bf16[128,2048]{1,0:T(8,128)(2,1)S(1)} collective-permute-done((bf16[128,2048]{1,0:T(8,128)(2,1)S(1)}, bf16[128,2048]{1,0:T(8,128)(2,1)S(1)}, u32[]{:S(2)}, u32[]{:S(2)}) %collective-permute-start.22) | collective-permute-done | bytes 524320 | tf_op jit(solution)/shard_map/ppermute | solution.py:311
  181.5 8.1 collective-permute-done.21.refs_2_
  190.3 5.2 all-to-all-start.2
  196.8 19.6 %all-to-all-done.2 = bf16[8,128,384]{2,1,0:T(8,128)(2,1)} async-done(((bf16[8,128,384]{2,1,0:T(8,128)(2,1)}), bf16[8,128,384]{2,1,0:T(8,128)(2,1)}, u32[]{:S(2)}, u32[]{:S(2)}) %all-to-all-start.2) | async-done | bytes 786464 | tf_op jit(solution)/shard_map/all_to_all | solution.py:345
  229.5 9.0 collective-permute-done.35
  243.0 4.6 convert_add_fusion.3
  253.2 14.8 %collective-permute-done.25 = bf16[128,2048]{1,0:T(8,128)(2,1)} collective-permute-done((bf16[128,2048]{1,0:T(8,128)(2,1)}, bf16[128,2048]{1,0:T(8,128)(2,1)}, u32[]{:S(2)}, u32[]{:S(2)}) %collective-permute-start.25) | collective-permute-done | bytes 524320 | tf_op jit(solution)/shard_map/ppermute | solution.py:311
  268.0 9.0 collective-permute-done.27
  277.0 15.9 %collective-permute-done.26 = bf16[128,2048]{1,0:T(8,128)(2,1)} collective-permute-done((bf16[128,2048]{1,0:T(8,128)(2,1)}, bf16[128,2048]{1,0:T(8,128)(2,1)}, u32[]{:S(2)}, u32[]{:S(2)}) %collective-permute-start.26) | collective-permute-done | bytes 524320 | tf_op jit(solution)/shard_map/ppermute | solution.py:311
  302.1 7.8 collective-permute-done.28
  315.3 6.8 collective-permute-done.31.refs_1_
  323.5 5.0 collective-permute-done.32.refs_1_
  354.5 4.8 all-to-all-start.5
  364.8 20.3 %collective-permute-done.42 = bf16[32,2048]{1,0:T(8,128)(2,1)S(1)} collective-permute-done((bf16[32,2048]{1,0:T(8,128)(2,1)S(1)}, bf16[32,2048]{1,0:T(8,128)(2,1)S(1)}, u32[]{:S(2)}, u32[]{:S(2)}) %collective-permute-start.42) | collective-permute-done | bytes 131104 | tf_op jit(solution)/shard_map/ppermute | solution.py:311
  403.2 4.8 all-to-all-start.4
  416.0 25.3 %collective-permute-done.52.refs_3_ = bf16[32,2048]{1,0:T(8,128)(2,1)S(1)} collective-permute-done((bf16[32,2048]{1,0:T(8,128)(2,1)S(1)}, bf16[32,2048]{1,0:T(8,128)(2,1)S(1)}, u32[]{:S(2)}, u32[]{:S(2)}) %collective-permute-start.52) | collective-permute-done | bytes 131104 | tf_op jit(solution)/shard_map/ppermute | solution.py:311
  441.2 13.5 %collective-permute-start.50 = (bf16[32,2048]{1,0:T(8,128)(2,1)S(1)}, bf16[32,2048]{1,0:T(8,128)(2,1)S(1)}, u32[]{:S(2)}, u32[]{:S(2)}) collective-permute-start(bf16[32,2048]{1,0:T(8,128)(2,1)S(1)} %convert_element_type.417.refs_0_), channel_id=1, source_target_pairs={{0,8},{1,9},{2,10},{3,11},{4,12},{5,13},{6,14},{7,15},{8,0},{9,1},... | collective-permute-start | bytes 393224 | tf_op jit(solution)/shard_map/ppermute | solution.py:311
  464.4 9.6 collective-permute-done.55.refs_3_
  474.0 9.8 %collective-permute-done.54.refs_2_ = bf16[128,2048]{1,0:T(8,128)(2,1)S(1)} collective-permute-done((bf16[128,2048]{1,0:T(8,128)(2,1)S(1)}, bf16[128,2048]{1,0:T(8,128)(2,1)S(1)}, u32[]{:S(2)}, u32[]{:S(2)}) %collective-permute-start.54) | collective-permute-done | bytes 524320 | tf_op jit(solution)/shard_map/ppermute | solution.py:311
  510.1 21.6 %collective-permute-done.58 = bf16[128,2048]{1,0:T(8,128)(2,1)S(1)} collective-permute-done((bf16[128,2048]{1,0:T(8,128)(2,1)S(1)}, bf16[128,2048]{1,0:T(8,128)(2,1)S(1)}, u32[]{:S(2)}, u32[]{:S(2)}) %collective-permute-start.58) | collective-permute-done | bytes 524320 | tf_op jit(solution)/shard_map/ppermute | solution.py:311
  549.6 7.9 collective-permute-done.64.refs_1_
  559.0 6.3 collective-permute-done.65.refs_1_
  608.0 13.0 %collective-permute-done.76 = bf16[32,2048]{1,0:T(8,128)(2,1)S(1)} collective-permute-done((bf16[32,2048]{1,0:T(8,128)(2,1)S(1)}, bf16[32,2048]{1,0:T(8,128)(2,1)S(1)}, u32[]{:S(2)}, u32[]{:S(2)}) %collective-permute-start.76) | collective-permute-done | bytes 131104 | tf_op jit(solution)/shard_map/ppermute | solution.py:311
  642.3 5.1 collective-permute-done.118
  667.7 4.7 collective-permute-done.121
  672.4 6.4 collective-permute-done.85.refs_3_
  678.8 9.5 collective-permute-done.84.refs_2_
  692.2 11.6 %collective-permute-done.122 = bf16[256,256]{1,0:T(8,128)(2,1)S(1)} collective-permute-done((bf16[256,256]{1,0:T(8,128)(2,1)S(1)}, bf16[256,256]{1,0:T(8,128)(2,1)S(1)}, u32[]{:S(2)}, u32[]{:S(2)}) %collective-permute-start.122) | collective-permute-done | bytes 131104 | tf_op jit(solution)/shard_map/ppermute | solution.py:311
  703.9 5.5 collective-permute-done.126
  741.2 11.4 %collective-permute-done.88 = bf16[128,2048]{1,0:T(8,128)(2,1)S(1)} collective-permute-done((bf16[128,2048]{1,0:T(8,128)(2,1)S(1)}, bf16[128,2048]{1,0:T(8,128)(2,1)S(1)}, u32[]{:S(2)}, u32[]{:S(2)}) %collective-permute-start.88) | collective-permute-done | bytes 524320 | tf_op jit(solution)/shard_map/ppermute | solution.py:311
  752.6 11.2 %collective-permute-done.90 = bf16[128,2048]{1,0:T(8,128)(2,1)S(1)} collective-permute-done((bf16[128,2048]{1,0:T(8,128)(2,1)S(1)}, bf16[128,2048]{1,0:T(8,128)(2,1)S(1)}, u32[]{:S(2)}, u32[]{:S(2)}) %collective-permute-start.90) | collective-permute-done | bytes 524320 | tf_op jit(solution)/shard_map/ppermute | solution.py:311
  763.8 10.5 %collective-permute-done.89 = bf16[128,2048]{1,0:T(8,128)(2,1)S(1)} collective-permute-done((bf16[128,2048]{1,0:T(8,128)(2,1)S(1)}, bf16[128,2048]{1,0:T(8,128)(2,1)S(1)}, u32[]{:S(2)}, u32[]{:S(2)}) %collective-permute-start.89) | collective-permute-done | bytes 524320 | tf_op jit(solution)/shard_map/ppermute | solution.py:311
  802.9 19.1 %collective-permute-done.94.refs_1_ = bf16[32,2048]{1,0:T(8,128)(2,1)S(1)} collective-permute-done((bf16[32,2048]{1,0:T(8,128)(2,1)S(1)}, bf16[32,2048]{1,0:T(8,128)(2,1)S(1)}, u32[]{:S(2)}, u32[]{:S(2)}) %collective-permute-start.94) | collective-permute-done | bytes 131104 | tf_op jit(solution)/shard_map/ppermute | solution.py:311
  825.9 4.7 all-to-all-start.6
  845.5 14.4 %collective-permute-done.80 = bf16[32,2048]{1,0:T(8,128)(2,1)S(1)} collective-permute-done((bf16[32,2048]{1,0:T(8,128)(2,1)S(1)}, bf16[32,2048]{1,0:T(8,128)(2,1)S(1)}, u32[]{:S(2)}, u32[]{:S(2)}) %collective-permute-start.80) | collective-permute-done | bytes 131104 | tf_op jit(solution)/shard_map/ppermute | solution.py:311
  866.9 11.0 %collective-permute-done.81 = bf16[32,2048]{1,0:T(8,128)(2,1)S(1)} collective-permute-done((bf16[32,2048]{1,0:T(8,128)(2,1)S(1)}, bf16[32,2048]{1,0:T(8,128)(2,1)S(1)}, u32[]{:S(2)}, u32[]{:S(2)}) %collective-permute-start.81) | collective-permute-done | bytes 131104 | tf_op jit(solution)/shard_map/ppermute | solution.py:311
  898.9 5.4 shard_map.284
  920.4 4.8 collective-permute-done.108
  929.9 6.0 collective-permute-done.111
  944.1 10.5 %collective-permute-done.123 = bf16[256,256]{1,0:T(8,128)(2,1)S(1)} collective-permute-done((bf16[256,256]{1,0:T(8,128)(2,1)S(1)}, bf16[256,256]{1,0:T(8,128)(2,1)S(1)}, u32[]{:S(2)}, u32[]{:S(2)}) %collective-permute-start.123) | collective-permute-done | bytes 131104 | tf_op jit(solution)/shard_map/ppermute | solution.py:311
  (818 shorter events, 457.9 us)
Async XLA Ops:
  22.9 36.2 %collective-permute-start.10 = (bf16[256,256]{1,0:T(8,128)(2,1)}, bf16[256,256]{1,0:T(8,128)(2,1)}, u32[]{:S(2)}, u32[]{:S(2)}) collective-permute-start(bf16[256,256]{1,0:T(8,128)(2,1)} %split.335), channel_id=1, source_target_pairs={{0,16},{1,17},{2,18},{3,19},{4,20},{5,21},{6,22},{7,23},{8,24},{9,... | collective-permute-start | bytes 393224 | tf_op jit(solution)/shard_map/ppermute | solution.py:311
  25.8 25.7 %collective-permute-start.3 = (bf16[256,512]{1,0:T(8,128)(2,1)S(1)}, bf16[256,512]{1,0:T(8,128)(2,1)S(1)}, u32[]{:S(2)}, u32[]{:S(2)}) collective-permute-start(bf16[256,512]{1,0:T(8,128)(2,1)S(1)} %split.333), channel_id=1, source_target_pairs={{0,16},{1,17},{2,18},{3,19},{4,20},{5,21},{6,22},{7,23},{8,24},{9,... | collective-permute-start | bytes 786440 | tf_op jit(solution)/shard_map/ppermute | solution.py:311
  53.3 25.6 %collective-permute-start.5 = (bf16[2,256,512]{2,1,0:T(8,128)(2,1)S(1)}, bf16[2,256,512]{2,1,0:T(8,128)(2,1)S(1)}, u32[]{:S(2)}, u32[]{:S(2)}) collective-permute-start(bf16[2,256,512]{2,1,0:T(8,128)(2,1)S(1)} %bitcast.269), channel_id=1, source_target_pairs={{0,8},{1,9},{2,10},{3,11},{4,12},{5,13},{6,14},{7,15},{8,0},{9,1},... | collective-permute-start | bytes 1572872 | tf_op jit(solution)/shard_map/ppermute | solution.py:311
  59.9 25.3 %collective-permute-start.13 = (bf16[2,256,256]{2,1,0:T(8,128)(2,1)S(1)}, bf16[2,256,256]{2,1,0:T(8,128)(2,1)S(1)}, u32[]{:S(2)}, u32[]{:S(2)}) collective-permute-start(bf16[2,256,256]{2,1,0:T(8,128)(2,1)S(1)} %bitcast.272), channel_id=1, source_target_pairs={{0,12},{1,13},{2,14},{3,15},{4,8},{5,9},{6,10},{7,11},{8,4},{9,5},... | collective-permute-start | bytes 786440 | tf_op jit(solution)/shard_map/ppermute | solution.py:311
  97.4 32.9 %all-to-all-start.3 = ((bf16[8,192,256]{2,1,0:T(8,128)(2,1)}), bf16[8,192,256]{2,1,0:T(8,128)(2,1)S(1)}, u32[]{:S(2)}, u32[]{:S(2)}) async-start(bf16[8,192,256]{2,1,0:T(8,128)(2,1)} %bitcast.305), calls=%async_computation.3 | async-start | bytes 1572864 | tf_op jit(solution)/shard_map/all_to_all | solution.py:345
  130.3 60.0 %all-to-all-start.1 = ((bf16[8,128,384]{2,1,0:T(8,128)(2,1)}), bf16[8,128,384]{2,1,0:T(8,128)(2,1)}, u32[]{:S(2)}, u32[]{:S(2)}) async-start(bf16[8,128,384]{2,1,0:T(8,128)(2,1)} %get-tuple-element.99), calls=%async_computation.1 | async-start | bytes 1572864 | tf_op jit(solution)/shard_map/all_to_all | solution.py:345
  138.4 27.3 %collective-permute-start.18 = (bf16[32,2048]{1,0:T(8,128)(2,1)S(1)}, bf16[32,2048]{1,0:T(8,128)(2,1)S(1)}, u32[]{:S(2)}, u32[]{:S(2)}) collective-permute-start(bf16[32,2048]{1,0:T(8,128)(2,1)S(1)} %multiply_convert_fusion.14.refs_0_), channel_id=1, source_target_pairs={{0,16},{1,17},{2,18},{3,19},{4,20},{5,21},{6,22},{7,23},{8,24},{9,... | collective-permute-start | bytes 393224 | tf_op jit(solution)/shard_map/ppermute | solution.py:311
  138.4 27.3 %collective-permute-start.17 = (bf16[32,2048]{1,0:T(8,128)(2,1)S(1)}, bf16[32,2048]{1,0:T(8,128)(2,1)S(1)}, u32[]{:S(2)}, u32[]{:S(2)}) collective-permute-start(bf16[32,2048]{1,0:T(8,128)(2,1)S(1)} %multiply_convert_fusion.14.refs_0_), channel_id=1, source_target_pairs={{0,8},{1,9},{2,10},{3,11},{4,12},{5,13},{6,14},{7,15},{8,0},{9,1},... | collective-permute-start | bytes 393224 | tf_op jit(solution)/shard_map/ppermute | solution.py:311
  190.2 27.7 %collective-permute-start.23 = (bf16[512,2048]{1,0:T(8,128)(2,1)S(1)}, bf16[512,2048]{1,0:T(8,128)(2,1)}, u32[]{:S(2)}, u32[]{:S(2)}) collective-permute-start(bf16[512,2048]{1,0:T(8,128)(2,1)S(1)} %shard_map.248), channel_id=1, source_target_pairs={{0,1},{1,0},{2,3},{3,2},{4,5},{5,4},{6,7},{7,6},{8,9},{9,8},{10,11... | collective-permute-start | bytes 6291464 | tf_op jit(solution)/shard_map/ppermute | solution.py:311
  190.3 26.1 %all-to-all-start.2 = ((bf16[8,128,384]{2,1,0:T(8,128)(2,1)}), bf16[8,128,384]{2,1,0:T(8,128)(2,1)}, u32[]{:S(2)}, u32[]{:S(2)}) async-start(bf16[8,128,384]{2,1,0:T(8,128)(2,1)} %get-tuple-element.100), calls=%async_computation.2 | async-start | bytes 1572864 | tf_op jit(solution)/shard_map/all_to_all | solution.py:345
  195.5 135.1 %all-gather.6.cloned.1.call-start = ((), (), s32[]{:S(2)}) async-start(), calls=%async_computation.12 | async-start | bytes 1310720 | tf_op jit(solution)/shard_map/all_gather | solution.py:409
  226.5 25.7 %collective-permute-start.34 = (bf16[256,256]{1,0:T(8,128)(2,1)}, bf16[256,256]{1,0:T(8,128)(2,1)S(1)}, u32[]{:S(2)}, u32[]{:S(2)}) collective-permute-start(bf16[256,256]{1,0:T(8,128)(2,1)} %get-tuple-element.359), channel_id=1, source_target_pairs={{0,16},{1,17},{2,18},{3,19},{4,20},{5,21},{6,22},{7,23},{8,24},{9,... | collective-permute-start | bytes 393224 | tf_op jit(solution)/shard_map/ppermute | solution.py:311
  239.3 98.1 %all-gather.4.cloned.1.call-start = ((), (), s32[]{:S(2)}) async-start(), calls=%async_computation.11 | async-start | bytes 1310720 | tf_op jit(solution)/shard_map/all_gather | solution.py:409
  249.3 27.6 %collective-permute-start.27 = (bf16[128,2048]{1,0:T(8,128)(2,1)}, bf16[128,2048]{1,0:T(8,128)(2,1)}, u32[]{:S(2)}, u32[]{:S(2)}) collective-permute-start(bf16[128,2048]{1,0:T(8,128)(2,1)} %get-tuple-element.309), channel_id=1, source_target_pairs={{0,6},{1,7},{2,4},{3,5},{4,2},{5,3},{6,0},{7,1},{8,14},{9,15},{10,... | collective-permute-start | bytes 1572872 | tf_op jit(solution)/shard_map/ppermute | solution.py:311
  250.9 41.9 %collective-permute-start.26 = (bf16[128,2048]{1,0:T(8,128)(2,1)}, bf16[128,2048]{1,0:T(8,128)(2,1)}, u32[]{:S(2)}, u32[]{:S(2)}) collective-permute-start(bf16[128,2048]{1,0:T(8,128)(2,1)} %get-tuple-element.310), channel_id=1, source_target_pairs={{0,4},{1,5},{2,6},{3,7},{4,0},{5,1},{6,2},{7,3},{8,12},{9,13},{10,... | collective-permute-start | bytes 1572872 | tf_op jit(solution)/shard_map/ppermute | solution.py:311
  253.0 94.4 %all-gather.8.cloned.1.call-start = ((), (), s32[]{:S(2)}) async-start(), calls=%async_computation.13 | async-start | bytes 1310720 | tf_op jit(solution)/shard_map/all_gather | solution.py:409
  253.1 48.3 %collective-permute-start.39 = (bf16[256,256]{1,0:T(8,128)(2,1)}, bf16[256,256]{1,0:T(8,128)(2,1)S(1)}, u32[]{:S(2)}, u32[]{:S(2)}) collective-permute-start(bf16[256,256]{1,0:T(8,128)(2,1)} %get-tuple-element.357), channel_id=1, source_target_pairs={{0,16},{1,17},{2,18},{3,19},{4,20},{5,21},{6,22},{7,23},{8,24},{9,... | collective-permute-start | bytes 393224 | tf_op jit(solution)/shard_map/ppermute | solution.py:311
  354.5 48.7 %all-to-all-start.5 = ((bf16[8,192,256]{2,1,0:T(8,128)(2,1)}), bf16[8,192,256]{2,1,0:T(8,128)(2,1)}, u32[]{:S(2)}, u32[]{:S(2)}) async-start(bf16[8,192,256]{2,1,0:T(8,128)(2,1)} %bitcast.304), calls=%async_computation.5 | async-start | bytes 1572864 | tf_op jit(solution)/shard_map/all_to_all | solution.py:345
  400.2 61.3 %collective-permute-start.48 = (bf16[128,2048]{1,0:T(8,128)(2,1)}, bf16[128,2048]{1,0:T(8,128)(2,1)}, u32[]{:S(2)}, u32[]{:S(2)}) collective-permute-start(bf16[128,2048]{1,0:T(8,128)(2,1)} %shard_map.259.refs_0_), channel_id=1, source_target_pairs={{0,6},{1,7},{2,4},{3,5},{4,2},{5,3},{6,0},{7,1},{8,14},{9,15},{10,... | collective-permute-start | bytes 1572872 | tf_op jit(solution)/shard_map/ppermute | solution.py:311
  403.2 84.4 %all-to-all-start.4 = ((bf16[8,256,384]{2,1,0:T(8,128)(2,1)}), bf16[8,256,384]{2,1,0:T(8,128)(2,1)}, u32[]{:S(2)}, u32[]{:S(2)}) async-start(bf16[8,256,384]{2,1,0:T(8,128)(2,1)} %copy-done.14), calls=%async_computation.4 | async-start | bytes 3145728 | tf_op jit(solution)/shard_map/all_to_all | solution.py:345
  407.9 53.8 %collective-permute-start.47 = (bf16[128,2048]{1,0:T(8,128)(2,1)}, bf16[128,2048]{1,0:T(8,128)(2,1)S(1)}, u32[]{:S(2)}, u32[]{:S(2)}) collective-permute-start(bf16[128,2048]{1,0:T(8,128)(2,1)} %shard_map.259.refs_0_), channel_id=1, source_target_pairs={{0,4},{1,5},{2,6},{3,7},{4,0},{5,1},{6,2},{7,3},{8,12},{9,13},{10,... | collective-permute-start | bytes 1572872 | tf_op jit(solution)/shard_map/ppermute | solution.py:311
  409.9 51.9 %collective-permute-start.46 = (bf16[128,2048]{1,0:T(8,128)(2,1)}, bf16[128,2048]{1,0:T(8,128)(2,1)S(1)}, u32[]{:S(2)}, u32[]{:S(2)}) collective-permute-start(bf16[128,2048]{1,0:T(8,128)(2,1)} %shard_map.259.refs_0_), channel_id=1, source_target_pairs={{0,2},{1,3},{2,0},{3,1},{4,6},{5,7},{6,4},{7,5},{8,10},{9,11},{10,... | collective-permute-start | bytes 1572872 | tf_op jit(solution)/shard_map/ppermute | solution.py:311
  412.6 28.6 %collective-permute-start.52 = (bf16[32,2048]{1,0:T(8,128)(2,1)S(1)}, bf16[32,2048]{1,0:T(8,128)(2,1)S(1)}, u32[]{:S(2)}, u32[]{:S(2)}) collective-permute-start(bf16[32,2048]{1,0:T(8,128)(2,1)S(1)} %convert_element_type.417.refs_0_), channel_id=1, source_target_pairs={{0,24},{1,25},{2,26},{3,27},{4,28},{5,29},{6,30},{7,31},{8,16},{9,... | collective-permute-start | bytes 393224 | tf_op jit(solution)/shard_map/ppermute | solution.py:311
  416.0 39.9 %collective-permute-start.51 = (bf16[32,2048]{1,0:T(8,128)(2,1)S(1)}, bf16[32,2048]{1,0:T(8,128)(2,1)S(1)}, u32[]{:S(2)}, u32[]{:S(2)}) collective-permute-start(bf16[32,2048]{1,0:T(8,128)(2,1)S(1)} %convert_element_type.417.refs_0_), channel_id=1, source_target_pairs={{0,16},{1,17},{2,18},{3,19},{4,20},{5,21},{6,22},{7,23},{8,24},{9,... | collective-permute-start | bytes 393224 | tf_op jit(solution)/shard_map/ppermute | solution.py:311
  506.6 25.1 %collective-permute-start.58 = (bf16[128,2048]{1,0:T(8,128)(2,1)S(1)}, bf16[128,2048]{1,0:T(8,128)(2,1)S(1)}, u32[]{:S(2)}, u32[]{:S(2)}) collective-permute-start(bf16[128,2048]{1,0:T(8,128)(2,1)S(1)} %get-tuple-element.305), channel_id=1, source_target_pairs={{0,2},{1,3},{2,0},{3,1},{4,6},{5,7},{6,4},{7,5},{8,10},{9,11},{10,... | collective-permute-start | bytes 1572872 | tf_op jit(solution)/shard_map/ppermute | solution.py:311
  590.2 136.8 %all-to-all-start.9 = ((bf16[8,192,256]{2,1,0:T(8,128)(2,1)}), bf16[8,192,256]{2,1,0:T(8,128)(2,1)}, u32[]{:S(2)}, u32[]{:S(2)}) async-start(bf16[8,192,256]{2,1,0:T(8,128)(2,1)} %bitcast.302), calls=%async_computation.9 | async-start | bytes 1572864 | tf_op jit(solution)/shard_map/all_to_all | solution.py:345
  647.4 31.4 %collective-permute-start.85 = (bf16[128,2048]{1,0:T(8,128)(2,1)S(1)}, bf16[128,2048]{1,0:T(8,128)(2,1)S(1)}, u32[]{:S(2)}, u32[]{:S(2)}) collective-permute-start(bf16[128,2048]{1,0:T(8,128)(2,1)S(1)} %shard_map.270.refs_0_), channel_id=1, source_target_pairs={{0,6},{1,7},{2,4},{3,5},{4,2},{5,3},{6,0},{7,1},{8,14},{9,15},{10,... | collective-permute-start | bytes 1572872 | tf_op jit(solution)/shard_map/ppermute | solution.py:311
  649.9 38.4 %collective-permute-start.84 = (bf16[128,2048]{1,0:T(8,128)(2,1)S(1)}, bf16[128,2048]{1,0:T(8,128)(2,1)S(1)}, u32[]{:S(2)}, u32[]{:S(2)}) collective-permute-start(bf16[128,2048]{1,0:T(8,128)(2,1)S(1)} %shard_map.270.refs_0_), channel_id=1, source_target_pairs={{0,4},{1,5},{2,6},{3,7},{4,0},{5,1},{6,2},{7,3},{8,12},{9,13},{10,... | collective-permute-start | bytes 1572872 | tf_op jit(solution)/shard_map/ppermute | solution.py:311
  652.2 36.2 %collective-permute-start.83 = (bf16[128,2048]{1,0:T(8,128)(2,1)S(1)}, bf16[128,2048]{1,0:T(8,128)(2,1)S(1)}, u32[]{:S(2)}, u32[]{:S(2)}) collective-permute-start(bf16[128,2048]{1,0:T(8,128)(2,1)S(1)} %shard_map.270.refs_0_), channel_id=1, source_target_pairs={{0,2},{1,3},{2,0},{3,1},{4,6},{5,7},{6,4},{7,5},{8,10},{9,11},{10,... | collective-permute-start | bytes 1572872 | tf_op jit(solution)/shard_map/ppermute | solution.py:311
  667.7 51.2 %collective-permute-start.67 = (bf16[512,2048]{1,0:T(8,128)(2,1)}, bf16[512,2048]{1,0:T(8,128)(2,1)S(1)}, u32[]{:S(2)}, u32[]{:S(2)}) collective-permute-start(bf16[512,2048]{1,0:T(8,128)(2,1)} %convolution_convert_fusion), channel_id=1, source_target_pairs={{0,1},{1,0},{2,3},{3,2},{4,5},{5,4},{6,7},{7,6},{8,9},{9,8},{10,11... | collective-permute-start | bytes 6291464 | tf_op jit(solution)/shard_map/ppermute | solution.py:311
  727.0 65.1 %all-to-all-start.8 = ((bf16[8,256,384]{2,1,0:T(8,128)(2,1)}), bf16[8,256,384]{2,1,0:T(8,128)(2,1)}, u32[]{:S(2)}, u32[]{:S(2)}) async-start(bf16[8,256,384]{2,1,0:T(8,128)(2,1)} %bitcast.284), calls=%async_computation.8 | async-start | bytes 3145728 | tf_op jit(solution)/shard_map/all_to_all | solution.py:345
  734.4 29.4 %collective-permute-start.90 = (bf16[128,2048]{1,0:T(8,128)(2,1)S(1)}, bf16[128,2048]{1,0:T(8,128)(2,1)S(1)}, u32[]{:S(2)}, u32[]{:S(2)}) collective-permute-start(bf16[128,2048]{1,0:T(8,128)(2,1)S(1)} %get-tuple-element.300), channel_id=1, source_target_pairs={{0,6},{1,7},{2,4},{3,5},{4,2},{5,3},{6,0},{7,1},{8,14},{9,15},{10,... | collective-permute-start | bytes 1572872 | tf_op jit(solution)/shard_map/ppermute | solution.py:311
  736.4 37.9 %collective-permute-start.89 = (bf16[128,2048]{1,0:T(8,128)(2,1)S(1)}, bf16[128,2048]{1,0:T(8,128)(2,1)S(1)}, u32[]{:S(2)}, u32[]{:S(2)}) collective-permute-start(bf16[128,2048]{1,0:T(8,128)(2,1)S(1)} %get-tuple-element.301), channel_id=1, source_target_pairs={{0,4},{1,5},{2,6},{3,7},{4,0},{5,1},{6,2},{7,3},{8,12},{9,13},{10,... | collective-permute-start | bytes 1572872 | tf_op jit(solution)/shard_map/ppermute | solution.py:311
  737.8 94.9 %collective-permute-start.70 = (bf16[128,2048]{1,0:T(8,128)(2,1)}, bf16[128,2048]{1,0:T(8,128)(2,1)}, u32[]{:S(2)}, u32[]{:S(2)}) collective-permute-start(bf16[128,2048]{1,0:T(8,128)(2,1)} %get-tuple-element.302), channel_id=1, source_target_pairs={{0,6},{1,7},{2,4},{3,5},{4,2},{5,3},{6,0},{7,1},{8,14},{9,15},{10,... | collective-permute-start | bytes 1572872 | tf_op jit(solution)/shard_map/ppermute | solution.py:311
  740.4 92.3 %collective-permute-start.69 = (bf16[128,2048]{1,0:T(8,128)(2,1)}, bf16[128,2048]{1,0:T(8,128)(2,1)}, u32[]{:S(2)}, u32[]{:S(2)}) collective-permute-start(bf16[128,2048]{1,0:T(8,128)(2,1)} %get-tuple-element.303), channel_id=1, source_target_pairs={{0,4},{1,5},{2,6},{3,7},{4,0},{5,1},{6,2},{7,3},{8,12},{9,13},{10,... | collective-permute-start | bytes 1572872 | tf_op jit(solution)/shard_map/ppermute | solution.py:311
  781.6 51.1 %collective-permute-start.68 = (bf16[128,2048]{1,0:T(8,128)(2,1)}, bf16[128,2048]{1,0:T(8,128)(2,1)}, u32[]{:S(2)}, u32[]{:S(2)}) collective-permute-start(bf16[128,2048]{1,0:T(8,128)(2,1)} %get-tuple-element.304), channel_id=1, source_target_pairs={{0,2},{1,3},{2,0},{3,1},{4,6},{5,7},{6,4},{7,5},{8,10},{9,11},{10,... | collective-permute-start | bytes 1572872 | tf_op jit(solution)/shard_map/ppermute | solution.py:311
  792.1 33.8 %all-to-all-start.7 = ((bf16[8,192,256]{2,1,0:T(8,128)(2,1)}), bf16[8,192,256]{2,1,0:T(8,128)(2,1)}, u32[]{:S(2)}, u32[]{:S(2)}) async-start(bf16[8,192,256]{2,1,0:T(8,128)(2,1)} %bitcast.257), calls=%async_computation.7 | async-start | bytes 1572864 | tf_op jit(solution)/shard_map/all_to_all | solution.py:345
  825.9 62.8 %all-to-all-start.6 = ((bf16[8,256,384]{2,1,0:T(8,128)(2,1)}), bf16[8,256,384]{2,1,0:T(8,128)(2,1)}, u32[]{:S(2)}, u32[]{:S(2)}) async-start(bf16[8,256,384]{2,1,0:T(8,128)(2,1)} %bitcast.285), calls=%async_computation.6 | async-start | bytes 3145728 | tf_op jit(solution)/shard_map/all_to_all | solution.py:345
  834.6 25.3 %collective-permute-start.80 = (bf16[32,2048]{1,0:T(8,128)(2,1)S(1)}, bf16[32,2048]{1,0:T(8,128)(2,1)S(1)}, u32[]{:S(2)}, u32[]{:S(2)}) collective-permute-start(bf16[32,2048]{1,0:T(8,128)(2,1)S(1)} %get-tuple-element.330), channel_id=1, source_target_pairs={{0,8},{1,9},{2,10},{3,11},{4,12},{5,13},{6,14},{7,15},{8,0},{9,1},... | collective-permute-start | bytes 393224 | tf_op jit(solution)/shard_map/ppermute | solution.py:311
  836.6 30.3 %collective-permute-start.82 = (bf16[32,2048]{1,0:T(8,128)(2,1)S(1)}, bf16[32,2048]{1,0:T(8,128)(2,1)S(1)}, u32[]{:S(2)}, u32[]{:S(2)}) collective-permute-start(bf16[32,2048]{1,0:T(8,128)(2,1)S(1)} %get-tuple-element.331), channel_id=1, source_target_pairs={{0,24},{1,25},{2,26},{3,27},{4,28},{5,29},{6,30},{7,31},{8,16},{9,... | collective-permute-start | bytes 393224 | tf_op jit(solution)/shard_map/ppermute | solution.py:311
  839.0 39.0 %collective-permute-start.81 = (bf16[32,2048]{1,0:T(8,128)(2,1)S(1)}, bf16[32,2048]{1,0:T(8,128)(2,1)S(1)}, u32[]{:S(2)}, u32[]{:S(2)}) collective-permute-start(bf16[32,2048]{1,0:T(8,128)(2,1)S(1)} %get-tuple-element.332), channel_id=1, source_target_pairs={{0,16},{1,17},{2,18},{3,19},{4,20},{5,21},{6,22},{7,23},{8,24},{9,... | collective-permute-start | bytes 393224 | tf_op jit(solution)/shard_map/ppermute | solution.py:311
  842.4 36.7 %collective-permute-start.97 = (bf16[256,256]{1,0:T(8,128)(2,1)S(1)}, bf16[256,256]{1,0:T(8,128)(2,1)S(1)}, u32[]{:S(2)}, u32[]{:S(2)}) collective-permute-start(bf16[256,256]{1,0:T(8,128)(2,1)S(1)} %get-tuple-element.121), channel_id=1, source_target_pairs={{0,4},{1,5},{2,6},{3,7},{4,0},{5,1},{6,2},{7,3},{8,12},{9,13},{10,... | collective-permute-start | bytes 393224 | tf_op jit(solution)/shard_map/ppermute | solution.py:311
  844.0 35.2 %collective-permute-start.98 = (bf16[256,256]{1,0:T(8,128)(2,1)S(1)}, bf16[256,256]{1,0:T(8,128)(2,1)S(1)}, u32[]{:S(2)}, u32[]{:S(2)}) collective-permute-start(bf16[256,256]{1,0:T(8,128)(2,1)S(1)} %get-tuple-element.122), channel_id=1, source_target_pairs={{0,8},{1,9},{2,10},{3,11},{4,12},{5,13},{6,14},{7,15},{8,0},{9,1},... | collective-permute-start | bytes 393224 | tf_op jit(solution)/shard_map/ppermute | solution.py:311
  882.6 29.7 %collective-permute-start.103 = (bf16[2,256,256]{2,1,0:T(8,128)(2,1)}, bf16[2,256,256]{2,1,0:T(8,128)(2,1)}, u32[]{:S(2)}, u32[]{:S(2)}) collective-permute-start(bf16[2,256,256]{2,1,0:T(8,128)(2,1)} %get-tuple-element.126), channel_id=1, source_target_pairs={{0,4},{1,5},{2,6},{3,7},{4,0},{5,1},{6,2},{7,3},{8,12},{9,13},{10,... | collective-permute-start | bytes 786440 | tf_op jit(solution)/shard_map/ppermute | solution.py:311
  883.9 31.0 %collective-permute-start.104 = (bf16[2,256,256]{2,1,0:T(8,128)(2,1)}, bf16[2,256,256]{2,1,0:T(8,128)(2,1)}, u32[]{:S(2)}, u32[]{:S(2)}) collective-permute-start(bf16[2,256,256]{2,1,0:T(8,128)(2,1)} %get-tuple-element.127), channel_id=1, source_target_pairs={{0,8},{1,9},{2,10},{3,11},{4,12},{5,13},{6,14},{7,15},{8,0},{9,1},... | collective-permute-start | bytes 786440 | tf_op jit(solution)/shard_map/ppermute | solution.py:311
  883.9 31.6 %collective-permute-start.105 = (bf16[2,256,256]{2,1,0:T(8,128)(2,1)S(1)}, bf16[2,256,256]{2,1,0:T(8,128)(2,1)}, u32[]{:S(2)}, u32[]{:S(2)}) collective-permute-start(bf16[2,256,256]{2,1,0:T(8,128)(2,1)S(1)} %get-tuple-element.128), channel_id=1, source_target_pairs={{0,12},{1,13},{2,14},{3,15},{4,8},{5,9},{6,10},{7,11},{8,4},{9,5},... | collective-permute-start | bytes 786440 | tf_op jit(solution)/shard_map/ppermute | solution.py:311
  887.4 28.5 %collective-permute-start.106 = (bf16[2,256,256]{2,1,0:T(8,128)(2,1)}, bf16[2,256,256]{2,1,0:T(8,128)(2,1)}, u32[]{:S(2)}, u32[]{:S(2)}) collective-permute-start(bf16[2,256,256]{2,1,0:T(8,128)(2,1)} %get-tuple-element.130), channel_id=1, source_target_pairs={{0,4},{1,5},{2,6},{3,7},{4,0},{5,1},{6,2},{7,3},{8,12},{9,13},{10,... | collective-permute-start | bytes 786440 | tf_op jit(solution)/shard_map/ppermute | solution.py:311
  909.0 52.4 %all-to-all-start.10 = ((f32[32,1,1536]{2,1,0:T(1,128)}), f32[32,1,1536]{2,1,0:T(1,128)}, u32[]{:S(2)}, u32[]{:S(2)}) async-start(f32[32,1,1536]{2,1,0:T(1,128)} %all_to_all.46), calls=%async_computation.10 | async-start | bytes 393216 | tf_op jit(solution)/shard_map/all_to_all | solution.py:708
  (251 other events, 3169.9 us)
Sparse Core Ops, SparseCore 0:
  239.4 31.1 all-gather.5
  272.7 31.2 all-gather.3
  306.1 31.2 all-gather.7

commit v4 on v3

--- a/solution.py
+++ b/solution.py
@@ -589,7 +589,7 @@
             current = block_out
 
     def finish_attn(left, late):
-        out_pieces, *projected = after(left, late)
+        (out_pieces,), projected = after(left[:1], late[0]), after(left[1:], late[1])
         d_out = jnp.concatenate(links.scatter_end(out_pieces), axis=1).T
         shards = [links.scatter_end(pieces) for pieces in projected]
         halves = [jnp.concatenate(pair, axis=1) for pair in zip(*shards)]
@@ -624,7 +624,7 @@
             grad_all = links.gather_square(line)
             final_pieces = after(final_pieces, line)
             final_out = middle_last + links.reduce_end(final_pieces)
-            weight_grads[layer + 1] = finish_attn(left, line)
+            weight_grads[layer + 1] = finish_attn(left, (line, line))
         partial, d_in, d_down = [], 0.0, 0.0
         weights = ffn_weights[layer]
         for rows, grad_rows, (gate, up, hidden) in zip(normed_mid, grad_all, inner):
@@ -688,7 +688,7 @@
             projected.append(links.scatter_start(mm_tn(normed_in, grads)))
         left = (out_pieces, *projected)
         if layer == 0:
-            weight_grads[0] = finish_attn(left, grad_res)
+            weight_grads[0] = finish_attn(left, (partial, grad_res))
             every = after((moved, last_moved), partial)
             d_gate, d_up = unpack([piece[0] for piece in every])
             d_down = [piece[1].reshape(contexts * units, shard) for piece in every]

time: 982 us -> 1000 us (1.018)
  starting transfers between devices: 216 us -> 229 us
  waiting for transfers between devices: 536 us -> 525 us
    ppermute x127, waiting for transfers between devices: 516 us -> 505 us  [swap(): return lax.ppermute(value, AXES, [(i, i ^ mask) for i in range(self.count)])]
    ppermute x127, starting transfers between devices: 162 us -> 173 us  [swap(): return lax.ppermute(value, AXES, [(i, i ^ mask) for i in range(self.count)])]
    unnamed x319 -> x297, local copies, waits for them, and re-layouts: 14.4 us -> 22.5 us
  transfers between devices with their start and end apart: 141 -> 141, of which waited for: 83 -> 76; matrix products, arithmetic and copies ran while one was open for 14% -> 15% of each run, Pallas kernels for 3% -> 3%
where the time goes in v4:
time: 1000 us; the launch traced here: 991 us
  waiting for transfers between devices  525 us (52%)
  starting transfers between devices  229 us (23%)
  matrix products  72.3 us (7%)
  other arithmetic  59.3 us (6%)
  local copies, waits for them, and re-layouts  55.3 us (6%)
  Pallas kernels  32.8 us (3%)
  between operations  17.1 us (2%)
    ppermute x127, waiting for transfers between devices, swap(): return lax.ppermute(value, AXES, [(i, i ^ mask) for i in range(self.count)])  505 us
    ppermute x127, starting transfers between devices, swap(): return lax.ppermute(value, AXES, [(i, i ^ mask) for i in range(self.count)])  173 us
    all_to_all x10, starting transfers between devices, exchange_context(): return lax.all_to_all(chunks, CONTEXT, 0, 0)  52.1 us
    pallas_call x35, Pallas kernels, rows_call(): pl.pallas_call(kernel, out_shape=[jax.ShapeDtypeStruct(shape, kind) for s...  27.9 us
    dot_general x14, matrix products, mm_tn(): lax.dot_general(a, b, (((0,), (0,)), ((), ())), preferred_element_type=F32)  26.7 us
    dot_general x13, matrix products, mm_nt(): lax.dot_general(a, b, (((1,), (1,)), ((), ())), preferred_element_type=F32)  23.2 us
    unnamed x297, local copies, waits for them, and re-layouts  22.5 us
    dot_general x13, matrix products, mm(): return jnp.dot(a, b, preferred_element_type=F32)  22.5 us
  transfers between devices with their start and end apart: 141, of which 76 were waited for; matrix products, arithmetic and copies ran while one was open for 15% of the time, Pallas kernels for 3%

profile of v4, /device:TPU:0, one launch (start us, length us, event | category | flops | bytes accessed | tf_op | source)
XLA Modules:
  0.0 991.3 jit_solution(16937318112024603943)
XLA Ops:
  8.6 7.3 all-to-all-start
  30.7 18.0 %collective-permute-done.refs_1_ = bf16[32,2048]{1,0:T(8,128)(2,1)S(1)} collective-permute-done((bf16[32,2048]{1,0:T(8,128)(2,1)S(1)}, bf16[32,2048]{1,0:T(8,128)(2,1)S(1)}, u32[]{:S(2)}, u32[]{:S(2)}) %collective-permute-start) | collective-permute-done | bytes 131104 | tf_op jit(solution)/shard_map/ppermute | solution.py:311
  68.1 10.8 %collective-permute-done.5.refs_2_ = bf16[2,256,512]{2,1,0:T(8,128)(2,1)S(1)} collective-permute-done((bf16[2,256,512]{2,1,0:T(8,128)(2,1)S(1)}, bf16[2,256,512]{2,1,0:T(8,128)(2,1)S(1)}, u32[]{:S(2)}, u32[]{:S(2)}) %collective-permute-start.5) | collective-permute-done | bytes 524320 | tf_op jit(solution)/shard_map/ppermute | solution.py:311
  97.5 6.3 all-to-all-start.3
  105.7 7.9 collective-permute-done.15
  117.8 12.3 %collective-permute-done.16 = bf16[32,2048]{1,0:T(8,128)(2,1)S(1)} collective-permute-done((bf16[32,2048]{1,0:T(8,128)(2,1)S(1)}, bf16[32,2048]{1,0:T(8,128)(2,1)S(1)}, u32[]{:S(2)}, u32[]{:S(2)}) %collective-permute-start.16) | collective-permute-done | bytes 131104 | tf_op jit(solution)/shard_map/ppermute | solution.py:311
  139.1 16.4 %collective-permute-done.19.refs_3_ = bf16[32,2048]{1,0:T(8,128)(2,1)S(1)} collective-permute-done((bf16[32,2048]{1,0:T(8,128)(2,1)S(1)}, bf16[32,2048]{1,0:T(8,128)(2,1)S(1)}, u32[]{:S(2)}, u32[]{:S(2)}) %collective-permute-start.19) | collective-permute-done | bytes 131104 | tf_op jit(solution)/shard_map/ppermute | solution.py:311
  155.5 10.2 %collective-permute-done.18.refs_2_ = bf16[32,2048]{1,0:T(8,128)(2,1)S(1)} collective-permute-done((bf16[32,2048]{1,0:T(8,128)(2,1)S(1)}, bf16[32,2048]{1,0:T(8,128)(2,1)S(1)}, u32[]{:S(2)}, u32[]{:S(2)}) %collective-permute-start.18) | collective-permute-done | bytes 131104 | tf_op jit(solution)/shard_map/ppermute | solution.py:311
  169.3 12.2 %collective-permute-done.22.refs_3_ = bf16[128,2048]{1,0:T(8,128)(2,1)S(1)} collective-permute-done((bf16[128,2048]{1,0:T(8,128)(2,1)S(1)}, bf16[128,2048]{1,0:T(8,128)(2,1)S(1)}, u32[]{:S(2)}, u32[]{:S(2)}) %collective-permute-start.22) | collective-permute-done | bytes 524320 | tf_op jit(solution)/shard_map/ppermute | solution.py:311
  181.6 8.1 collective-permute-done.21.refs_2_
  196.8 19.6 %all-to-all-done.2 = bf16[8,128,384]{2,1,0:T(8,128)(2,1)} async-done(((bf16[8,128,384]{2,1,0:T(8,128)(2,1)}), bf16[8,128,384]{2,1,0:T(8,128)(2,1)}, u32[]{:S(2)}, u32[]{:S(2)}) %all-to-all-start.2) | async-done | bytes 786464 | tf_op jit(solution)/shard_map/all_to_all | solution.py:345
  229.5 9.0 collective-permute-done.35
  253.2 14.8 %collective-permute-done.25 = bf16[128,2048]{1,0:T(8,128)(2,1)} collective-permute-done((bf16[128,2048]{1,0:T(8,128)(2,1)}, bf16[128,2048]{1,0:T(8,128)(2,1)}, u32[]{:S(2)}, u32[]{:S(2)}) %collective-permute-start.25) | collective-permute-done | bytes 524320 | tf_op jit(solution)/shard_map/ppermute | solution.py:311
  268.0 9.0 collective-permute-done.27
  277.0 15.9 %collective-permute-done.26 = bf16[128,2048]{1,0:T(8,128)(2,1)} collective-permute-done((bf16[128,2048]{1,0:T(8,128)(2,1)}, bf16[128,2048]{1,0:T(8,128)(2,1)}, u32[]{:S(2)}, u32[]{:S(2)}) %collective-permute-start.26) | collective-permute-done | bytes 524320 | tf_op jit(solution)/shard_map/ppermute | solution.py:311
  302.2 7.8 collective-permute-done.28
  315.4 6.8 collective-permute-done.31.refs_1_
  364.8 20.3 %collective-permute-done.42 = bf16[32,2048]{1,0:T(8,128)(2,1)S(1)} collective-permute-done((bf16[32,2048]{1,0:T(8,128)(2,1)S(1)}, bf16[32,2048]{1,0:T(8,128)(2,1)S(1)}, u32[]{:S(2)}, u32[]{:S(2)}) %collective-permute-start.42) | collective-permute-done | bytes 131104 | tf_op jit(solution)/shard_map/ppermute | solution.py:311
  416.0 25.3 %collective-permute-done.52.refs_3_ = bf16[32,2048]{1,0:T(8,128)(2,1)S(1)} collective-permute-done((bf16[32,2048]{1,0:T(8,128)(2,1)S(1)}, bf16[32,2048]{1,0:T(8,128)(2,1)S(1)}, u32[]{:S(2)}, u32[]{:S(2)}) %collective-permute-start.52) | collective-permute-done | bytes 131104 | tf_op jit(solution)/shard_map/ppermute | solution.py:311
  441.3 13.5 %collective-permute-start.50 = (bf16[32,2048]{1,0:T(8,128)(2,1)S(1)}, bf16[32,2048]{1,0:T(8,128)(2,1)S(1)}, u32[]{:S(2)}, u32[]{:S(2)}) collective-permute-start(bf16[32,2048]{1,0:T(8,128)(2,1)S(1)} %convert_element_type.417.refs_0_), channel_id=1, source_target_pairs={{0,8},{1,9},{2,10},{3,11},{4,12},{5,13},{6,14},{7,15},{8,0},{9,1},... | collective-permute-start | bytes 393224 | tf_op jit(solution)/shard_map/ppermute | solution.py:311
  464.5 9.6 collective-permute-done.55.refs_3_
  474.1 9.8 collective-permute-done.54.refs_2_
  510.2 21.6 %collective-permute-done.58 = bf16[128,2048]{1,0:T(8,128)(2,1)S(1)} collective-permute-done((bf16[128,2048]{1,0:T(8,128)(2,1)S(1)}, bf16[128,2048]{1,0:T(8,128)(2,1)S(1)}, u32[]{:S(2)}, u32[]{:S(2)}) %collective-permute-start.58) | collective-permute-done | bytes 524320 | tf_op jit(solution)/shard_map/ppermute | solution.py:311
  549.7 7.9 collective-permute-done.64.refs_1_
  559.1 6.3 collective-permute-done.65.refs_1_
  605.5 6.3 collective-permute-done.75
  655.0 11.5 %collective-permute-done.85.refs_3_ = bf16[128,2048]{1,0:T(8,128)(2,1)S(1)} collective-permute-done((bf16[128,2048]{1,0:T(8,128)(2,1)S(1)}, bf16[128,2048]{1,0:T(8,128)(2,1)S(1)}, u32[]{:S(2)}, u32[]{:S(2)}) %collective-permute-start.85) | collective-permute-done | bytes 524320 | tf_op jit(solution)/shard_map/ppermute | solution.py:311
  666.5 8.3 collective-permute-start.125
  674.8 6.7 collective-permute-done.84.refs_2_
  688.1 12.2 %collective-permute-done.118 = bf16[256,256]{1,0:T(8,128)(2,1)S(1)} collective-permute-done((bf16[256,256]{1,0:T(8,128)(2,1)S(1)}, bf16[256,256]{1,0:T(8,128)(2,1)S(1)}, u32[]{:S(2)}, u32[]{:S(2)}) %collective-permute-start.118) | collective-permute-done | bytes 131104 | tf_op jit(solution)/shard_map/ppermute | solution.py:311
  719.2 8.6 collective-permute-done.70
  727.8 10.6 %collective-permute-done.69 = bf16[128,2048]{1,0:T(8,128)(2,1)S(1)} collective-permute-done((bf16[128,2048]{1,0:T(8,128)(2,1)S(1)}, bf16[128,2048]{1,0:T(8,128)(2,1)S(1)}, u32[]{:S(2)}, u32[]{:S(2)}) %collective-permute-start.69) | collective-permute-done | bytes 524320 | tf_op jit(solution)/shard_map/ppermute | solution.py:311
  758.5 10.6 %collective-permute-done.88 = bf16[128,2048]{1,0:T(8,128)(2,1)S(1)} collective-permute-done((bf16[128,2048]{1,0:T(8,128)(2,1)S(1)}, bf16[128,2048]{1,0:T(8,128)(2,1)S(1)}, u32[]{:S(2)}, u32[]{:S(2)}) %collective-permute-start.88) | collective-permute-done | bytes 524320 | tf_op jit(solution)/shard_map/ppermute | solution.py:311
  769.1 6.1 collective-permute-done.90
  775.2 10.4 %collective-permute-done.89 = bf16[128,2048]{1,0:T(8,128)(2,1)S(1)} collective-permute-done((bf16[128,2048]{1,0:T(8,128)(2,1)S(1)}, bf16[128,2048]{1,0:T(8,128)(2,1)S(1)}, u32[]{:S(2)}, u32[]{:S(2)}) %collective-permute-start.89) | collective-permute-done | bytes 524320 | tf_op jit(solution)/shard_map/ppermute | solution.py:311
  787.1 5.6 all-to-all-start.7
  803.0 6.5 collective-permute-done.91
  809.6 6.1 collective-permute-done.93
  815.7 7.4 collective-permute-done.92
  825.7 5.3 all-to-all-start.6
  840.6 19.6 %collective-permute-done.80 = bf16[32,2048]{1,0:T(8,128)(2,1)S(1)} collective-permute-done((bf16[32,2048]{1,0:T(8,128)(2,1)S(1)}, bf16[32,2048]{1,0:T(8,128)(2,1)S(1)}, u32[]{:S(2)}, u32[]{:S(2)}) %collective-permute-start.80) | collective-permute-done | bytes 131104 | tf_op jit(solution)/shard_map/ppermute | solution.py:311
  860.2 6.1 collective-permute-done.82
  866.3 11.8 %collective-permute-done.81 = bf16[32,2048]{1,0:T(8,128)(2,1)S(1)} collective-permute-done((bf16[32,2048]{1,0:T(8,128)(2,1)S(1)}, bf16[32,2048]{1,0:T(8,128)(2,1)S(1)}, u32[]{:S(2)}, u32[]{:S(2)}) %collective-permute-start.81) | collective-permute-done | bytes 131104 | tf_op jit(solution)/shard_map/ppermute | solution.py:311
  901.0 5.5 shard_map.284
  911.7 9.9 collective-permute-done.122
  922.8 6.7 collective-permute-done.101
  955.6 7.3 collective-permute-done.108
  968.4 7.6 collective-permute-done.117
  (796 shorter events, 471.0 us)
Async XLA Ops:
  22.9 36.2 %collective-permute-start.10 = (bf16[256,256]{1,0:T(8,128)(2,1)}, bf16[256,256]{1,0:T(8,128)(2,1)}, u32[]{:S(2)}, u32[]{:S(2)}) collective-permute-start(bf16[256,256]{1,0:T(8,128)(2,1)} %split.335), channel_id=1, source_target_pairs={{0,16},{1,17},{2,18},{3,19},{4,20},{5,21},{6,22},{7,23},{8,24},{9,... | collective-permute-start | bytes 393224 | tf_op jit(solution)/shard_map/ppermute | solution.py:311
  25.8 25.7 %collective-permute-start.3 = (bf16[256,512]{1,0:T(8,128)(2,1)S(1)}, bf16[256,512]{1,0:T(8,128)(2,1)S(1)}, u32[]{:S(2)}, u32[]{:S(2)}) collective-permute-start(bf16[256,512]{1,0:T(8,128)(2,1)S(1)} %split.333), channel_id=1, source_target_pairs={{0,16},{1,17},{2,18},{3,19},{4,20},{5,21},{6,22},{7,23},{8,24},{9,... | collective-permute-start | bytes 786440 | tf_op jit(solution)/shard_map/ppermute | solution.py:311
  53.3 25.6 %collective-permute-start.5 = (bf16[2,256,512]{2,1,0:T(8,128)(2,1)S(1)}, bf16[2,256,512]{2,1,0:T(8,128)(2,1)S(1)}, u32[]{:S(2)}, u32[]{:S(2)}) collective-permute-start(bf16[2,256,512]{2,1,0:T(8,128)(2,1)S(1)} %bitcast.269), channel_id=1, source_target_pairs={{0,8},{1,9},{2,10},{3,11},{4,12},{5,13},{6,14},{7,15},{8,0},{9,1},... | collective-permute-start | bytes 1572872 | tf_op jit(solution)/shard_map/ppermute | solution.py:311
  60.0 25.3 %collective-permute-start.13 = (bf16[2,256,256]{2,1,0:T(8,128)(2,1)S(1)}, bf16[2,256,256]{2,1,0:T(8,128)(2,1)S(1)}, u32[]{:S(2)}, u32[]{:S(2)}) collective-permute-start(bf16[2,256,256]{2,1,0:T(8,128)(2,1)S(1)} %bitcast.272), channel_id=1, source_target_pairs={{0,12},{1,13},{2,14},{3,15},{4,8},{5,9},{6,10},{7,11},{8,4},{9,5},... | collective-permute-start | bytes 786440 | tf_op jit(solution)/shard_map/ppermute | solution.py:311
  97.5 32.9 %all-to-all-start.3 = ((bf16[8,192,256]{2,1,0:T(8,128)(2,1)}), bf16[8,192,256]{2,1,0:T(8,128)(2,1)S(1)}, u32[]{:S(2)}, u32[]{:S(2)}) async-start(bf16[8,192,256]{2,1,0:T(8,128)(2,1)} %bitcast.305), calls=%async_computation.3 | async-start | bytes 1572864 | tf_op jit(solution)/shard_map/all_to_all | solution.py:345
  130.3 60.0 %all-to-all-start.1 = ((bf16[8,128,384]{2,1,0:T(8,128)(2,1)}), bf16[8,128,384]{2,1,0:T(8,128)(2,1)}, u32[]{:S(2)}, u32[]{:S(2)}) async-start(bf16[8,128,384]{2,1,0:T(8,128)(2,1)} %get-tuple-element.99), calls=%async_computation.1 | async-start | bytes 1572864 | tf_op jit(solution)/shard_map/all_to_all | solution.py:345
  138.5 27.3 %collective-permute-start.18 = (bf16[32,2048]{1,0:T(8,128)(2,1)S(1)}, bf16[32,2048]{1,0:T(8,128)(2,1)S(1)}, u32[]{:S(2)}, u32[]{:S(2)}) collective-permute-start(bf16[32,2048]{1,0:T(8,128)(2,1)S(1)} %multiply_convert_fusion.14.refs_0_), channel_id=1, source_target_pairs={{0,16},{1,17},{2,18},{3,19},{4,20},{5,21},{6,22},{7,23},{8,24},{9,... | collective-permute-start | bytes 393224 | tf_op jit(solution)/shard_map/ppermute | solution.py:311
  138.5 27.3 %collective-permute-start.17 = (bf16[32,2048]{1,0:T(8,128)(2,1)S(1)}, bf16[32,2048]{1,0:T(8,128)(2,1)S(1)}, u32[]{:S(2)}, u32[]{:S(2)}) collective-permute-start(bf16[32,2048]{1,0:T(8,128)(2,1)S(1)} %multiply_convert_fusion.14.refs_0_), channel_id=1, source_target_pairs={{0,8},{1,9},{2,10},{3,11},{4,12},{5,13},{6,14},{7,15},{8,0},{9,1},... | collective-permute-start | bytes 393224 | tf_op jit(solution)/shard_map/ppermute | solution.py:311
  190.3 27.7 %collective-permute-start.23 = (bf16[512,2048]{1,0:T(8,128)(2,1)S(1)}, bf16[512,2048]{1,0:T(8,128)(2,1)}, u32[]{:S(2)}, u32[]{:S(2)}) collective-permute-start(bf16[512,2048]{1,0:T(8,128)(2,1)S(1)} %shard_map.248), channel_id=1, source_target_pairs={{0,1},{1,0},{2,3},{3,2},{4,5},{5,4},{6,7},{7,6},{8,9},{9,8},{10,11... | collective-permute-start | bytes 6291464 | tf_op jit(solution)/shard_map/ppermute | solution.py:311
  190.4 26.1 %all-to-all-start.2 = ((bf16[8,128,384]{2,1,0:T(8,128)(2,1)}), bf16[8,128,384]{2,1,0:T(8,128)(2,1)}, u32[]{:S(2)}, u32[]{:S(2)}) async-start(bf16[8,128,384]{2,1,0:T(8,128)(2,1)} %get-tuple-element.100), calls=%async_computation.2 | async-start | bytes 1572864 | tf_op jit(solution)/shard_map/all_to_all | solution.py:345
  195.6 135.1 %all-gather.6.cloned.1.call-start = ((), (), s32[]{:S(2)}) async-start(), calls=%async_computation.12 | async-start | bytes 1310720 | tf_op jit(solution)/shard_map/all_gather | solution.py:409
  226.6 25.7 %collective-permute-start.34 = (bf16[256,256]{1,0:T(8,128)(2,1)}, bf16[256,256]{1,0:T(8,128)(2,1)S(1)}, u32[]{:S(2)}, u32[]{:S(2)}) collective-permute-start(bf16[256,256]{1,0:T(8,128)(2,1)} %get-tuple-element.359), channel_id=1, source_target_pairs={{0,16},{1,17},{2,18},{3,19},{4,20},{5,21},{6,22},{7,23},{8,24},{9,... | collective-permute-start | bytes 393224 | tf_op jit(solution)/shard_map/ppermute | solution.py:311
  239.3 98.1 %all-gather.4.cloned.1.call-start = ((), (), s32[]{:S(2)}) async-start(), calls=%async_computation.11 | async-start | bytes 1310720 | tf_op jit(solution)/shard_map/all_gather | solution.py:409
  249.4 27.6 %collective-permute-start.27 = (bf16[128,2048]{1,0:T(8,128)(2,1)}, bf16[128,2048]{1,0:T(8,128)(2,1)}, u32[]{:S(2)}, u32[]{:S(2)}) collective-permute-start(bf16[128,2048]{1,0:T(8,128)(2,1)} %get-tuple-element.309), channel_id=1, source_target_pairs={{0,6},{1,7},{2,4},{3,5},{4,2},{5,3},{6,0},{7,1},{8,14},{9,15},{10,... | collective-permute-start | bytes 1572872 | tf_op jit(solution)/shard_map/ppermute | solution.py:311
  251.0 41.9 %collective-permute-start.26 = (bf16[128,2048]{1,0:T(8,128)(2,1)}, bf16[128,2048]{1,0:T(8,128)(2,1)}, u32[]{:S(2)}, u32[]{:S(2)}) collective-permute-start(bf16[128,2048]{1,0:T(8,128)(2,1)} %get-tuple-element.310), channel_id=1, source_target_pairs={{0,4},{1,5},{2,6},{3,7},{4,0},{5,1},{6,2},{7,3},{8,12},{9,13},{10,... | collective-permute-start | bytes 1572872 | tf_op jit(solution)/shard_map/ppermute | solution.py:311
  253.1 94.4 %all-gather.8.cloned.1.call-start = ((), (), s32[]{:S(2)}) async-start(), calls=%async_computation.13 | async-start | bytes 1310720 | tf_op jit(solution)/shard_map/all_gather | solution.py:409
  253.1 48.3 %collective-permute-start.39 = (bf16[256,256]{1,0:T(8,128)(2,1)}, bf16[256,256]{1,0:T(8,128)(2,1)S(1)}, u32[]{:S(2)}, u32[]{:S(2)}) collective-permute-start(bf16[256,256]{1,0:T(8,128)(2,1)} %get-tuple-element.357), channel_id=1, source_target_pairs={{0,16},{1,17},{2,18},{3,19},{4,20},{5,21},{6,22},{7,23},{8,24},{9,... | collective-permute-start | bytes 393224 | tf_op jit(solution)/shard_map/ppermute | solution.py:311
  354.5 48.7 %all-to-all-start.5 = ((bf16[8,192,256]{2,1,0:T(8,128)(2,1)}), bf16[8,192,256]{2,1,0:T(8,128)(2,1)}, u32[]{:S(2)}, u32[]{:S(2)}) async-start(bf16[8,192,256]{2,1,0:T(8,128)(2,1)} %bitcast.304), calls=%async_computation.5 | async-start | bytes 1572864 | tf_op jit(solution)/shard_map/all_to_all | solution.py:345
  400.3 61.3 %collective-permute-start.48 = (bf16[128,2048]{1,0:T(8,128)(2,1)}, bf16[128,2048]{1,0:T(8,128)(2,1)}, u32[]{:S(2)}, u32[]{:S(2)}) collective-permute-start(bf16[128,2048]{1,0:T(8,128)(2,1)} %shard_map.259.refs_0_), channel_id=1, source_target_pairs={{0,6},{1,7},{2,4},{3,5},{4,2},{5,3},{6,0},{7,1},{8,14},{9,15},{10,... | collective-permute-start | bytes 1572872 | tf_op jit(solution)/shard_map/ppermute | solution.py:311
  403.2 84.4 %all-to-all-start.4 = ((bf16[8,256,384]{2,1,0:T(8,128)(2,1)}), bf16[8,256,384]{2,1,0:T(8,128)(2,1)}, u32[]{:S(2)}, u32[]{:S(2)}) async-start(bf16[8,256,384]{2,1,0:T(8,128)(2,1)} %copy-done.14), calls=%async_computation.4 | async-start | bytes 3145728 | tf_op jit(solution)/shard_map/all_to_all | solution.py:345
  407.9 53.9 %collective-permute-start.47 = (bf16[128,2048]{1,0:T(8,128)(2,1)}, bf16[128,2048]{1,0:T(8,128)(2,1)S(1)}, u32[]{:S(2)}, u32[]{:S(2)}) collective-permute-start(bf16[128,2048]{1,0:T(8,128)(2,1)} %shard_map.259.refs_0_), channel_id=1, source_target_pairs={{0,4},{1,5},{2,6},{3,7},{4,0},{5,1},{6,2},{7,3},{8,12},{9,13},{10,... | collective-permute-start | bytes 1572872 | tf_op jit(solution)/shard_map/ppermute | solution.py:311
  409.9 52.0 %collective-permute-start.46 = (bf16[128,2048]{1,0:T(8,128)(2,1)}, bf16[128,2048]{1,0:T(8,128)(2,1)S(1)}, u32[]{:S(2)}, u32[]{:S(2)}) collective-permute-start(bf16[128,2048]{1,0:T(8,128)(2,1)} %shard_map.259.refs_0_), channel_id=1, source_target_pairs={{0,2},{1,3},{2,0},{3,1},{4,6},{5,7},{6,4},{7,5},{8,10},{9,11},{10,... | collective-permute-start | bytes 1572872 | tf_op jit(solution)/shard_map/ppermute | solution.py:311
  412.6 28.7 %collective-permute-start.52 = (bf16[32,2048]{1,0:T(8,128)(2,1)S(1)}, bf16[32,2048]{1,0:T(8,128)(2,1)S(1)}, u32[]{:S(2)}, u32[]{:S(2)}) collective-permute-start(bf16[32,2048]{1,0:T(8,128)(2,1)S(1)} %convert_element_type.417.refs_0_), channel_id=1, source_target_pairs={{0,24},{1,25},{2,26},{3,27},{4,28},{5,29},{6,30},{7,31},{8,16},{9,... | collective-permute-start | bytes 393224 | tf_op jit(solution)/shard_map/ppermute | solution.py:311
  416.0 40.0 %collective-permute-start.51 = (bf16[32,2048]{1,0:T(8,128)(2,1)S(1)}, bf16[32,2048]{1,0:T(8,128)(2,1)S(1)}, u32[]{:S(2)}, u32[]{:S(2)}) collective-permute-start(bf16[32,2048]{1,0:T(8,128)(2,1)S(1)} %convert_element_type.417.refs_0_), channel_id=1, source_target_pairs={{0,16},{1,17},{2,18},{3,19},{4,20},{5,21},{6,22},{7,23},{8,24},{9,... | collective-permute-start | bytes 393224 | tf_op jit(solution)/shard_map/ppermute | solution.py:311
  506.6 25.2 %collective-permute-start.58 = (bf16[128,2048]{1,0:T(8,128)(2,1)S(1)}, bf16[128,2048]{1,0:T(8,128)(2,1)S(1)}, u32[]{:S(2)}, u32[]{:S(2)}) collective-permute-start(bf16[128,2048]{1,0:T(8,128)(2,1)S(1)} %get-tuple-element.305), channel_id=1, source_target_pairs={{0,2},{1,3},{2,0},{3,1},{4,6},{5,7},{6,4},{7,5},{8,10},{9,11},{10,... | collective-permute-start | bytes 1572872 | tf_op jit(solution)/shard_map/ppermute | solution.py:311
  582.3 156.9 %all-to-all-start.9 = ((bf16[8,192,256]{2,1,0:T(8,128)(2,1)}), bf16[8,192,256]{2,1,0:T(8,128)(2,1)}, u32[]{:S(2)}, u32[]{:S(2)}) async-start(bf16[8,192,256]{2,1,0:T(8,128)(2,1)} %bitcast.301), calls=%async_computation.9 | async-start | bytes 1572864 | tf_op jit(solution)/shard_map/all_to_all | solution.py:345
  639.6 42.7 %collective-permute-start.123 = (bf16[2,256,256]{2,1,0:T(8,128)(2,1)S(1)}, bf16[2,256,256]{2,1,0:T(8,128)(2,1)S(1)}, u32[]{:S(2)}, u32[]{:S(2)}) collective-permute-start(bf16[2,256,256]{2,1,0:T(8,128)(2,1)S(1)} %get-tuple-element.166), channel_id=1, source_target_pairs={{0,4},{1,5},{2,6},{3,7},{4,0},{5,1},{6,2},{7,3},{8,12},{9,13},{10,... | collective-permute-start | bytes 786440 | tf_op jit(solution)/shard_map/ppermute | solution.py:311
  642.1 42.9 %collective-permute-start.124 = (bf16[2,256,256]{2,1,0:T(8,128)(2,1)S(1)}, bf16[2,256,256]{2,1,0:T(8,128)(2,1)S(1)}, u32[]{:S(2)}, u32[]{:S(2)}) collective-permute-start(bf16[2,256,256]{2,1,0:T(8,128)(2,1)S(1)} %get-tuple-element.167), channel_id=1, source_target_pairs={{0,8},{1,9},{2,10},{3,11},{4,12},{5,13},{6,14},{7,15},{8,0},{9,1},... | collective-permute-start | bytes 786440 | tf_op jit(solution)/shard_map/ppermute | solution.py:311
  646.8 34.7 %collective-permute-start.84 = (bf16[128,2048]{1,0:T(8,128)(2,1)S(1)}, bf16[128,2048]{1,0:T(8,128)(2,1)S(1)}, u32[]{:S(2)}, u32[]{:S(2)}) collective-permute-start(bf16[128,2048]{1,0:T(8,128)(2,1)S(1)} %shard_map.270.refs_0_), channel_id=1, source_target_pairs={{0,4},{1,5},{2,6},{3,7},{4,0},{5,1},{6,2},{7,3},{8,12},{9,13},{10,... | collective-permute-start | bytes 1572872 | tf_op jit(solution)/shard_map/ppermute | solution.py:311
  653.4 28.1 %collective-permute-start.83 = (bf16[128,2048]{1,0:T(8,128)(2,1)S(1)}, bf16[128,2048]{1,0:T(8,128)(2,1)S(1)}, u32[]{:S(2)}, u32[]{:S(2)}) collective-permute-start(bf16[128,2048]{1,0:T(8,128)(2,1)S(1)} %shard_map.270.refs_0_), channel_id=1, source_target_pairs={{0,2},{1,3},{2,0},{3,1},{4,6},{5,7},{6,4},{7,5},{8,10},{9,11},{10,... | collective-permute-start | bytes 1572872 | tf_op jit(solution)/shard_map/ppermute | solution.py:311
  681.5 27.4 %collective-permute-start.67 = (bf16[512,2048]{1,0:T(8,128)(2,1)S(1)}, bf16[512,2048]{1,0:T(8,128)(2,1)}, u32[]{:S(2)}, u32[]{:S(2)}) collective-permute-start(bf16[512,2048]{1,0:T(8,128)(2,1)S(1)} %convolution_convert_fusion), channel_id=1, source_target_pairs={{0,1},{1,0},{2,3},{3,2},{4,5},{5,4},{6,7},{7,6},{8,9},{9,8},{10,11... | collective-permute-start | bytes 6291464 | tf_op jit(solution)/shard_map/ppermute | solution.py:311
  708.9 37.2 %collective-permute-start.87 = (bf16[512,2048]{1,0:T(8,128)(2,1)}, bf16[512,2048]{1,0:T(8,128)(2,1)}, u32[]{:S(2)}, u32[]{:S(2)}) collective-permute-start(bf16[512,2048]{1,0:T(8,128)(2,1)} %convolution_convert_fusion.4), channel_id=1, source_target_pairs={{0,1},{1,0},{2,3},{3,2},{4,5},{5,4},{6,7},{7,6},{8,9},{9,8},{10,11... | collective-permute-start | bytes 6291464 | tf_op jit(solution)/shard_map/ppermute | solution.py:311
  714.9 24.4 %collective-permute-start.68 = (bf16[128,2048]{1,0:T(8,128)(2,1)S(1)}, bf16[128,2048]{1,0:T(8,128)(2,1)}, u32[]{:S(2)}, u32[]{:S(2)}) collective-permute-start(bf16[128,2048]{1,0:T(8,128)(2,1)S(1)} %get-tuple-element.304), channel_id=1, source_target_pairs={{0,2},{1,3},{2,0},{3,1},{4,6},{5,7},{6,4},{7,5},{8,10},{9,11},{10,... | collective-permute-start | bytes 1572872 | tf_op jit(solution)/shard_map/ppermute | solution.py:311
  739.2 47.9 %all-to-all-start.8 = ((bf16[8,256,384]{2,1,0:T(8,128)(2,1)}), bf16[8,256,384]{2,1,0:T(8,128)(2,1)}, u32[]{:S(2)}, u32[]{:S(2)}) async-start(bf16[8,256,384]{2,1,0:T(8,128)(2,1)} %bitcast.284), calls=%async_computation.8 | async-start | bytes 3145728 | tf_op jit(solution)/shard_map/all_to_all | solution.py:345
  749.6 25.6 %collective-permute-start.90 = (bf16[128,2048]{1,0:T(8,128)(2,1)S(1)}, bf16[128,2048]{1,0:T(8,128)(2,1)S(1)}, u32[]{:S(2)}, u32[]{:S(2)}) collective-permute-start(bf16[128,2048]{1,0:T(8,128)(2,1)S(1)} %get-tuple-element.300), channel_id=1, source_target_pairs={{0,6},{1,7},{2,4},{3,5},{4,2},{5,3},{6,0},{7,1},{8,14},{9,15},{10,... | collective-permute-start | bytes 1572872 | tf_op jit(solution)/shard_map/ppermute | solution.py:311
  752.4 33.2 %collective-permute-start.89 = (bf16[128,2048]{1,0:T(8,128)(2,1)S(1)}, bf16[128,2048]{1,0:T(8,128)(2,1)S(1)}, u32[]{:S(2)}, u32[]{:S(2)}) collective-permute-start(bf16[128,2048]{1,0:T(8,128)(2,1)S(1)} %get-tuple-element.301), channel_id=1, source_target_pairs={{0,4},{1,5},{2,6},{3,7},{4,0},{5,1},{6,2},{7,3},{8,12},{9,13},{10,... | collective-permute-start | bytes 1572872 | tf_op jit(solution)/shard_map/ppermute | solution.py:311
  787.1 38.5 %all-to-all-start.7 = ((bf16[8,192,256]{2,1,0:T(8,128)(2,1)}), bf16[8,192,256]{2,1,0:T(8,128)(2,1)}, u32[]{:S(2)}, u32[]{:S(2)}) async-start(bf16[8,192,256]{2,1,0:T(8,128)(2,1)} %bitcast.303), calls=%async_computation.7 | async-start | bytes 1572864 | tf_op jit(solution)/shard_map/all_to_all | solution.py:345
  798.3 24.8 %collective-permute-start.92 = (bf16[32,2048]{1,0:T(8,128)(2,1)S(1)}, bf16[32,2048]{1,0:T(8,128)(2,1)S(1)}, u32[]{:S(2)}, u32[]{:S(2)}) collective-permute-start(bf16[32,2048]{1,0:T(8,128)(2,1)S(1)} %get-tuple-element.329), channel_id=1, source_target_pairs={{0,16},{1,17},{2,18},{3,19},{4,20},{5,21},{6,22},{7,23},{8,24},{9,... | collective-permute-start | bytes 393224 | tf_op jit(solution)/shard_map/ppermute | solution.py:311
  825.7 70.7 %all-to-all-start.6 = ((bf16[8,256,384]{2,1,0:T(8,128)(2,1)}), bf16[8,256,384]{2,1,0:T(8,128)(2,1)}, u32[]{:S(2)}, u32[]{:S(2)}) async-start(bf16[8,256,384]{2,1,0:T(8,128)(2,1)} %bitcast.93), calls=%async_computation.6 | async-start | bytes 3145728 | tf_op jit(solution)/shard_map/all_to_all | solution.py:345
  833.9 26.3 %collective-permute-start.80 = (bf16[32,2048]{1,0:T(8,128)(2,1)S(1)}, bf16[32,2048]{1,0:T(8,128)(2,1)S(1)}, u32[]{:S(2)}, u32[]{:S(2)}) collective-permute-start(bf16[32,2048]{1,0:T(8,128)(2,1)S(1)} %get-tuple-element.330), channel_id=1, source_target_pairs={{0,8},{1,9},{2,10},{3,11},{4,12},{5,13},{6,14},{7,15},{8,0},{9,1},... | collective-permute-start | bytes 393224 | tf_op jit(solution)/shard_map/ppermute | solution.py:311
  836.0 30.3 %collective-permute-start.82 = (bf16[32,2048]{1,0:T(8,128)(2,1)S(1)}, bf16[32,2048]{1,0:T(8,128)(2,1)S(1)}, u32[]{:S(2)}, u32[]{:S(2)}) collective-permute-start(bf16[32,2048]{1,0:T(8,128)(2,1)S(1)} %get-tuple-element.331), channel_id=1, source_target_pairs={{0,24},{1,25},{2,26},{3,27},{4,28},{5,29},{6,30},{7,31},{8,16},{9,... | collective-permute-start | bytes 393224 | tf_op jit(solution)/shard_map/ppermute | solution.py:311
  838.3 39.7 %collective-permute-start.81 = (bf16[32,2048]{1,0:T(8,128)(2,1)S(1)}, bf16[32,2048]{1,0:T(8,128)(2,1)S(1)}, u32[]{:S(2)}, u32[]{:S(2)}) collective-permute-start(bf16[32,2048]{1,0:T(8,128)(2,1)S(1)} %get-tuple-element.332), channel_id=1, source_target_pairs={{0,16},{1,17},{2,18},{3,19},{4,20},{5,21},{6,22},{7,23},{8,24},{9,... | collective-permute-start | bytes 393224 | tf_op jit(solution)/shard_map/ppermute | solution.py:311
  839.8 39.1 %collective-permute-start.96 = (bf16[128,2048]{1,0:T(8,128)(2,1)S(1)}, bf16[128,2048]{1,0:T(8,128)(2,1)S(1)}, u32[]{:S(2)}, u32[]{:S(2)}) collective-permute-start(bf16[128,2048]{1,0:T(8,128)(2,1)S(1)} %shard_map.273.refs_0_), channel_id=1, source_target_pairs={{0,1},{1,0},{2,3},{3,2},{4,5},{5,4},{6,7},{7,6},{8,9},{9,8},{10,11... | collective-permute-start | bytes 1572872 | tf_op jit(solution)/shard_map/ppermute | solution.py:311
  891.9 59.2 %collective-permute-start.103 = (bf16[2,256,256]{2,1,0:T(8,128)(2,1)S(1)}, bf16[2,256,256]{2,1,0:T(8,128)(2,1)}, u32[]{:S(2)}, u32[]{:S(2)}) collective-permute-start(bf16[2,256,256]{2,1,0:T(8,128)(2,1)S(1)} %get-tuple-element.126), channel_id=1, source_target_pairs={{0,4},{1,5},{2,6},{3,7},{4,0},{5,1},{6,2},{7,3},{8,12},{9,13},{10,... | collective-permute-start | bytes 786440 | tf_op jit(solution)/shard_map/ppermute | solution.py:311
  906.5 49.0 %collective-permute-start.104 = (bf16[2,256,256]{2,1,0:T(8,128)(2,1)S(1)}, bf16[2,256,256]{2,1,0:T(8,128)(2,1)}, u32[]{:S(2)}, u32[]{:S(2)}) collective-permute-start(bf16[2,256,256]{2,1,0:T(8,128)(2,1)S(1)} %get-tuple-element.127), channel_id=1, source_target_pairs={{0,8},{1,9},{2,10},{3,11},{4,12},{5,13},{6,14},{7,15},{8,0},{9,1},... | collective-permute-start | bytes 786440 | tf_op jit(solution)/shard_map/ppermute | solution.py:311
  906.7 48.8 %collective-permute-start.105 = (bf16[2,256,256]{2,1,0:T(8,128)(2,1)S(1)}, bf16[2,256,256]{2,1,0:T(8,128)(2,1)}, u32[]{:S(2)}, u32[]{:S(2)}) collective-permute-start(bf16[2,256,256]{2,1,0:T(8,128)(2,1)S(1)} %get-tuple-element.128), channel_id=1, source_target_pairs={{0,12},{1,13},{2,14},{3,15},{4,8},{5,9},{6,10},{7,11},{8,4},{9,5},... | collective-permute-start | bytes 786440 | tf_op jit(solution)/shard_map/ppermute | solution.py:311
  908.8 46.8 %collective-permute-start.106 = (bf16[2,256,256]{2,1,0:T(8,128)(2,1)S(1)}, bf16[2,256,256]{2,1,0:T(8,128)(2,1)}, u32[]{:S(2)}, u32[]{:S(2)}) collective-permute-start(bf16[2,256,256]{2,1,0:T(8,128)(2,1)S(1)} %get-tuple-element.130), channel_id=1, source_target_pairs={{0,4},{1,5},{2,6},{3,7},{4,0},{5,1},{6,2},{7,3},{8,12},{9,13},{10,... | collective-permute-start | bytes 786440 | tf_op jit(solution)/shard_map/ppermute | solution.py:311
  946.3 35.3 %all-to-all-start.10 = ((f32[32,1,1536]{2,1,0:T(1,128)}), f32[32,1,1536]{2,1,0:T(1,128)}, u32[]{:S(2)}, u32[]{:S(2)}) async-start(f32[32,1,1536]{2,1,0:T(1,128)} %all_to_all.46), calls=%async_computation.10 | async-start | bytes 393216 | tf_op jit(solution)/shard_map/all_to_all | solution.py:708
  (240 other events, 2859.7 us)
Sparse Core Ops, SparseCore 0:
  239.4 31.1 all-gather.5
  272.7 31.2 all-gather.3
  306.2 31.2 all-gather.7
